TPU v7x, 32 devices: a whole 2x2x4 slice. The times are simulated.
32 devices in a mesh: dp: 8 (over z, y), seq: 4 (over x, core).
Axes of the slice: x: 2, y: 2, z: 4, core: 2. Of those that a mesh axis runs over, the one named last changes fastest.
Arguments:
- inputs: bfloat16 [8, 1024, 768], P('dp', 'seq'), may hold values from -6 to 6
- lengths: int32 [8], P('dp'), may hold values from 1 to 1024, 6144 in all
- gain_attend: bfloat16 [2, 768], P(None, ('dp', 'seq')), may hold values from 0.5 to 1.5
- shift_attend: bfloat16 [2, 768], P(None, ('dp', 'seq')), may hold values from -1.5 to 1.5
- weight_query: bfloat16 [2, 768, 768], P(None, ('dp', 'seq')), may hold values from -0.3125 to 0.3125
- weight_key: bfloat16 [2, 768, 768], P(None, ('dp', 'seq')), may hold values from -0.3125 to 0.3125
- weight_value: bfloat16 [2, 768, 768], P(None, ('dp', 'seq')), may hold values from -0.21875 to 0.21875
- weight_output: bfloat16 [2, 768, 768], P(None, ('dp', 'seq')), may hold values from -0.875 to 0.875
- gain_mixer: bfloat16 [2, 768], P(None, ('dp', 'seq')), may hold values from 0.5 to 1.5
- shift_mixer: bfloat16 [2, 768], P(None, ('dp', 'seq')), may hold values from -1.5 to 1.5
- weight_inner: bfloat16 [2, 768, 3072], P(None, ('dp', 'seq')), may hold values from -0.21875 to 0.21875
- bias_inner: bfloat16 [2, 3072], P(None, ('dp', 'seq')), may hold values from -2.5 to 2.5
- weight_outer: bfloat16 [2, 3072, 768], P(None, ('dp', 'seq')), may hold values from -0.109375 to 0.109375
- bias_outer: bfloat16 [2, 768], P(None, ('dp', 'seq')), may hold values from -1.5 to 1.5
- cotangent: float32 [8, 1024, 768], P('dp', 'seq'), may hold values from -6 to 6
Outputs:
- output: float32 [8, 1024, 768], P('dp', 'seq')
- input_grad: float32 [8, 1024, 768], P('dp', 'seq')
- grad_gain_attend: float32 [2, 768], P(None, ('dp', 'seq'))
- grad_shift_attend: float32 [2, 768], P(None, ('dp', 'seq'))
- grad_weight_query: float32 [2, 768, 768], P(None, ('dp', 'seq'))
- grad_weight_key: float32 [2, 768, 768], P(None, ('dp', 'seq'))
- grad_weight_value: float32 [2, 768, 768], P(None, ('dp', 'seq'))
- grad_weight_output: float32 [2, 768, 768], P(None, ('dp', 'seq'))
- grad_gain_mixer: float32 [2, 768], P(None, ('dp', 'seq'))
- grad_shift_mixer: float32 [2, 768], P(None, ('dp', 'seq'))
- grad_weight_inner: float32 [2, 768, 3072], P(None, ('dp', 'seq'))
- grad_bias_inner: float32 [2, 3072], P(None, ('dp', 'seq'))
- grad_weight_outer: float32 [2, 3072, 768], P(None, ('dp', 'seq'))
- grad_bias_outer: float32 [2, 768], P(None, ('dp', 'seq'))
- selected_share: float32 [], replicated
Inputs may be any that keep to these rules, and one draw needn't show every extreme that they name: `lengths`: each sequence's count of real tokens; the longest sequence has exactly 1024.
All inputs are finite; a program needn't handle non-finite values. No bound on the sum of `lengths` on one device may be relied on, other than what follows from the above.
Results may differ from a plain program's by a relative error of at most 0.024.
Values may be sent and summed in bfloat16 or wider, within the bound.
No kernel may reach another device: no remote copies, remote signals or barrier semaphores. Data moves between devices by JAX's collectives and lax.ppermute only.
A program may use at most 320 MiB of HBM per device.

v0:
```python
import jax
import jax.numpy as jnp
from jax import lax
from jax.sharding import PartitionSpec as P

HEADS = 12


norm_eps = 1e-05
share_level = 0.5
select_strength = 2.0
masked_value = -1e30


def prefix(array, axis, combine, identity, reverse):
    size, place = (lax.axis_size(axis), lax.axis_index(axis))
    everything = lax.all_gather(array, axis)
    start = jnp.broadcast_to(jnp.asarray(identity, array.dtype), array.shape)

    def step(k, before):
        at = size - 1 - k if reverse else k
        reached = at > place if reverse else at < place
        new = combine(before, everything[at])
        return jnp.where(reached, new, before)

    return lax.fori_loop(0, size, step, start)


def layer_norm(hidden, gain, shift):
    average = jnp.mean(hidden, axis=-1, keepdims=True)
    centered = hidden - average
    spread = jnp.mean(centered * centered, axis=-1, keepdims=True)
    return centered * lax.rsqrt(spread + norm_eps) * gain + shift


def adding(earlier, later):
    return earlier + later


def product(left, right, form):
    return jnp.einsum(form, left, right, preferred_element_type=jnp.float32)


def join_rows(members, devices):
    return jnp.concatenate([member.reshape(devices, -1) for member in members], axis=1)


def split_rows(joined, shapes, devices):
    results = []
    offset = 0
    for shape in shapes:
        count = 1
        for extent in shape:
            count = count * extent
        count = count // devices
        piece = joined[:, offset : offset + count]
        results.append(piece.reshape((shape[0] // devices,) + tuple(shape[1:])))
        offset = offset + count
    return results


def local(
    inputs,
    lengths,
    gain_attend,
    shift_attend,
    weight_query,
    weight_key,
    weight_value,
    weight_output,
    gain_mixer,
    shift_mixer,
    weight_inner,
    bias_inner,
    weight_outer,
    bias_outer,
    cotangent,
):
    layers = gain_attend.shape[0]
    seq_dev, local_len, width = inputs.shape
    heads = HEADS
    head = width // heads
    seq_count = lax.axis_size("seq")
    devices = lax.axis_size(("dp", "seq"))
    full_len = local_len * seq_count
    highest = lax.Precision.HIGHEST
    is_last = lax.axis_index("seq") == seq_count - 1
    position = lax.axis_index("seq") * local_len + jnp.arange(local_len, dtype=jnp.int32)
    key_place = jnp.arange(full_len, dtype=jnp.int32)
    valid_keys = key_place[None, :] < lengths[:, None]
    valid_query = position[None, :] < lengths[:, None]
    select_mask = (
        (position[None, :, None] > key_place[None, None, :])
        & (key_place[None, None, :] >= 1)
        & valid_query[:, :, None]
        & valid_keys[:, None, :]
    )
    allowed = ((position[None, :, None] >= key_place[None, None, :]) & valid_keys[:, None, :])[
        :, None
    ]
    row_index = jnp.arange(local_len, dtype=jnp.int32)
    strict_lower = (row_index[:, None] > row_index[None, :]).astype(jnp.float32)
    select_scale = select_strength / full_len

    def score_block(query, keys_whole):
        scores = (
            product(query, keys_whole.reshape(seq_dev, full_len, heads, head), "sqhe,skhe->shqk")
            * 0.125
        )
        select = jnp.where(select_mask, jax.nn.relu(scores[:, 0]), 0.0) * select_scale
        return (scores, select)

    def logits_from(scores, select, before):
        carried = before[:, None, :] + jnp.einsum(
            "qr,srk->sqk", strict_lower, select, precision=highest
        )
        return jnp.where(allowed, scores - carried[:, None], masked_value)

    hidden = inputs.astype(jnp.float32)
    share_sum = jnp.zeros((), jnp.float32)
    saved = []
    gathered = []
    for layer_index in range(layers):
        params = (
            lax.all_gather(gain_attend[layer_index], ("dp", "seq"), axis=0, tiled=True),
            lax.all_gather(shift_attend[layer_index], ("dp", "seq"), axis=0, tiled=True),
            lax.all_gather(weight_query[layer_index], ("dp", "seq"), axis=0, tiled=True),
            lax.all_gather(weight_key[layer_index], ("dp", "seq"), axis=0, tiled=True),
            lax.all_gather(weight_value[layer_index], ("dp", "seq"), axis=0, tiled=True),
            lax.all_gather(weight_output[layer_index], ("dp", "seq"), axis=0, tiled=True),
            lax.all_gather(gain_mixer[layer_index], ("dp", "seq"), axis=0, tiled=True),
            lax.all_gather(shift_mixer[layer_index], ("dp", "seq"), axis=0, tiled=True),
            lax.all_gather(weight_inner[layer_index], ("dp", "seq"), axis=0, tiled=True),
            lax.all_gather(bias_inner[layer_index], ("dp", "seq"), axis=0, tiled=True),
            lax.all_gather(weight_outer[layer_index], ("dp", "seq"), axis=0, tiled=True),
            lax.all_gather(bias_outer[layer_index], ("dp", "seq"), axis=0, tiled=True),
        )
        (
            forward_gain_a,
            forward_shift_a,
            forward_w_query,
            forward_w_key,
            forward_w_value,
            forward_w_output,
            forward_gain_m,
            forward_shift_m,
            forward_w_inner,
            forward_b_inner,
            forward_w_outer,
            forward_b_outer,
        ) = params
        forward_normed = (
            layer_norm(
                hidden, forward_gain_a.astype(jnp.float32), forward_shift_a.astype(jnp.float32)
            )
            .astype(jnp.bfloat16)
            .reshape(-1, width)
        )
        forward_query = (
            jnp.dot(forward_normed, forward_w_query, preferred_element_type=jnp.float32)
            .astype(jnp.bfloat16)
            .reshape(seq_dev, local_len, heads, head)
        )
        forward_keys = (
            jnp.dot(forward_normed, forward_w_key, preferred_element_type=jnp.float32)
            .astype(jnp.bfloat16)
            .reshape(seq_dev, local_len, width)
        )
        forward_values = (
            jnp.dot(forward_normed, forward_w_value, preferred_element_type=jnp.float32)
            .astype(jnp.bfloat16)
            .reshape(seq_dev, local_len, width)
        )
        forward_keys_whole = lax.all_gather(forward_keys, "seq", axis=1, tiled=True)
        forward_values_whole = lax.all_gather(forward_values, "seq", axis=1, tiled=True)
        forward_scores, forward_select = score_block(forward_query, forward_keys_whole)
        column = jnp.sum(forward_select, axis=1)
        forward_before = prefix(column, "seq", adding, jnp.zeros_like(column), False)
        logits = logits_from(forward_scores, forward_select, forward_before)
        peak = jnp.max(logits, axis=-1, keepdims=True)
        expo = jnp.exp(logits - peak)
        denominator = jnp.sum(expo, axis=-1, keepdims=True)
        forward_probs = expo / denominator
        forward_log_total = peak + jnp.log(denominator)
        forward_mixed = (
            product(
                forward_probs.astype(jnp.bfloat16),
                forward_values_whole.reshape(seq_dev, full_len, heads, head),
                "shqk,skhe->sqhe",
            )
            .astype(jnp.bfloat16)
            .reshape(-1, width)
        )
        forward_after = hidden + jnp.dot(
            forward_mixed, forward_w_output, preferred_element_type=jnp.float32
        ).reshape(hidden.shape)
        forward_normed_two = (
            layer_norm(
                forward_after,
                forward_gain_m.astype(jnp.float32),
                forward_shift_m.astype(jnp.float32),
            )
            .astype(jnp.bfloat16)
            .reshape(-1, width)
        )
        forward_inner = jnp.dot(
            forward_normed_two, forward_w_inner, preferred_element_type=jnp.float32
        ) + forward_b_inner.astype(jnp.float32)
        forward_active = jax.nn.gelu(forward_inner).astype(jnp.bfloat16)
        outer = jnp.dot(
            forward_active, forward_w_outer, preferred_element_type=jnp.float32
        ) + forward_b_outer.astype(jnp.float32)
        result = forward_after + outer.reshape(hidden.shape)
        totals = forward_before + column
        share = jnp.where(
            is_last,
            jnp.sum(jnp.where(valid_keys, jnp.minimum(totals / share_level, 1.0), 0.0)),
            0.0,
        )
        forward_kept = (
            hidden,
            forward_normed,
            forward_query,
            forward_keys,
            forward_values,
            forward_keys_whole,
            forward_values_whole,
            forward_before,
            forward_log_total,
            forward_mixed,
            forward_after,
            forward_normed_two,
            forward_inner,
            forward_active,
        )
        hidden = result
        share_sum = share_sum + share
        saved.append(forward_kept)
        gathered.append(params)
    grad_hidden = cotangent
    layer_grads = [None] * layers
    for layer_index in reversed(range(layers)):
        params = (
            lax.all_gather(gain_attend[layer_index], ("dp", "seq"), axis=0, tiled=True),
            lax.all_gather(shift_attend[layer_index], ("dp", "seq"), axis=0, tiled=True),
            lax.all_gather(weight_query[layer_index], ("dp", "seq"), axis=0, tiled=True),
            lax.all_gather(weight_key[layer_index], ("dp", "seq"), axis=0, tiled=True),
            lax.all_gather(weight_value[layer_index], ("dp", "seq"), axis=0, tiled=True),
            lax.all_gather(weight_output[layer_index], ("dp", "seq"), axis=0, tiled=True),
            lax.all_gather(gain_mixer[layer_index], ("dp", "seq"), axis=0, tiled=True),
            lax.all_gather(shift_mixer[layer_index], ("dp", "seq"), axis=0, tiled=True),
            lax.all_gather(weight_inner[layer_index], ("dp", "seq"), axis=0, tiled=True),
            lax.all_gather(bias_inner[layer_index], ("dp", "seq"), axis=0, tiled=True),
            lax.all_gather(weight_outer[layer_index], ("dp", "seq"), axis=0, tiled=True),
            lax.all_gather(bias_outer[layer_index], ("dp", "seq"), axis=0, tiled=True),
        )
        (
            gain_a,
            shift_a,
            w_query,
            w_key,
            w_value,
            w_output,
            gain_m,
            shift_m,
            w_inner,
            b_inner,
            w_outer,
            b_outer,
        ) = params
        (
            backward_hidden,
            normed,
            backward_query,
            keys,
            values,
            backward_keys_whole,
            values_whole,
            backward_before,
            log_total,
            mixed,
            after,
            normed_two,
            inner,
            active,
        ) = saved[layer_index]
        grad_y = grad_hidden.astype(jnp.bfloat16).reshape(-1, width)
        grad_b_outer = jnp.sum(grad_y, axis=0, dtype=jnp.float32)
        grad_w_outer = product(active, grad_y, "tf,td->fd")
        grad_active = product(grad_y, w_outer, "td,fd->tf")
        gelu_back = jax.vjp(jax.nn.gelu, inner)[1]
        grad_inner = gelu_back(grad_active)[0].astype(jnp.bfloat16)
        grad_b_inner = jnp.sum(grad_inner, axis=0, dtype=jnp.float32)
        grad_w_inner = product(normed_two, grad_inner, "td,tf->df")
        grad_normed_two = product(grad_inner, w_inner, "tf,df->td").reshape(after.shape)
        norm_back_two = jax.vjp(
            layer_norm, after, gain_m.astype(jnp.float32), shift_m.astype(jnp.float32)
        )[1]
        after_part, grad_gain_m, grad_shift_m = norm_back_two(grad_normed_two)
        grad_after = grad_hidden + after_part
        grad_attn = grad_after.astype(jnp.bfloat16).reshape(-1, width)
        grad_w_output = product(mixed, grad_attn, "tc,td->cd")
        grad_mixed = (
            product(grad_attn, w_output, "td,cd->tc")
            .astype(jnp.bfloat16)
            .reshape(seq_dev, local_len, heads, head)
        )
        backward_scores, backward_select = score_block(backward_query, backward_keys_whole)
        probs = jnp.exp(logits_from(backward_scores, backward_select, backward_before) - log_total)
        values_heads = values_whole.reshape(seq_dev, full_len, heads, head)
        grad_probs = product(grad_mixed, values_heads, "sqhe,skhe->shqk")
        delta = jnp.sum(probs * grad_probs, axis=-1, keepdims=True)
        grad_logits = probs * (grad_probs - delta)
        grad_carried = -jnp.sum(grad_logits, axis=1)
        column_back = jnp.sum(grad_carried, axis=1)
        later_rows = prefix(column_back, "seq", adding, jnp.zeros_like(column_back), True)
        grad_select = later_rows[:, None, :] + jnp.einsum(
            "qr,sqk->srk", strict_lower, grad_carried, precision=highest
        )
        grad_first = jnp.where(
            select_mask & (backward_scores[:, 0] > 0.0), grad_select * select_scale, 0.0
        )
        grad_scores = grad_logits.at[:, 0].add(grad_first).astype(jnp.bfloat16)
        grad_query = (
            (
                product(
                    grad_scores,
                    backward_keys_whole.reshape(seq_dev, full_len, heads, head),
                    "shqk,skhe->sqhe",
                )
                * 0.125
            )
            .astype(jnp.bfloat16)
            .reshape(-1, width)
        )
        grad_values = product(probs.astype(jnp.bfloat16), grad_mixed, "shqk,sqhe->skhe")
        key_part = (product(grad_scores, backward_query, "shqk,sqhe->skhe") * 0.125).reshape(
            seq_dev, full_len, width
        )
        grad_keys = lax.psum_scatter(
            key_part.astype(jnp.bfloat16), "seq", scatter_dimension=1, tiled=True
        ).astype(jnp.float32)
        grad_vals = lax.psum_scatter(
            grad_values.reshape(seq_dev, full_len, width).astype(jnp.bfloat16),
            "seq",
            scatter_dimension=1,
            tiled=True,
        ).astype(jnp.float32)
        grad_keys = grad_keys.astype(jnp.bfloat16).reshape(-1, width)
        grad_vals = grad_vals.astype(jnp.bfloat16).reshape(-1, width)
        grad_w_query = product(normed, grad_query, "tc,td->cd")
        grad_w_key = product(normed, grad_keys, "tc,td->cd")
        grad_w_value = product(normed, grad_vals, "tc,td->cd")
        grad_normed = (
            product(grad_query, w_query, "td,cd->tc")
            + product(grad_keys, w_key, "td,cd->tc")
            + product(grad_vals, w_value, "td,cd->tc")
        )
        norm_back_one = jax.vjp(
            layer_norm, backward_hidden, gain_a.astype(jnp.float32), shift_a.astype(jnp.float32)
        )[1]
        hidden_part, grad_gain_a, grad_shift_a = norm_back_one(
            grad_normed.reshape(backward_hidden.shape)
        )
        grads = (
            grad_gain_a,
            grad_shift_a,
            grad_w_query,
            grad_w_key,
            grad_w_value,
            grad_w_output,
            grad_gain_m,
            grad_shift_m,
            grad_w_inner,
            grad_b_inner,
            grad_w_outer,
            grad_b_outer,
        )
        grad_hidden, grads = (grad_after + hidden_part, grads)
        shapes = [member.shape for member in grads]
        joined = join_rows(grads, devices)
        reduced = lax.psum_scatter(joined, ("dp", "seq"), scatter_dimension=0, tiled=True)
        layer_grads[layer_index] = split_rows(reduced, shapes, devices)
    stacked = tuple(
        (
            jnp.stack([layer_grads[layer_index][member] for layer_index in range(layers)])
            for member in range(12)
        )
    )
    count = jnp.where(is_last, jnp.sum(lengths).astype(jnp.float32), 0.0)
    share_all, count_all = lax.psum((share_sum, count), ("dp", "seq"))
    selected = share_all / (layers * count_all)
    return (
        hidden,
        grad_hidden,
        stacked[0],
        stacked[1],
        stacked[2],
        stacked[3],
        stacked[4],
        stacked[5],
        stacked[6],
        stacked[7],
        stacked[8],
        stacked[9],
        stacked[10],
        stacked[11],
        selected,
    )


def solution(mesh):
    placed = (
        P("dp", "seq", None),
        P("dp"),
        P(None, ("dp", "seq")),
        P(None, ("dp", "seq")),
        P(None, ("dp", "seq"), None),
        P(None, ("dp", "seq"), None),
        P(None, ("dp", "seq"), None),
        P(None, ("dp", "seq"), None),
        P(None, ("dp", "seq")),
        P(None, ("dp", "seq")),
        P(None, ("dp", "seq"), None),
        P(None, ("dp", "seq")),
        P(None, ("dp", "seq"), None),
        P(None, ("dp", "seq")),
        P("dp", "seq", None),
    )
    return jax.shard_map(
        local,
        mesh=mesh,
        in_specs=placed,
        out_specs=(
            P("dp", "seq", None),
            P("dp", "seq", None),
            P(None, ("dp", "seq")),
            P(None, ("dp", "seq")),
            P(None, ("dp", "seq"), None),
            P(None, ("dp", "seq"), None),
            P(None, ("dp", "seq"), None),
            P(None, ("dp", "seq"), None),
            P(None, ("dp", "seq")),
            P(None, ("dp", "seq")),
            P(None, ("dp", "seq"), None),
            P(None, ("dp", "seq")),
            P(None, ("dp", "seq"), None),
            P(None, ("dp", "seq")),
            P(),
        ),
        check_vma=False,
    )
```

profile of v0, /device:TPU:0, one launch (start us, length us, event | category | flops | bytes accessed | tf_op | source)
XLA Modules:
  0.0 2187.5 jit_solution(6449019602425621920)
XLA Ops:
  18.7 43.3 %all-reduce.16 = (bf16[768]{0:T(1024)(128)(2,1)S(1)}, bf16[768]{0:T(1024)(128)(2,1)S(1)}, bf16[768]{0:T(1024)(128)(2,1)S(1)}, bf16[3072]{0:T(1024)(128)(2,1)S(1)...) all-reduce(bf16[768]{0:T(1024)(128)(2,1)S(1)} %dynamic-update-slice, ...), channel_id=3, replica_groups=mesh['dp'=8,'seq'=4] {'dp','seq'}, use_global_device_ids=true, to_apply=%add.1 | all-reduce | flops 13824 | bytes 55296
  71.0 53.8 %all-gather.49.cloned.1.call-done = bf16[1,768,768]{2,1,0:T(8,128)(2,1)} async-done(((bf16[1,24,768]{2,1,0:T(8,128)(2,1)}), bf16[1,768,768]{2,1,0:T(8,128)(2,1)}) %all-gather.49.cloned.1.call-update) | async-done | bytes 1179664 | tf_op jit(solution)/shard_map/all_gather | solution.py:129
  133.7 47.5 %all-gather.53.cloned.1.call-done = bf16[1,768,768]{2,1,0:T(8,128)(2,1)} async-done(((bf16[1,24,768]{2,1,0:T(8,128)(2,1)}), bf16[1,768,768]{2,1,0:T(8,128)(2,1)}) %all-gather.53.cloned.1.call-update) | async-done | bytes 1179664 | tf_op jit(solution)/shard_map/all_gather | solution.py:127
  183.2 18.5 all-gather.57.cloned.1.call-done
  209.8 12.5 multiply_bitcast_fusion.1
  257.6 22.5 %all-gather.59.cloned.1.call-done = bf16[1,768,768]{2,1,0:T(8,128)(2,1)} async-done(((bf16[1,24,768]{2,1,0:T(8,128)(2,1)}), bf16[1,768,768]{2,1,0:T(8,128)(2,1)}) %all-gather.59.cloned.1.call-update) | async-done | bytes 1179664 | tf_op jit(solution)/shard_map/all_gather | solution.py:130
  282.2 63.9 %all-gather.61.cloned.1.call-done = bf16[1,768,3072]{2,1,0:T(8,128)(2,1)} async-done(((bf16[1,24,3072]{2,1,0:T(8,128)(2,1)}), bf16[1,768,3072]{2,1,0:T(8,128)(2,1)}) %all-gather.61.cloned.1.call-update) | async-done | bytes 4718608 | tf_op jit(solution)/shard_map/all_gather | solution.py:133
  351.6 59.9 %all-gather.63.cloned.1.call-done = bf16[1,3072,768]{2,1,0:T(8,128)(2,1)} async-done(((bf16[1,96,768]{2,1,0:T(8,128)(2,1)}), bf16[1,3072,768]{2,1,0:T(8,128)(2,1)}) %all-gather.63.cloned.1.call-update) | async-done | bytes 4718608 | tf_op jit(solution)/shard_map/all_gather | solution.py:135
  418.0 48.7 %all-gather.71.cloned.1.call-done = bf16[1,768,768]{2,1,0:T(8,128)(2,1)} async-done(((bf16[1,24,768]{2,1,0:T(8,128)(2,1)}), bf16[1,768,768]{2,1,0:T(8,128)(2,1)}) %all-gather.71.cloned.1.call-update) | async-done | bytes 1179664 | tf_op jit(solution)/shard_map/all_gather | solution.py:128
  469.3 53.0 %all-gather.65.cloned.1.call-done = bf16[1,768,768]{2,1,0:T(8,128)(2,1)} async-done(((bf16[1,24,768]{2,1,0:T(8,128)(2,1)}), bf16[1,768,768]{2,1,0:T(8,128)(2,1)}) %all-gather.65.cloned.1.call-update) | async-done | bytes 1179664 | tf_op jit(solution)/shard_map/all_gather | solution.py:129
  527.3 50.8 %all-gather.69.cloned.1.call-done = bf16[1,768,768]{2,1,0:T(8,128)(2,1)} async-done(((bf16[1,24,768]{2,1,0:T(8,128)(2,1)}), bf16[1,768,768]{2,1,0:T(8,128)(2,1)}) %all-gather.69.cloned.1.call-update) | async-done | bytes 1179664 | tf_op jit(solution)/shard_map/all_gather | solution.py:127
  580.0 18.6 all-gather.73.cloned.1.call-done
  609.1 12.2 multiply_bitcast_fusion
  658.0 19.1 all-gather.75.cloned.1.call-done
  680.9 62.1 %all-gather.77.cloned.1.call-done = bf16[1,768,3072]{2,1,0:T(8,128)(2,1)} async-done(((bf16[1,24,3072]{2,1,0:T(8,128)(2,1)}), bf16[1,768,3072]{2,1,0:T(8,128)(2,1)}) %all-gather.77.cloned.1.call-update) | async-done | bytes 4718608 | tf_op jit(solution)/shard_map/all_gather | solution.py:133
  748.6 59.6 %all-gather.79.cloned.1.call-done = bf16[1,3072,768]{2,1,0:T(8,128)(2,1)} async-done(((bf16[1,96,768]{2,1,0:T(8,128)(2,1)}), bf16[1,3072,768]{2,1,0:T(8,128)(2,1)}) %all-gather.79.cloned.1.call-update) | async-done | bytes 4718608 | tf_op jit(solution)/shard_map/all_gather | solution.py:135
  822.3 12.4 multiply_reduce_fusion.1
  835.6 13.7 fusion.256
  849.3 11.9 copy.106
  880.7 9.8 fusion.68
  910.1 27.4 %reduce-scatter.7.cloned.1.call-done = bf16[1,256,768]{1,2,0:T(8,128)(2,1)} async-done(((bf16[1,1024,768]{1,2,0:T(8,128)(2,1)}), bf16[1,256,768]{1,2,0:T(8,128)(2,1)}) %reduce-scatter.7.cloned.1.call-update) | async-done | bytes 393232 | tf_op jit(solution)/shard_map/reduce_scatter | solution.py:343
  955.9 12.3 multiply_reduce_fusion
  968.1 13.5 fusion.255
  981.7 12.0 copy.113
  1137.9 9.3 dynamic-update-slice.21
  1156.6 9.3 dynamic-update-slice.23
  1168.9 28.8 %dynamic-update-slice.26 = f32[32,221400]{1,0:T(8,128)} dynamic-update-slice(f32[32,221400]{1,0:T(8,128)} %dynamic-update-slice.25, f32[32,73728]{1,0:T(8,128)} %reshape.1512, s32[]{} %constant.349, s32[]{} %constant.357) | dynamic-update-slice | bytes 18874372
  1199.2 28.4 %dynamic-update-slice.28 = f32[32,221400]{1,0:T(8,128)} dynamic-update-slice(f32[32,221400]{1,0:T(8,128)} %dynamic-update-slice.27, f32[32,73728]{1,0:T(8,128)} %reshape.1514, s32[]{} %constant.349, s32[]{} %constant.359) | dynamic-update-slice | bytes 18874372
  1288.8 28.8 %dynamic-update-slice.38 = f32[32,221400]{1,0:T(8,128)} dynamic-update-slice(f32[32,221400]{1,0:T(8,128)} %dynamic-update-slice.37, f32[32,73728]{1,0:T(8,128)} %reshape.1498, s32[]{} %constant.349, s32[]{} %constant.357) | dynamic-update-slice | bytes 18874372
  1319.1 28.3 %dynamic-update-slice.40 = f32[32,221400]{1,0:T(8,128)} dynamic-update-slice(f32[32,221400]{1,0:T(8,128)} %dynamic-update-slice.39, f32[32,73728]{1,0:T(8,128)} %reshape.1500, s32[]{} %constant.349, s32[]{} %constant.359) | dynamic-update-slice | bytes 18874372
  1352.1 41.6 %all-reduce.14 = (f32[]{:T(128)}, f32[]{:T(128)}) all-reduce(f32[]{:T(128)S(6)} %add.505, f32[]{:T(128)S(6)} %select_n.177), channel_id=1, replica_groups=mesh['dp'=8,'seq'=4] {'dp','seq'}, use_global_device_ids=true, to_apply=%region_56.57 | all-reduce | flops 2 | bytes 16 | tf_op jit(solution)/shard_map/psum | solution.py:391
  1402.5 754.4 %all-reduce.19.cloned.1.call-done = (f32[32,221400]{1,0:T(8,128)}, f32[32,221400]{1,0:T(8,128)}) async-done(((f32[32,221400]{1,0:T(8,128)}, f32[32,221400]{1,0:T(8,128)}), (f32[32,221400]{1,0:T(8,128)}, f32[32,221400]{1,0:T(8,128)})) %all-reduce.19.cloned.1.call-update) | async-done | bytes 56678416
  (578 shorter events, 481.4 us)
Async XLA Ops:
  7.2 117.7 %copy-start.1 = (bf16[1,256,768]{2,1,0:T(8,128)(2,1)S(1)}, bf16[1,256,768]{2,1,0:T(8,128)(2,1)}, u32[]{:S(2)}) copy-start(bf16[1,256,768]{2,1,0:T(8,128)(2,1)} %param.27) | copy-start | bytes 1179652
  7.2 61.1 %all-gather.55.cloned.1.call-start = ((), (), s32[]{:S(2)}) async-start(), calls=%async_computation.11 | async-start | bytes 1216512 | tf_op jit(solution)/shard_map/all_gather | solution.py:128
  8.7 116.1 %all-gather.49.cloned.1.call-start = ((), (), s32[]{:S(2)}) async-start(), calls=%async_computation.8 | async-start | bytes 1216512 | tf_op jit(solution)/shard_map/all_gather | solution.py:129
  10.2 171.0 %all-gather.53.cloned.1.call-start = ((), (), s32[]{:S(2)}) async-start(), calls=%async_computation.10 | async-start | bytes 1216512 | tf_op jit(solution)/shard_map/all_gather | solution.py:127
  11.7 190.0 %all-gather.57.cloned.1.call-start = ((), (), s32[]{:S(2)}) async-start(), calls=%async_computation.12 | async-start | bytes 1966080 | tf_op jit(solution)/shard_map/all_gather | solution.py:174
  62.1 119.1 %copy-start.44 = (f32[768]{0:T(1024)}, f32[768]{0:T(1024)S(1)}, u32[]{:S(2)}) copy-start(f32[768]{0:T(1024)S(1)} %convert_element_type.349) | copy-start | bytes 9220
  62.1 119.1 %copy-start.57 = (f32[768]{0:T(1024)}, f32[768]{0:T(1024)S(1)}, u32[]{:S(2)}) copy-start(f32[768]{0:T(1024)S(1)} %convert_element_type.350) | copy-start | bytes 9220
  63.2 118.0 %copy-start.68 = (f32[256]{0:T(256)}, f32[256]{0:T(256)S(1)}, u32[]{:S(2)}) copy-start(f32[256]{0:T(256)S(1)} %broadcast_multiply_fusion.3) | copy-start | bytes 3076
  64.5 116.6 %copy-start.70 = (f32[256]{0:T(256)}, f32[256]{0:T(256)S(1)}, u32[]{:S(2)}) copy-start(f32[256]{0:T(256)S(1)} %fusion.229) | copy-start | bytes 3076
  71.0 176.3 %all-gather.51.cloned.1.call-start = ((), (), s32[]{:S(2)}) async-start(), calls=%async_computation.9 | async-start | bytes 1966080 | tf_op jit(solution)/shard_map/all_gather | solution.py:175
  127.4 152.6 %all-gather.59.cloned.1.call-start = ((), (), s32[]{:S(2)}) async-start(), calls=%async_computation.13 | async-start | bytes 1216512 | tf_op jit(solution)/shard_map/all_gather | solution.py:130
  128.2 217.9 %all-gather.61.cloned.1.call-start = ((), (), s32[]{:S(2)}) async-start(), calls=%async_computation.14 | async-start | bytes 4866048 | tf_op jit(solution)/shard_map/all_gather | solution.py:133
  129.0 282.5 %all-gather.63.cloned.1.call-start = ((), (), s32[]{:S(2)}) async-start(), calls=%async_computation.15 | async-start | bytes 4866048 | tf_op jit(solution)/shard_map/all_gather | solution.py:135
  129.8 336.9 %all-gather.71.cloned.1.call-start = ((), (), s32[]{:S(2)}) async-start(), calls=%async_computation.19 | async-start | bytes 1216512 | tf_op jit(solution)/shard_map/all_gather | solution.py:128
  130.5 391.8 %all-gather.65.cloned.1.call-start = ((), (), s32[]{:S(2)}) async-start(), calls=%async_computation.16 | async-start | bytes 1216512 | tf_op jit(solution)/shard_map/all_gather | solution.py:129
  131.1 446.9 %all-gather.69.cloned.1.call-start = ((), (), s32[]{:S(2)}) async-start(), calls=%async_computation.18 | async-start | bytes 1216512 | tf_op jit(solution)/shard_map/all_gather | solution.py:127
  131.9 466.7 %all-gather.73.cloned.1.call-start = ((), (), s32[]{:S(2)}) async-start(), calls=%async_computation.20 | async-start | bytes 1966080 | tf_op jit(solution)/shard_map/all_gather | solution.py:174
  132.7 213.4 %copy-start.54 = (f32[768]{0:T(1024)}, f32[768]{0:T(1024)S(1)}, u32[]{:S(2)}) copy-start(f32[768]{0:T(1024)S(1)} %convert_element_type.352) | copy-start | bytes 9220
  132.7 285.0 %copy-start.66 = (f32[768]{0:T(1024)}, f32[768]{0:T(1024)S(1)}, u32[]{:S(2)}) copy-start(f32[768]{0:T(1024)S(1)} %convert_element_type.355) | copy-start | bytes 9220
  281.9 129.6 %copy-start.12 = (f32[1,256,768]{2,1,0:T(8,128)}, f32[1,256,768]{2,1,0:T(8,128)S(1)}, u32[]{:S(2)}) copy-start(f32[1,256,768]{2,1,0:T(8,128)S(1)} %get-tuple-element.598) | copy-start | bytes 2359300
  416.8 260.3 %copy-start.5 = (f32[1,256,768]{2,1,0:T(8,128)}, f32[1,256,768]{2,1,0:T(8,128)S(1)}, u32[]{:S(2)}) copy-start(f32[1,256,768]{2,1,0:T(8,128)S(1)} %get-tuple-element.600) | copy-start | bytes 2359300
  417.8 108.9 %copy-start.120 = (bf16[768]{0:T(1024)(128)(2,1)S(1)}, bf16[768]{0:T(1024)(128)(2,1)}, u32[]{:S(2)}) copy-start(bf16[768]{0:T(1024)(128)(2,1)} %get-tuple-element.551) | copy-start | bytes 4612
  417.8 109.5 %copy-start.92 = (f32[256]{0:T(256)}, f32[256]{0:T(256)S(1)}, u32[]{:S(2)}) copy-start(f32[256]{0:T(256)S(1)} %fusion.231) | copy-start | bytes 3076
  469.2 165.3 %all-gather.67.cloned.1.call-start = ((), (), s32[]{:S(2)}) async-start(), calls=%async_computation.17 | async-start | bytes 1966080 | tf_op jit(solution)/shard_map/all_gather | solution.py:175
  524.8 152.3 %all-gather.75.cloned.1.call-start = ((), (), s32[]{:S(2)}) async-start(), calls=%async_computation.21 | async-start | bytes 1216512 | tf_op jit(solution)/shard_map/all_gather | solution.py:130
  525.4 217.6 %all-gather.77.cloned.1.call-start = ((), (), s32[]{:S(2)}) async-start(), calls=%async_computation.22 | async-start | bytes 4866048 | tf_op jit(solution)/shard_map/all_gather | solution.py:133
  526.0 282.3 %all-gather.79.cloned.1.call-start = ((), (), s32[]{:S(2)}) async-start(), calls=%async_computation.23 | async-start | bytes 4866048 | tf_op jit(solution)/shard_map/all_gather | solution.py:135
  526.6 380.5 %reduce-scatter.5.cloned.1.call-start = ((), (), s32[]{:S(2)}) async-start(), calls=%async_computation.4 | async-start | bytes 1966080 | tf_op jit(solution)/shard_map/reduce_scatter | solution.py:340
  880.6 56.9 %reduce-scatter.7.cloned.1.call-start = ((), (), s32[]{:S(2)}) async-start(), calls=%async_computation.5 | async-start | bytes 1966080 | tf_op jit(solution)/shard_map/reduce_scatter | solution.py:343
  890.5 340.3 %reduce-scatter.9.cloned.1.call-start = ((), (), s32[]{:S(2)}) async-start(), calls=%async_computation.6 | async-start | bytes 1966080 | tf_op jit(solution)/shard_map/reduce_scatter | solution.py:340
  1010.0 222.7 %reduce-scatter.11.cloned.1.call-start = ((), (), s32[]{:S(2)}) async-start(), calls=%async_computation.7 | async-start | bytes 1966080 | tf_op jit(solution)/shard_map/reduce_scatter | solution.py:343
  1066.0 1091.0 %all-reduce.19.cloned.1.call-start = ((), (), s32[]{:S(2)}) async-start(), calls=%async_computation.24 | async-start | bytes 113377280
  (122 other events, 2396.8 us)
Sparse Core Ops, SparseCore 0:
  11.5 56.7 all-gather.54
  71.7 53.0 all-gather.48
  128.3 52.8 all-gather.52
  183.2 18.5 all-gather.56
  203.7 19.6 all-gather.50
  226.1 53.9 all-gather.58
  283.6 62.4 all-gather.60
  349.6 61.9 all-gather.62
  414.4 52.2 all-gather.70
  469.4 52.8 all-gather.64
  525.2 52.8 all-gather.68
  580.0 18.5 all-gather.72
  600.7 19.6 all-gather.66
  623.1 53.9 all-gather.74
  680.4 62.4 all-gather.76
  746.3 61.9 all-gather.78
  880.7 26.3 reduce-scatter.4
  909.5 28.0 reduce-scatter.6
  1010.1 28.0 reduce-scatter.8
  1066.1 28.3 reduce-scatter.10
  1349.0 807.9 all-reduce.18
where the time goes:
time: 2200 us; the launch traced here: 2190 us
  waiting for transfers between devices  1370 us (62%)
  local copies, waits for them, and re-layouts  344 us (16%)
  matrix products  232 us (11%)
  other arithmetic  109 us (5%)
  blocking collectives  106 us (5%)
    unnamed x22, waiting for transfers between devices  758 us
    unnamed x320, local copies, waits for them, and re-layouts  244 us
    dot_general x36, matrix products, product(): return jnp.einsum(form, left, right, preferred_element_type=jnp.float32)  178 us
    all_gather x2, waiting for transfers between devices, local(): lax.all_gather(weight_inner[layer_index], ('dp', 'seq'), axis=0, tiled=True)  126 us
    all_gather x2, waiting for transfers between devices, local(): lax.all_gather(weight_outer[layer_index], ('dp', 'seq'), axis=0, tiled=True)  120 us
    all_gather x2, waiting for transfers between devices, local(): lax.all_gather(weight_value[layer_index], ('dp', 'seq'), axis=0, tiled=True)  107 us
    all_gather x2, waiting for transfers between devices, local(): lax.all_gather(weight_query[layer_index], ('dp', 'seq'), axis=0, tiled=True)  98.3 us
    reshape x24, local copies, waits for them, and re-layouts, join_rows(): member.reshape(devices, -1)  59.9 us
  transfers between devices with their start and end apart: 21, of which 17 were waited for; matrix products, arithmetic and copies ran while one was open for 19% of the time, Pallas kernels for 0%

commit v1 on v0

--- a/solution.py
+++ b/solution.py
@@ -10,20 +10,6 @@
 share_level = 0.5
 select_strength = 2.0
 masked_value = -1e30
-
-
-def prefix(array, axis, combine, identity, reverse):
-    size, place = (lax.axis_size(axis), lax.axis_index(axis))
-    everything = lax.all_gather(array, axis)
-    start = jnp.broadcast_to(jnp.asarray(identity, array.dtype), array.shape)
-
-    def step(k, before):
-        at = size - 1 - k if reverse else k
-        reached = at > place if reverse else at < place
-        new = combine(before, everything[at])
-        return jnp.where(reached, new, before)
-
-    return lax.fori_loop(0, size, step, start)
 
 
 def layer_norm(hidden, gain, shift):
@@ -33,30 +19,91 @@
     return centered * lax.rsqrt(spread + norm_eps) * gain + shift
 
 
-def adding(earlier, later):
-    return earlier + later
-
-
 def product(left, right, form):
     return jnp.einsum(form, left, right, preferred_element_type=jnp.float32)
 
 
-def join_rows(members, devices):
-    return jnp.concatenate([member.reshape(devices, -1) for member in members], axis=1)
-
-
-def split_rows(joined, shapes, devices):
-    results = []
-    offset = 0
-    for shape in shapes:
-        count = 1
-        for extent in shape:
-            count = count * extent
-        count = count // devices
-        piece = joined[:, offset : offset + count]
-        results.append(piece.reshape((shape[0] // devices,) + tuple(shape[1:])))
-        offset = offset + count
-    return results
+def flip(array, axis, bit):
+    size = lax.axis_size(axis)
+    return lax.ppermute(array, axis, [(i, i ^ bit) for i in range(size)])
+
+
+def bits_of(axis):
+    size = lax.axis_size(axis)
+    return [1 << k for k in range(size.bit_length() - 1)]
+
+
+def upper(axis, bit):
+    return (lax.axis_index(axis) & bit) != 0
+
+
+def gather_line(array, axis):
+    blocks = array[None]
+    for bit in reversed(bits_of(axis)):
+        other = flip(blocks, axis, bit)
+        is_upper = upper(axis, bit)
+        low = jnp.where(is_upper, other, blocks)
+        high = jnp.where(is_upper, blocks, other)
+        blocks = jnp.stack([low, high])
+        blocks = blocks.reshape((-1,) + array.shape)
+    steps = len(bits_of(axis))
+    blocks = blocks.reshape((2,) * steps + array.shape)
+    order = tuple(reversed(range(steps))) + tuple(range(steps, blocks.ndim))
+    return blocks.transpose(order).reshape((-1,) + array.shape)
+
+
+def scatter_line(blocks, axis):
+    steps = len(bits_of(axis))
+    rest = blocks.shape[1:]
+    blocks = blocks.reshape((2,) * steps + rest)
+    for bit in bits_of(axis):
+        is_upper = upper(axis, bit)
+        low = lax.index_in_dim(blocks, 0, blocks.ndim - len(rest) - 1, False)
+        high = lax.index_in_dim(blocks, 1, blocks.ndim - len(rest) - 1, False)
+        keep = jnp.where(is_upper, high, low)
+        send = jnp.where(is_upper, low, high)
+        blocks = keep + flip(send, axis, bit)
+    return blocks
+
+
+def line_prefix(array, axis, reverse):
+    total = array
+    before = jnp.zeros_like(array)
+    for bit in bits_of(axis):
+        other = flip(total, axis, bit)
+        is_upper = upper(axis, bit)
+        take = jnp.logical_not(is_upper) if reverse else is_upper
+        before = before + jnp.where(take, other, 0.0)
+        total = total + other
+    return before, total
+
+
+def sum_all(array, axes):
+    for axis in axes:
+        for bit in bits_of(axis):
+            array = array + flip(array, axis, bit)
+    return array
+
+
+def pack_weights(w_query, w_key, w_value, w_output, w_inner, w_outer):
+    rows, width = w_query.shape
+    parts = w_inner.shape[1] // width
+    inner = w_inner.reshape(rows, parts, width).transpose(1, 0, 2)
+    outer = w_outer.reshape(parts, rows, width)
+    square = jnp.stack([w_query, w_key, w_value, w_output])
+    return jnp.concatenate([square, inner, outer])
+
+
+def unpack_outer(planes, devices):
+    parts, rows, width = planes.shape
+    split = planes.reshape(parts, devices, rows // devices, width)
+    return split.transpose(1, 0, 2, 3).reshape(parts * rows, width)
+
+
+def pack_outer(grad, parts, devices):
+    rows, width = grad.shape
+    split = grad.reshape(devices, parts, rows // (parts * devices), width)
+    return split.transpose(1, 0, 2, 3).reshape(parts, rows // parts, width)
 
 
 def local(
@@ -102,6 +149,39 @@
     strict_lower = (row_index[:, None] > row_index[None, :]).astype(jnp.float32)
     select_scale = select_strength / full_len
 
+    both = ("dp", "seq")
+    parts = weight_inner.shape[2] // width
+    vectors = jnp.concatenate(
+        [gain_attend, shift_attend, gain_mixer, shift_mixer, bias_outer, bias_inner], axis=1
+    )
+    vector_rows = gather_line(gather_line(vectors, "seq"), "dp")
+    per = width // devices
+    vector_rows = vector_rows.reshape(devices, layers, -1)
+    small = [
+        vector_rows[:, :, k * per : (k + 1) * per].transpose(1, 0, 2).reshape(layers, width)
+        for k in range(5)
+    ]
+    small.append(
+        vector_rows[:, :, 5 * per :].transpose(1, 0, 2).reshape(layers, parts * width)
+    )
+    whole = [
+        lax.all_gather(
+            pack_weights(
+                weight_query[k],
+                weight_key[k],
+                weight_value[k],
+                weight_output[k],
+                weight_inner[k],
+                weight_outer[k],
+            ),
+            both,
+            axis=1,
+            tiled=True,
+        )
+        for k in range(layers)
+    ]
+    w_outers = [unpack_outer(planes[4 + parts :], devices) for planes in whole]
+
     def score_block(query, keys_whole):
         scores = (
             product(query, keys_whole.reshape(seq_dev, full_len, heads, head), "sqhe,skhe->shqk")
@@ -119,36 +199,17 @@
     hidden = inputs.astype(jnp.float32)
     share_sum = jnp.zeros((), jnp.float32)
     saved = []
-    gathered = []
     for layer_index in range(layers):
-        params = (
-            lax.all_gather(gain_attend[layer_index], ("dp", "seq"), axis=0, tiled=True),
-            lax.all_gather(shift_attend[layer_index], ("dp", "seq"), axis=0, tiled=True),
-            lax.all_gather(weight_query[layer_index], ("dp", "seq"), axis=0, tiled=True),
-            lax.all_gather(weight_key[layer_index], ("dp", "seq"), axis=0, tiled=True),
-            lax.all_gather(weight_value[layer_index], ("dp", "seq"), axis=0, tiled=True),
-            lax.all_gather(weight_output[layer_index], ("dp", "seq"), axis=0, tiled=True),
-            lax.all_gather(gain_mixer[layer_index], ("dp", "seq"), axis=0, tiled=True),
-            lax.all_gather(shift_mixer[layer_index], ("dp", "seq"), axis=0, tiled=True),
-            lax.all_gather(weight_inner[layer_index], ("dp", "seq"), axis=0, tiled=True),
-            lax.all_gather(bias_inner[layer_index], ("dp", "seq"), axis=0, tiled=True),
-            lax.all_gather(weight_outer[layer_index], ("dp", "seq"), axis=0, tiled=True),
-            lax.all_gather(bias_outer[layer_index], ("dp", "seq"), axis=0, tiled=True),
-        )
-        (
-            forward_gain_a,
-            forward_shift_a,
-            forward_w_query,
-            forward_w_key,
-            forward_w_value,
-            forward_w_output,
-            forward_gain_m,
-            forward_shift_m,
-            forward_w_inner,
-            forward_b_inner,
-            forward_w_outer,
-            forward_b_outer,
-        ) = params
+        planes = whole[layer_index]
+        forward_gain_a, forward_shift_a, forward_gain_m, forward_shift_m = (
+            small[k][layer_index] for k in range(4)
+        )
+        forward_b_outer, forward_b_inner = (small[k][layer_index] for k in (4, 5))
+        forward_w_query, forward_w_key, forward_w_value, forward_w_output = (
+            planes[k] for k in range(4)
+        )
+        forward_w_inner = planes[4 : 4 + parts].transpose(1, 0, 2).reshape(width, parts * width)
+        forward_w_outer = w_outers[layer_index]
         forward_normed = (
             layer_norm(
                 hidden, forward_gain_a.astype(jnp.float32), forward_shift_a.astype(jnp.float32)
@@ -171,11 +232,17 @@
             .astype(jnp.bfloat16)
             .reshape(seq_dev, local_len, width)
         )
-        forward_keys_whole = lax.all_gather(forward_keys, "seq", axis=1, tiled=True)
-        forward_values_whole = lax.all_gather(forward_values, "seq", axis=1, tiled=True)
+        forward_keys_whole = (
+            gather_line(forward_keys, "seq").transpose(1, 0, 2, 3).reshape(seq_dev, full_len, width)
+        )
+        forward_values_whole = (
+            gather_line(forward_values, "seq")
+            .transpose(1, 0, 2, 3)
+            .reshape(seq_dev, full_len, width)
+        )
         forward_scores, forward_select = score_block(forward_query, forward_keys_whole)
         column = jnp.sum(forward_select, axis=1)
-        forward_before = prefix(column, "seq", adding, jnp.zeros_like(column), False)
+        forward_before, totals = line_prefix(column, "seq", False)
         logits = logits_from(forward_scores, forward_select, forward_before)
         peak = jnp.max(logits, axis=-1, keepdims=True)
         expo = jnp.exp(logits - peak)
@@ -211,7 +278,6 @@
             forward_active, forward_w_outer, preferred_element_type=jnp.float32
         ) + forward_b_outer.astype(jnp.float32)
         result = forward_after + outer.reshape(hidden.shape)
-        totals = forward_before + column
         share = jnp.where(
             is_last,
             jnp.sum(jnp.where(valid_keys, jnp.minimum(totals / share_level, 1.0), 0.0)),
@@ -236,38 +302,15 @@
         hidden = result
         share_sum = share_sum + share
         saved.append(forward_kept)
-        gathered.append(params)
     grad_hidden = cotangent
-    layer_grads = [None] * layers
+    reduced = [None] * layers
+    vector_grads = [None] * layers
     for layer_index in reversed(range(layers)):
-        params = (
-            lax.all_gather(gain_attend[layer_index], ("dp", "seq"), axis=0, tiled=True),
-            lax.all_gather(shift_attend[layer_index], ("dp", "seq"), axis=0, tiled=True),
-            lax.all_gather(weight_query[layer_index], ("dp", "seq"), axis=0, tiled=True),
-            lax.all_gather(weight_key[layer_index], ("dp", "seq"), axis=0, tiled=True),
-            lax.all_gather(weight_value[layer_index], ("dp", "seq"), axis=0, tiled=True),
-            lax.all_gather(weight_output[layer_index], ("dp", "seq"), axis=0, tiled=True),
-            lax.all_gather(gain_mixer[layer_index], ("dp", "seq"), axis=0, tiled=True),
-            lax.all_gather(shift_mixer[layer_index], ("dp", "seq"), axis=0, tiled=True),
-            lax.all_gather(weight_inner[layer_index], ("dp", "seq"), axis=0, tiled=True),
-            lax.all_gather(bias_inner[layer_index], ("dp", "seq"), axis=0, tiled=True),
-            lax.all_gather(weight_outer[layer_index], ("dp", "seq"), axis=0, tiled=True),
-            lax.all_gather(bias_outer[layer_index], ("dp", "seq"), axis=0, tiled=True),
-        )
-        (
-            gain_a,
-            shift_a,
-            w_query,
-            w_key,
-            w_value,
-            w_output,
-            gain_m,
-            shift_m,
-            w_inner,
-            b_inner,
-            w_outer,
-            b_outer,
-        ) = params
+        planes = whole[layer_index]
+        gain_a, shift_a, gain_m, shift_m = (small[k][layer_index] for k in range(4))
+        w_query, w_key, w_value, w_output = (planes[k] for k in range(4))
+        w_inner = planes[4 : 4 + parts].transpose(1, 0, 2).reshape(width, parts * width)
+        w_outer = w_outers[layer_index]
         (
             backward_hidden,
             normed,
@@ -313,7 +356,7 @@
         grad_logits = probs * (grad_probs - delta)
         grad_carried = -jnp.sum(grad_logits, axis=1)
         column_back = jnp.sum(grad_carried, axis=1)
-        later_rows = prefix(column_back, "seq", adding, jnp.zeros_like(column_back), True)
+        later_rows, _ = line_prefix(column_back, "seq", True)
         grad_select = later_rows[:, None, :] + jnp.einsum(
             "qr,sqk->srk", strict_lower, grad_carried, precision=highest
         )
@@ -337,17 +380,20 @@
         key_part = (product(grad_scores, backward_query, "shqk,sqhe->skhe") * 0.125).reshape(
             seq_dev, full_len, width
         )
-        grad_keys = lax.psum_scatter(
-            key_part.astype(jnp.bfloat16), "seq", scatter_dimension=1, tiled=True
-        ).astype(jnp.float32)
-        grad_vals = lax.psum_scatter(
-            grad_values.reshape(seq_dev, full_len, width).astype(jnp.bfloat16),
+        grad_keys = scatter_line(
+            key_part.astype(jnp.bfloat16)
+            .reshape(seq_dev, seq_count, local_len, width)
+            .transpose(1, 0, 2, 3),
             "seq",
-            scatter_dimension=1,
-            tiled=True,
-        ).astype(jnp.float32)
-        grad_keys = grad_keys.astype(jnp.bfloat16).reshape(-1, width)
-        grad_vals = grad_vals.astype(jnp.bfloat16).reshape(-1, width)
+        )
+        grad_vals = scatter_line(
+            grad_values.astype(jnp.bfloat16)
+            .reshape(seq_dev, seq_count, local_len, width)
+            .transpose(1, 0, 2, 3),
+            "seq",
+        )
+        grad_keys = grad_keys.reshape(-1, width)
+        grad_vals = grad_vals.reshape(-1, width)
         grad_w_query = product(normed, grad_query, "tc,td->cd")
         grad_w_key = product(normed, grad_keys, "tc,td->cd")
         grad_w_value = product(normed, grad_vals, "tc,td->cd")
@@ -362,49 +408,64 @@
         hidden_part, grad_gain_a, grad_shift_a = norm_back_one(
             grad_normed.reshape(backward_hidden.shape)
         )
-        grads = (
-            grad_gain_a,
-            grad_shift_a,
-            grad_w_query,
-            grad_w_key,
-            grad_w_value,
-            grad_w_output,
-            grad_gain_m,
-            grad_shift_m,
-            grad_w_inner,
-            grad_b_inner,
-            grad_w_outer,
-            grad_b_outer,
-        )
-        grad_hidden, grads = (grad_after + hidden_part, grads)
-        shapes = [member.shape for member in grads]
-        joined = join_rows(grads, devices)
-        reduced = lax.psum_scatter(joined, ("dp", "seq"), scatter_dimension=0, tiled=True)
-        layer_grads[layer_index] = split_rows(reduced, shapes, devices)
-    stacked = tuple(
-        (
-            jnp.stack([layer_grads[layer_index][member] for layer_index in range(layers)])
-            for member in range(12)
-        )
-    )
+        grad_hidden = grad_after + hidden_part
+        low = jnp.bfloat16
+        pieces = [
+            piece.astype(low)[None]
+            for piece in (grad_w_query, grad_w_key, grad_w_value, grad_w_output)
+        ]
+        pieces.append(grad_w_inner.astype(low).reshape(width, parts, width).transpose(1, 0, 2))
+        pieces.append(pack_outer(grad_w_outer.astype(low), parts, devices))
+        reduced[layer_index] = lax.psum_scatter(
+            jnp.concatenate(pieces), both, scatter_dimension=1, tiled=True
+        ).astype(jnp.float32)
+        vector_grads[layer_index] = jnp.concatenate(
+            [
+                grad_gain_a,
+                grad_shift_a,
+                grad_gain_m,
+                grad_shift_m,
+                grad_b_outer,
+                grad_b_inner,
+            ]
+        )
     count = jnp.where(is_last, jnp.sum(lengths).astype(jnp.float32), 0.0)
-    share_all, count_all = lax.psum((share_sum, count), ("dp", "seq"))
-    selected = share_all / (layers * count_all)
+    flat = jnp.concatenate(
+        vector_grads + [jnp.broadcast_to(share_sum, (128,)), jnp.broadcast_to(count, (128,))]
+    )
+    flat = sum_all(flat.reshape(-1, 128), ("seq", "dp")).reshape(-1)
+    size = (5 + parts) * width
+    selected = flat[layers * size] / (layers * flat[layers * size + 128])
+    place = lax.axis_index("dp") * seq_count + lax.axis_index("seq")
+    vec = flat[: layers * size].reshape(layers, size)
+
+    def mine(first, length):
+        return lax.dynamic_slice_in_dim(
+            vec[:, first * width : first * width + length], place * (length // devices),
+            length // devices, axis=1,
+        )
+
+    rows = width // devices
+    stack = jnp.stack(reduced)
+    grads_inner = (
+        stack[:, 4 : 4 + parts].transpose(0, 2, 1, 3).reshape(layers, rows, parts * width)
+    )
+    grads_outer = stack[:, 4 + parts :].reshape(layers, parts * rows, width)
     return (
         hidden,
         grad_hidden,
-        stacked[0],
-        stacked[1],
-        stacked[2],
-        stacked[3],
-        stacked[4],
-        stacked[5],
-        stacked[6],
-        stacked[7],
-        stacked[8],
-        stacked[9],
-        stacked[10],
-        stacked[11],
+        mine(0, width),
+        mine(1, width),
+        stack[:, 0],
+        stack[:, 1],
+        stack[:, 2],
+        stack[:, 3],
+        mine(2, width),
+        mine(3, width),
+        grads_inner,
+        mine(5, parts * width),
+        grads_outer,
+        mine(4, width),
         selected,
     )
 

time: 2200 us -> 858 us (0.39)
  waiting for transfers between devices: 1370 us -> 274 us
  local copies, waits for them, and re-layouts: 344 us -> 213 us
  blocking collectives: 106 us -> 0 us
  matrix products: 232 us -> 184 us
  starting transfers between devices: 1.1 us -> 29.8 us
    unnamed x22 -> x6, waiting for transfers between devices: 758 us -> 123 us
    all_gather x16 -> x2, waiting for transfers between devices: 582 us -> 82.2 us  [local(): lax.all_gather(pack_weights(weight_query[k], weight_key[k], weight_value[...]
    unnamed x320 -> x299, local copies, waits for them, and re-layouts: 244 us -> 93.4 us
    ppermute x0 -> x34, waiting for transfers between devices: none -> 68.7 us  [flip(): return lax.ppermute(array, axis, [(i, i ^ bit) for i in range(size)])]
    reshape x24 -> x2, local copies, waits for them, and re-layouts: 59.9 us -> 0.9 us  [the longest x1 0.86 us: local(): stack[:, 4:4 + parts].transpose(0, 2, 1, 3)]
    unnamed x1 -> x0, blocking collectives: 43.3 us -> none
    psum x1 -> x0, blocking collectives: 41.6 us -> none  [local(): share_all, count_all = lax.psum((share_sum, count), ('dp', 'seq'))]
    transpose x0 -> x12, local copies, waits for them, and re-layouts: none -> 35.9 us  [the longest x6 15.9 us: gather_line(): return blocks.transpose(order).reshape((-1,) + array.shape)]
  transfers between devices with their start and end apart: 21 -> 38, of which waited for: 17 -> 17; matrix products, arithmetic and copies ran while one was open for 19% -> 48% of each run, Pallas kernels for 0% -> 0%
where the time goes in v1:
time: 858 us; the launch traced here: 849 us
  waiting for transfers between devices  274 us (32%)
  local copies, waits for them, and re-layouts  213 us (25%)
  matrix products  184 us (21%)
  other arithmetic  128 us (15%)
  starting transfers between devices  29.8 us (3%)
  between operations  21.1 us (2%)
    dot_general x36, matrix products, product(): return jnp.einsum(form, left, right, preferred_element_type=jnp.float32)  142 us
    unnamed x6, waiting for transfers between devices  123 us
    unnamed x299, local copies, waits for them, and re-layouts  93.4 us
    all_gather x2, waiting for transfers between devices, local(): lax.all_gather(pack_weights(weight_query[k], weight_key[k], weight_value[...  82.2 us
    ppermute x34, waiting for transfers between devices, flip(): return lax.ppermute(array, axis, [(i, i ^ bit) for i in range(size)])  68.7 us
    reduce_sum x2, other arithmetic, local(): grad_carried = -jnp.sum(grad_logits, axis=1)  31.1 us
    ppermute x34, starting transfers between devices, flip(): return lax.ppermute(array, axis, [(i, i ^ bit) for i in range(size)])  29.7 us
    mul x2, other arithmetic, score_block(): product(query, keys_whole.reshape(seq_dev, full_len, heads, head), 'sqhe,...  25.8 us
  transfers between devices with their start and end apart: 38, of which 17 were waited for; matrix products, arithmetic and copies ran while one was open for 48% of the time, Pallas kernels for 0%

profile of v1, /device:TPU:0, one launch (start us, length us, event | category | flops | bytes accessed | tf_op | source)
XLA Modules:
  0.0 848.7 jit_solution(15219640348943659436)
XLA Ops:
  37.9 82.2 %all-gather.3.cloned.1.call-done = bf16[12,768,768]{2,1,0:T(8,128)(2,1)} async-done(((bf16[12,24,768]{2,1,0:T(8,128)(2,1)}), bf16[12,768,768]{2,1,0:T(8,128)(2,1)}) %all-gather.3.cloned.1.call-update) | async-done | bytes 14155792 | tf_op jit(solution)/shard_map/all_gather | solution.py:168
  134.9 8.0 fusion.254
  142.9 6.8 copy.460
  164.6 7.6 fusion.270
  172.1 13.7 %multiply_bitcast_fusion.1 = f32[1,12,256,1024]{3,2,1,0:T(8,128)} fusion(f32[12,256,1024]{2,1,0:T(8,128)} %fusion.270), kind=kLoop, calls=%fused_computation.13 | loop fusion | flops 3145728 | bytes 25165824 | tf_op jit(solution)/shard_map/mul | solution.py:187
  203.3 7.6 fusion.239
  211.0 8.3 fusion
  237.0 7.2 collective-permute-done.13
  245.2 7.9 fusion.253
  253.1 6.6 copy.465
  281.1 7.7 fusion.271
  288.8 12.1 %multiply_bitcast_fusion = f32[1,12,256,1024]{3,2,1,0:T(8,128)} fusion(f32[12,256,1024]{2,1,0:T(8,128)} %fusion.271), kind=kLoop, calls=%fused_computation.12 | loop fusion | flops 3145728 | bytes 25165824 | tf_op jit(solution)/shard_map/mul | solution.py:187
  320.0 7.3 fusion.240
  327.4 8.7 %fusion.1 = f32[12,256]{1,0:T(8,128)S(1)} fusion(f32[12,256]{1,0:T(8,128)S(1)} %fusion.240, f32[256,1024]{1,0:T(8,128)S(1)} %copy.417, f32[12,256,1024]{2,1,0:T(8,128)} %fusion.271, pred[256,1024]{1,0:T(8,128)(4,1)S(1)} %fusion.120), kind=kLoop, calls=%fused_computation.15 | loop fusion | flops 15725568 | bytes 13918208 | tf_op jit(solution)/shard_map/reduce_sum | solution.py:249
  360.1 9.6 %fusion.53 = bf16[1,1024,12,64]{1,3,2,0:T(8,128)(2,1)} fusion(bf16[256,12,64]{0,2,1:T(8,128)(2,1)} %bitcast.768, f32[12,256]{1,0:T(8,128)S(1)} %log_add_fusion.1, f32[12,256,1024]{2,1,0:T(8,128)} %fusion.271, f32[256,1024]{1,0:T(8,128)S(1)} %copy.417, pred[256,1024]{1,0:T(8,128)(4,1)S(1)} %fusion.120), kind=kOutput, calls=%fused_computation.86 | convolution fusion | flops 419168256 | bytes 15872000 | tf_op jit(solution)/shard_map/shqk,sqhe->skhe/dot_general | solution.py:23
  369.7 10.8 %multiply_reduce_fusion.1 = (f32[12,256]{1,0:T(8,128)S(1)}, f32[12,256,1024]{2,1,0:T(8,128)}) fusion(f32[12,256]{1,0:T(8,128)S(1)} %log_add_fusion.1, f32[256,1024]{1,0:T(8,128)S(1)} %copy.417, f32[12,256,1024]{2,1,0:T(8,128)} %fusion.271, pred[256,1024]{1,0:T(8,128)(4,1)S(1)} %fusion.120, bf16[256,12,64]{0,2,1:T(8,128)(2,1)S(1)} %bitcast.769, ...), kind=kOutput, calls=%fused_computation.4 | convolution fusion | flops 421524480 | bytes 28467200 | tf_op jit(solution)/shard_map/sqhe,skhe->shqk/dot_general | solution.py:23
  390.1 17.0 %fusion.248 = (f32[256,1024]{1,0:T(8,128)}, f32[1024]{0:T(1024)S(1)}, f32[12,256,1024]{2,1,0:T(8,128)}) fusion(f32[12,256,1024]{2,1,0:T(8,128)} %get-tuple-element.153, f32[12,256]{1,0:T(8,128)S(1)} %get-tuple-element.152, f32[12,256]{1,0:T(8,128)S(1)} %log_add_fusion.1, f32[256,1024]{1,0:T(8,128)S(1)} %copy.417, f32[12,256,1024]{2,1,0:T(8,128)} %fusion.271, ...), kind=kLoop, calls=%fused_computation.448 | loop fusion | flops 24902656 | bytes 40136704 | tf_op jit(solution)/shard_map/reduce_sum | solution.py:357
  427.9 11.8 %copy.487 = f32[1,12,256,1024]{3,2,1,0:T(8,128)} copy(f32[1,12,256,1024]{3,2,1,0:T(8,128)} %bitcast.713) | data formatting | bytes 25165824
  443.4 6.9 fusion.56
  470.7 7.1 fusion.93
  482.2 9.1 %collective-permute-done.22 = bf16[1,256,768]{2,1,0:T(8,128)(2,1)S(1)} collective-permute-done((bf16[1,256,768]{2,1,0:T(8,128)(2,1)S(1)}, bf16[1,256,768]{2,1,0:T(8,128)(2,1)S(1)}, u32[]{:S(2)}, u32[]{:S(2)}) %collective-permute-start.22) | collective-permute-done | bytes 393248 | tf_op jit(solution)/shard_map/ppermute | solution.py:28
  491.4 7.8 collective-permute-done.20
  529.7 9.0 %fusion.50 = bf16[1,1024,12,64]{1,3,2,0:T(8,128)(2,1)} fusion(bf16[256,12,64]{0,2,1:T(8,128)(2,1)S(1)} %bitcast.766, f32[12,256]{1,0:T(8,128)S(1)} %log_add_fusion, f32[12,256,1024]{2,1,0:T(8,128)} %fusion.270, f32[256,1024]{1,0:T(8,128)S(1)} %copy-done.1, pred[256,1024]{1,0:T(8,128)(4,1)S(1)} %fusion.120), kind=kOutput, calls=%fused_computation.85 | convolution fusion | flops 419168256 | bytes 15872000 | tf_op jit(solution)/shard_map/shqk,sqhe->skhe/dot_general | solution.py:23
  541.7 9.3 %multiply_reduce_fusion = (f32[12,256]{1,0:T(8,128)S(1)}, f32[12,256,1024]{2,1,0:T(8,128)S(1)}) fusion(f32[12,256]{1,0:T(8,128)S(1)} %log_add_fusion, f32[256,1024]{1,0:T(8,128)S(1)} %copy-done.1, f32[12,256,1024]{2,1,0:T(8,128)} %fusion.270, pred[256,1024]{1,0:T(8,128)(4,1)S(1)} %fusion.120, bf16[256,12,64]{0,2,1:T(8,128)(2,1)S(1)} %bitcast.767, ...), kind=kOutput, calls=%fused_computation.1 | convolution fusion | flops 421524480 | bytes 28467200 | tf_op jit(solution)/shard_map/sqhe,skhe->shqk/dot_general | solution.py:23
  551.1 14.1 %fusion.247 = (f32[256,1024]{1,0:T(8,128)}, f32[1024]{0:T(1024)S(1)}, f32[12,256,1024]{2,1,0:T(8,128)}) fusion(f32[12,256,1024]{2,1,0:T(8,128)S(1)} %get-tuple-element.157, f32[12,256]{1,0:T(8,128)S(1)} %get-tuple-element.156, f32[12,256]{1,0:T(8,128)S(1)} %log_add_fusion, f32[256,1024]{1,0:T(8,128)S(1)} %copy-done.1, f32[12,256,1024]{2,1,0:T(8,128)} %fusion.270, ...), kind=kLoop, calls=%fused_computation.447 | loop fusion | flops 24902656 | bytes 40136704 | tf_op jit(solution)/shard_map/reduce_sum | solution.py:357
  589.8 12.0 %copy.488 = f32[1,12,256,1024]{3,2,1,0:T(8,128)} copy(f32[1,12,256,1024]{3,2,1,0:T(8,128)} %bitcast.712) | data formatting | bytes 25165824
  606.2 7.0 fusion.59
  630.3 6.6 fusion.90
  641.7 8.9 %collective-permute-done.28 = bf16[1,256,768]{2,1,0:T(8,128)(2,1)S(1)} collective-permute-done((bf16[1,256,768]{2,1,0:T(8,128)(2,1)S(1)}, bf16[1,256,768]{2,1,0:T(8,128)(2,1)S(1)}, u32[]{:S(2)}, u32[]{:S(2)}) %collective-permute-start.28) | collective-permute-done | bytes 393248 | tf_op jit(solution)/shard_map/ppermute | solution.py:28
  650.7 11.1 %collective-permute-done.26 = bf16[1,256,768]{2,1,0:T(8,128)(2,1)S(1)} collective-permute-done((bf16[1,256,768]{2,1,0:T(8,128)(2,1)S(1)}, bf16[1,256,768]{2,1,0:T(8,128)(2,1)S(1)}, u32[]{:S(2)}, u32[]{:S(2)}) %collective-permute-start.26) | collective-permute-done | bytes 393248 | tf_op jit(solution)/shard_map/ppermute | solution.py:28
  690.4 6.6 fusion.87
  714.0 122.7 %reduce-scatter.7.cloned.1.call-done = bf16[24,9216]{1,0:T(8,128)(2,1)} async-done(((bf16[768,9216]{1,0:T(8,128)(2,1)}), bf16[24,9216]{1,0:T(8,128)(2,1)}) %reduce-scatter.7.cloned.1.call-update) | async-done | bytes 442384
  (598 shorter events, 347.9 us)
Async XLA Ops:
  7.3 112.8 %all-gather.3.cloned.1.call-start = ((), (), s32[]{:S(2)}) async-start(), calls=%async_computation.2 | async-start | bytes 14598144 | tf_op jit(solution)/shard_map/all_gather | solution.py:168
  14.6 215.6 %all-gather.5.cloned.1.call-start = ((), (), s32[]{:S(2)}) async-start(), calls=%async_computation.3 | async-start | bytes 14598144 | tf_op jit(solution)/shard_map/all_gather | solution.py:168
  16.8 695.8 %reduce-scatter.9.cloned.1.call-start = ((), (), s32[]{:S(2)}) async-start(), calls=%async_computation.5 | async-start | bytes 14598144
  17.0 4.5 collective-permute-start
  22.8 4.8 collective-permute-start.2
  121.9 12.7 %collective-permute-start.7 = (bf16[1,1,256,768]{3,2,1,0:T(8,128)(2,1)S(1)}, bf16[1,1,256,768]{3,2,1,0:T(8,128)(2,1)S(1)}, u32[]{:S(2)}, u32[]{:S(2)}) collective-permute-start(bf16[1,1,256,768]{3,2,1,0:T(8,128)(2,1)S(1)} %fusion.99), channel_id=1, source_target_pairs={{0,2},{1,3},{2,0},{3,1},{4,6},{5,7},{6,4},{7,5},{8,10},{9,11},{10,... | collective-permute-start | bytes 1179656 | tf_op jit(solution)/shard_map/ppermute | solution.py:28
  128.0 26.8 %collective-permute-start.5 = (bf16[1,1,256,768]{3,2,1,0:T(8,128)(2,1)S(1)}, bf16[1,1,256,768]{3,2,1,0:T(8,128)(2,1)}, u32[]{:S(2)}, u32[]{:S(2)}) collective-permute-start(bf16[1,1,256,768]{3,2,1,0:T(8,128)(2,1)S(1)} %fusion.98), channel_id=1, source_target_pairs={{0,2},{1,3},{2,0},{3,1},{4,6},{5,7},{6,4},{7,5},{8,10},{9,11},{10,... | collective-permute-start | bytes 1179656 | tf_op jit(solution)/shard_map/ppermute | solution.py:28
  134.8 22.5 %collective-permute-start.8 = (bf16[2,1,256,768]{3,2,0,1:T(8,128)(2,1)S(1)}, bf16[2,1,256,768]{3,2,0,1:T(8,128)(2,1)}, u32[]{:S(2)}, u32[]{:S(2)}) collective-permute-start(bf16[2,1,256,768]{3,2,0,1:T(8,128)(2,1)S(1)} %maximum_bitcast_fusion.5), channel_id=1, source_target_pairs={{0,1},{1,0},{2,3},{3,2},{4,5},{5,4},{6,7},{7,6},{8,9},{9,8},{10,11... | collective-permute-start | bytes 2359304 | tf_op jit(solution)/shard_map/ppermute | solution.py:28
  156.8 30.8 %collective-permute-start.6 = (bf16[2,1,256,768]{3,2,0,1:T(8,128)(2,1)}, bf16[2,1,256,768]{3,2,0,1:T(8,128)(2,1)}, u32[]{:S(2)}, u32[]{:S(2)}) collective-permute-start(bf16[2,1,256,768]{3,2,0,1:T(8,128)(2,1)} %maximum_bitcast_fusion.4), channel_id=1, source_target_pairs={{0,1},{1,0},{2,3},{3,2},{4,5},{5,4},{6,7},{7,6},{8,9},{9,8},{10,11... | collective-permute-start | bytes 2359304 | tf_op jit(solution)/shard_map/ppermute | solution.py:28
  188.9 8.6 %collective-permute-start.10 = (f32[1,1024]{1,0:T(1,128)S(1)}, f32[1,1024]{1,0:T(1,128)S(1)}, u32[]{:S(2)}, u32[]{:S(2)}) collective-permute-start(f32[1,1024]{1,0:T(1,128)S(1)} %add.378), channel_id=1, source_target_pairs={{0,2},{1,3},{2,0},{3,1},{4,6},{5,7},{6,4},{7,5},{8,10},{9,11},{10,... | collective-permute-start | bytes 12296 | tf_op jit(solution)/shard_map/ppermute | solution.py:28
  232.1 12.1 %collective-permute-start.13 = (bf16[1,1,256,768]{3,2,1,0:T(8,128)(2,1)S(1)}, bf16[1,1,256,768]{3,2,1,0:T(8,128)(2,1)S(1)}, u32[]{:S(2)}, u32[]{:S(2)}) collective-permute-start(bf16[1,1,256,768]{3,2,1,0:T(8,128)(2,1)S(1)} %fusion.101), channel_id=1, source_target_pairs={{0,2},{1,3},{2,0},{3,1},{4,6},{5,7},{6,4},{7,5},{8,10},{9,11},{10,... | collective-permute-start | bytes 1179656 | tf_op jit(solution)/shard_map/ppermute | solution.py:28
  235.1 31.6 %collective-permute-start.11 = (bf16[1,1,256,768]{3,2,1,0:T(8,128)(2,1)}, bf16[1,1,256,768]{3,2,1,0:T(8,128)(2,1)}, u32[]{:S(2)}, u32[]{:S(2)}) collective-permute-start(bf16[1,1,256,768]{3,2,1,0:T(8,128)(2,1)} %fusion.100), channel_id=1, source_target_pairs={{0,2},{1,3},{2,0},{3,1},{4,6},{5,7},{6,4},{7,5},{8,10},{9,11},{10,... | collective-permute-start | bytes 1179656 | tf_op jit(solution)/shard_map/ppermute | solution.py:28
  245.2 24.2 %collective-permute-start.14 = (bf16[2,1,256,768]{3,2,0,1:T(8,128)(2,1)}, bf16[2,1,256,768]{3,2,0,1:T(8,128)(2,1)}, u32[]{:S(2)}, u32[]{:S(2)}) collective-permute-start(bf16[2,1,256,768]{3,2,0,1:T(8,128)(2,1)} %maximum_bitcast_fusion.7), channel_id=1, source_target_pairs={{0,1},{1,0},{2,3},{3,2},{4,5},{5,4},{6,7},{7,6},{8,9},{9,8},{10,11... | collective-permute-start | bytes 2359304 | tf_op jit(solution)/shard_map/ppermute | solution.py:28
  268.9 33.8 %collective-permute-start.12 = (bf16[2,1,256,768]{3,2,0,1:T(8,128)(2,1)}, bf16[2,1,256,768]{3,2,0,1:T(8,128)(2,1)}, u32[]{:S(2)}, u32[]{:S(2)}) collective-permute-start(bf16[2,1,256,768]{3,2,0,1:T(8,128)(2,1)} %maximum_bitcast_fusion.6), channel_id=1, source_target_pairs={{0,1},{1,0},{2,3},{3,2},{4,5},{5,4},{6,7},{7,6},{8,9},{9,8},{10,11... | collective-permute-start | bytes 2359304 | tf_op jit(solution)/shard_map/ppermute | solution.py:28
  304.0 10.3 %collective-permute-start.16 = (f32[1,1024]{1,0:T(1,128)S(1)}, f32[1,1024]{1,0:T(1,128)S(1)}, u32[]{:S(2)}, u32[]{:S(2)}) collective-permute-start(f32[1,1024]{1,0:T(1,128)S(1)} %add.398), channel_id=1, source_target_pairs={{0,2},{1,3},{2,0},{3,1},{4,6},{5,7},{6,4},{7,5},{8,10},{9,11},{10,... | collective-permute-start | bytes 12296 | tf_op jit(solution)/shard_map/ppermute | solution.py:28
  407.1 12.1 %collective-permute-start.17 = (f32[1,1024]{1,0:T(1,128)S(1)}, f32[1,1024]{1,0:T(1,128)S(1)}, u32[]{:S(2)}, u32[]{:S(2)}) collective-permute-start(f32[1,1024]{1,0:T(1,128)S(1)} %bitcast.796), channel_id=1, source_target_pairs={{0,1},{1,0},{2,3},{3,2},{4,5},{5,4},{6,7},{7,6},{8,9},{9,8},{10,11... | collective-permute-start | bytes 12296 | tf_op jit(solution)/shard_map/ppermute | solution.py:28
  419.2 20.5 %collective-permute-start.18 = (f32[1,1024]{1,0:T(1,128)S(1)}, f32[1,1024]{1,0:T(1,128)S(1)}, u32[]{:S(2)}, u32[]{:S(2)}) collective-permute-start(f32[1,1024]{1,0:T(1,128)S(1)} %add.417), channel_id=1, source_target_pairs={{0,2},{1,3},{2,0},{3,1},{4,6},{5,7},{6,4},{7,5},{8,10},{9,11},{10,... | collective-permute-start | bytes 12296 | tf_op jit(solution)/shard_map/ppermute | solution.py:28
  426.7 51.1 %collective-permute-start.21 = (bf16[2,1,256,768]{3,2,0,1:T(8,128)(2,1)}, bf16[2,1,256,768]{3,2,0,1:T(8,128)(2,1)}, u32[]{:S(2)}, u32[]{:S(2)}) collective-permute-start(bf16[2,1,256,768]{3,2,0,1:T(8,128)(2,1)} %select_bitcast_fusion.2), channel_id=1, source_target_pairs={{0,1},{1,0},{2,3},{3,2},{4,5},{5,4},{6,7},{7,6},{8,9},{9,8},{10,11... | collective-permute-start | bytes 2359304 | tf_op jit(solution)/shard_map/ppermute | solution.py:28
  470.6 9.1 %collective-permute-start.19 = (bf16[2,1,256,768]{3,2,0,1:T(8,128)(2,1)S(1)}, bf16[2,1,256,768]{3,2,0,1:T(8,128)(2,1)S(1)}, u32[]{:S(2)}, u32[]{:S(2)}) collective-permute-start(bf16[2,1,256,768]{3,2,0,1:T(8,128)(2,1)S(1)} %select_bitcast_fusion.3), channel_id=1, source_target_pairs={{0,1},{1,0},{2,3},{3,2},{4,5},{5,4},{6,7},{7,6},{8,9},{9,8},{10,11... | collective-permute-start | bytes 2359304 | tf_op jit(solution)/shard_map/ppermute | solution.py:28
  479.3 12.1 %collective-permute-start.22 = (bf16[1,256,768]{2,1,0:T(8,128)(2,1)S(1)}, bf16[1,256,768]{2,1,0:T(8,128)(2,1)S(1)}, u32[]{:S(2)}, u32[]{:S(2)}) collective-permute-start(bf16[1,256,768]{2,1,0:T(8,128)(2,1)S(1)} %fusion.180), channel_id=1, source_target_pairs={{0,2},{1,3},{2,0},{3,1},{4,6},{5,7},{6,4},{7,5},{8,10},{9,11},{10,... | collective-permute-start | bytes 1179656 | tf_op jit(solution)/shard_map/ppermute | solution.py:28
  479.9 19.3 %collective-permute-start.20 = (bf16[1,256,768]{2,1,0:T(8,128)(2,1)S(1)}, bf16[1,256,768]{2,1,0:T(8,128)(2,1)S(1)}, u32[]{:S(2)}, u32[]{:S(2)}) collective-permute-start(bf16[1,256,768]{2,1,0:T(8,128)(2,1)S(1)} %fusion.183), channel_id=1, source_target_pairs={{0,2},{1,3},{2,0},{3,1},{4,6},{5,7},{6,4},{7,5},{8,10},{9,11},{10,... | collective-permute-start | bytes 1179656 | tf_op jit(solution)/shard_map/ppermute | solution.py:28
  509.3 327.5 %reduce-scatter.7.cloned.1.call-start = ((), (), s32[]{:S(2)}) async-start(), calls=%async_computation.4 | async-start | bytes 14598144
  565.8 17.0 %collective-permute-start.23 = (f32[1,1024]{1,0:T(1,128)}, f32[1,1024]{1,0:T(1,128)}, u32[]{:S(2)}, u32[]{:S(2)}) collective-permute-start(f32[1,1024]{1,0:T(1,128)} %bitcast.158), channel_id=1, source_target_pairs={{0,1},{1,0},{2,3},{3,2},{4,5},{5,4},{6,7},{7,6},{8,9},{9,8},{10,11... | collective-permute-start | bytes 12296 | tf_op jit(solution)/shard_map/ppermute | solution.py:28
  583.5 18.4 %collective-permute-start.24 = (f32[1,1024]{1,0:T(1,128)S(1)}, f32[1,1024]{1,0:T(1,128)S(1)}, u32[]{:S(2)}, u32[]{:S(2)}) collective-permute-start(f32[1,1024]{1,0:T(1,128)S(1)} %add.433), channel_id=1, source_target_pairs={{0,2},{1,3},{2,0},{3,1},{4,6},{5,7},{6,4},{7,5},{8,10},{9,11},{10,... | collective-permute-start | bytes 12296 | tf_op jit(solution)/shard_map/ppermute | solution.py:28
  589.4 47.7 %collective-permute-start.27 = (bf16[2,1,256,768]{3,2,1,0:T(8,128)(2,1)}, bf16[2,1,256,768]{3,2,1,0:T(8,128)(2,1)}, u32[]{:S(2)}, u32[]{:S(2)}) collective-permute-start(bf16[2,1,256,768]{3,2,1,0:T(8,128)(2,1)} %select_bitcast_fusion), channel_id=1, source_target_pairs={{0,1},{1,0},{2,3},{3,2},{4,5},{5,4},{6,7},{7,6},{8,9},{9,8},{10,11... | collective-permute-start | bytes 2359304 | tf_op jit(solution)/shard_map/ppermute | solution.py:28
  630.2 10.1 %collective-permute-start.25 = (bf16[2,1,256,768]{3,2,0,1:T(8,128)(2,1)S(1)}, bf16[2,1,256,768]{3,2,0,1:T(8,128)(2,1)S(1)}, u32[]{:S(2)}, u32[]{:S(2)}) collective-permute-start(bf16[2,1,256,768]{3,2,0,1:T(8,128)(2,1)S(1)} %select_bitcast_fusion.1), channel_id=1, source_target_pairs={{0,1},{1,0},{2,3},{3,2},{4,5},{5,4},{6,7},{7,6},{8,9},{9,8},{10,11... | collective-permute-start | bytes 2359304 | tf_op jit(solution)/shard_map/ppermute | solution.py:28
  638.6 12.1 %collective-permute-start.28 = (bf16[1,256,768]{2,1,0:T(8,128)(2,1)S(1)}, bf16[1,256,768]{2,1,0:T(8,128)(2,1)S(1)}, u32[]{:S(2)}, u32[]{:S(2)}) collective-permute-start(bf16[1,256,768]{2,1,0:T(8,128)(2,1)S(1)} %select_bitcast_fusion.12), channel_id=1, source_target_pairs={{0,2},{1,3},{2,0},{3,1},{4,6},{5,7},{6,4},{7,5},{8,10},{9,11},{10,... | collective-permute-start | bytes 1179656 | tf_op jit(solution)/shard_map/ppermute | solution.py:28
  640.7 21.2 %collective-permute-start.26 = (bf16[1,256,768]{2,1,0:T(8,128)(2,1)S(1)}, bf16[1,256,768]{2,1,0:T(8,128)(2,1)S(1)}, u32[]{:S(2)}, u32[]{:S(2)}) collective-permute-start(bf16[1,256,768]{2,1,0:T(8,128)(2,1)S(1)} %fusion.170), channel_id=1, source_target_pairs={{0,2},{1,3},{2,0},{3,1},{4,6},{5,7},{6,4},{7,5},{8,10},{9,11},{10,... | collective-permute-start | bytes 1179656 | tf_op jit(solution)/shard_map/ppermute | solution.py:28
  685.8 4.2 collective-permute-start.30
  690.0 7.1 collective-permute-start.31
  697.1 4.2 collective-permute-start.32
  701.3 5.5 collective-permute-start.33
  (135 other events, 2297.1 us)
Sparse Core Ops, SparseCore 0:
  14.8 105.2 all-gather.2
  123.6 103.3 all-gather.4
  509.3 160.7 reduce-scatter.8
  676.0 160.7 reduce-scatter.6

commit v2 on v1

--- a/solution.py
+++ b/solution.py
@@ -1,6 +1,8 @@
 import jax
 import jax.numpy as jnp
 from jax import lax
+from jax.experimental import pallas as pl
+from jax.experimental.pallas import tpu as pltpu
 from jax.sharding import PartitionSpec as P
 
 HEADS = 12
@@ -52,32 +54,6 @@
     return blocks.transpose(order).reshape((-1,) + array.shape)
 
 
-def scatter_line(blocks, axis):
-    steps = len(bits_of(axis))
-    rest = blocks.shape[1:]
-    blocks = blocks.reshape((2,) * steps + rest)
-    for bit in bits_of(axis):
-        is_upper = upper(axis, bit)
-        low = lax.index_in_dim(blocks, 0, blocks.ndim - len(rest) - 1, False)
-        high = lax.index_in_dim(blocks, 1, blocks.ndim - len(rest) - 1, False)
-        keep = jnp.where(is_upper, high, low)
-        send = jnp.where(is_upper, low, high)
-        blocks = keep + flip(send, axis, bit)
-    return blocks
-
-
-def line_prefix(array, axis, reverse):
-    total = array
-    before = jnp.zeros_like(array)
-    for bit in bits_of(axis):
-        other = flip(total, axis, bit)
-        is_upper = upper(axis, bit)
-        take = jnp.logical_not(is_upper) if reverse else is_upper
-        before = before + jnp.where(take, other, 0.0)
-        total = total + other
-    return before, total
-
-
 def sum_all(array, axes):
     for axis in axes:
         for bit in bits_of(axis):
@@ -104,6 +80,358 @@
     rows, width = grad.shape
     split = grad.reshape(devices, parts, rows // (parts * devices), width)
     return split.transpose(1, 0, 2, 3).reshape(parts, rows // parts, width)
+
+
+def dims_of(scalars, rows, cols):
+    place = scalars[0]
+    length = scalars[1]
+    local = rows
+    count = cols // rows
+    row = place * local + lax.broadcasted_iota(jnp.int32, (rows, cols), 0)
+    within = lax.broadcasted_iota(jnp.int32, (1, local), 1)
+    col = jnp.concatenate([(place ^ b) * local + within for b in range(count)], axis=1)
+    return row, col, length
+
+
+def half(array, which):
+    lane = lax.broadcasted_iota(jnp.int32, array.shape, 1)
+    keep = lane < array.shape[1] // 2
+    if which:
+        keep = jnp.logical_not(keep)
+    return jnp.where(keep, array, jnp.zeros_like(array))
+
+
+def rowdot(left, right):
+    return lax.dot_general(
+        left, right, (((1,), (1,)), ((), ())), preferred_element_type=jnp.float32
+    )
+
+
+def coldot(left, right):
+    return lax.dot_general(
+        left, right, (((0,), (0,)), ((), ())), preferred_element_type=jnp.float32
+    )
+
+
+def plain(left, right):
+    return jnp.dot(left, right, preferred_element_type=jnp.float32)
+
+
+def triangle(rows, upper):
+    first = lax.broadcasted_iota(jnp.int32, (rows, rows), 0)
+    second = lax.broadcasted_iota(jnp.int32, (rows, rows), 1)
+    inside = (first < second) if upper else (first > second)
+    return jnp.where(inside, 1.0, 0.0).astype(jnp.bfloat16)
+
+
+def exact_sums(matrix, array):
+    high = array.astype(jnp.bfloat16)
+    rest = array - high.astype(jnp.float32)
+    mid = rest.astype(jnp.bfloat16)
+    low = (rest - mid.astype(jnp.float32)).astype(jnp.bfloat16)
+    return plain(matrix, high) + plain(matrix, mid) + plain(matrix, low)
+
+
+def pick_kernel(scalars, q_ref, *refs):
+    count = len(refs) - 2
+    keys = refs[:count]
+    carried_ref, column_ref = refs[count:]
+    rows = q_ref.shape[0]
+    cols = rows * count
+    row, col, length = dims_of(scalars, rows, cols)
+    query = half(q_ref[...], 0)
+    scores = jnp.concatenate([rowdot(query, key[...]) for key in keys], axis=1)
+    mask = (row > col) & (col >= 1) & (row < length) & (col < length)
+    select = jnp.where(mask, jnp.maximum(scores, 0.0), 0.0) * (0.125 * select_strength / cols)
+    carried_ref[...] = exact_sums(triangle(rows, False), select)
+    column_ref[...] = jnp.sum(select, axis=0, keepdims=True)
+
+
+def fill_bias(scalars, bias_ref, carried_ref, before_ref):
+    rows, cols = bias_ref.shape
+    row, col, length = dims_of(scalars, rows, cols)
+    carried = carried_ref[...] + before_ref[...]
+    bias_ref[...] = jnp.where((row >= col) & (col < length), -carried, masked_value)
+
+
+CHUNK = 32
+
+
+def mix_kernel(scalars, q_ref, carried_ref, before_ref, *refs):
+    count = (len(refs) - 5) // 2
+    keys = refs[:count]
+    values = refs[count : 2 * count]
+    mixed_ref, total_ref, bias_ref, score_ref, prob_ref = refs[2 * count :]
+    rows = q_ref.shape[0]
+
+    @pl.when(pl.program_id(0) == 0)
+    def _():
+        fill_bias(scalars, bias_ref, carried_ref, before_ref)
+
+    outs = []
+    for which in range(2):
+        query = half(q_ref[...], which) * jnp.asarray(0.125, jnp.bfloat16)
+        for b in range(count):
+            score_ref[which, :, b * rows : (b + 1) * rows] = rowdot(query, keys[b][...])
+    for which in range(2):
+        for chunk in range(rows // CHUNK):
+            at = slice(chunk * CHUNK, (chunk + 1) * CHUNK)
+            logits = score_ref[which, at, :] + bias_ref[at, :]
+            peak = jnp.max(logits, axis=1, keepdims=True)
+            expo = jnp.exp(logits - peak)
+            denominator = jnp.sum(expo, axis=1, keepdims=True)
+            prob_ref[which, at, :] = (expo * (1.0 / denominator)).astype(jnp.bfloat16)
+            total = peak + jnp.log(denominator)
+            width = total_ref.shape[1] // 2
+            total_ref[at, which * width : (which + 1) * width] = jnp.broadcast_to(
+                total, (CHUNK, width)
+            )
+        acc = plain(prob_ref[which, :, 0:rows], values[0][...])
+        for b in range(1, count):
+            acc = acc + plain(prob_ref[which, :, b * rows : (b + 1) * rows], values[b][...])
+        outs.append(acc)
+    mixed_ref[...] = (half(outs[0], 0) + half(outs[1], 1)).astype(jnp.bfloat16)
+
+
+def back_kernel(scalars, q_ref, dm_ref, total_ref, carried_ref, before_ref, *refs):
+    count = (len(refs) - 11) // 2
+    keys = refs[:count]
+    values = refs[count : 2 * count]
+    (
+        dq_ref,
+        dk_ref,
+        dv_ref,
+        sum_ref,
+        first_ref,
+        column_ref,
+        bias_ref,
+        score_ref,
+        dprob_ref,
+        prob_ref,
+        ds_ref,
+    ) = refs[2 * count :]
+    rows = q_ref.shape[0]
+    step = pl.program_id(0)
+
+    @pl.when(step == 0)
+    def _():
+        fill_bias(scalars, bias_ref, carried_ref, before_ref)
+        sum_ref[...] = jnp.zeros_like(sum_ref)
+
+    eighth = jnp.asarray(0.125, jnp.bfloat16)
+    queries = [half(q_ref[...], which) * eighth for which in range(2)]
+    grads = [half(dm_ref[...], which) for which in range(2)]
+    for which in range(2):
+        for b in range(count):
+            at = slice(b * rows, (b + 1) * rows)
+            score_ref[which, :, at] = rowdot(queries[which], keys[b][...])
+            dprob_ref[which, :, at] = rowdot(grads[which], values[b][...])
+    for which in range(2):
+        width = total_ref.shape[1] // 2
+        for chunk in range(rows // CHUNK):
+            at = slice(chunk * CHUNK, (chunk + 1) * CHUNK)
+            total = total_ref[at, which * width : which * width + 1]
+            probs = jnp.exp(score_ref[which, at, :] + bias_ref[at, :] - total)
+            dprob = dprob_ref[which, at, :]
+            delta = jnp.sum(probs * dprob, axis=1, keepdims=True)
+            dlogits = probs * (dprob - delta)
+            prob_ref[which, at, :] = probs.astype(jnp.bfloat16)
+            sum_ref[at, :] = sum_ref[at, :] + dlogits
+            ds_ref[which, at, :] = dlogits.astype(jnp.bfloat16)
+            if which == 0:
+
+                @pl.when(step == 0)
+                def _():
+                    first_ref[at, :] = dlogits
+
+    @pl.when(step == 0)
+    def _():
+        ds_ref[0] = jnp.zeros_like(ds_ref[0])
+
+    dq = []
+    for which in range(2):
+        acc = plain(ds_ref[which, :, 0:rows], keys[0][...])
+        for b in range(1, count):
+            acc = acc + plain(ds_ref[which, :, b * rows : (b + 1) * rows], keys[b][...])
+        dq.append(acc)
+    dq_ref[...] = ((half(dq[0], 0) + half(dq[1], 1)) * 0.125).astype(jnp.bfloat16)
+    for b in range(count):
+        at = slice(b * rows, (b + 1) * rows)
+        dk = coldot(ds_ref[0, :, at], queries[0]) + coldot(ds_ref[1, :, at], queries[1])
+        dv = coldot(prob_ref[0, :, at], grads[0]) + coldot(prob_ref[1, :, at], grads[1])
+        dk_ref[b] = dk.astype(jnp.bfloat16)
+        dv_ref[b] = dv.astype(jnp.bfloat16)
+
+    @pl.when(step == pl.num_programs(0) - 1)
+    def _():
+        column_ref[...] = jnp.sum(sum_ref[...], axis=0, keepdims=True)
+
+
+def first_kernel(scalars, q_ref, sum_ref, first_ref, later_ref, dq_in, dk_in, *refs):
+    count = len(refs) - 2
+    keys = refs[:count]
+    dq_ref, dk_ref = refs[count:]
+    rows = q_ref.shape[0]
+    cols = rows * count
+    row, col, length = dims_of(scalars, rows, cols)
+    query = half(q_ref[...], 0)
+    scores = jnp.concatenate([rowdot(query, key[...]) for key in keys], axis=1)
+    mask = (row > col) & (col >= 1) & (row < length) & (col < length) & (scores > 0.0)
+    later = exact_sums(triangle(rows, True), sum_ref[...]) + later_ref[...]
+    extra = jnp.where(mask, later, 0.0) * (-select_strength / cols)
+    dscores = (first_ref[...] + extra).astype(jnp.bfloat16)
+    acc = plain(dscores[:, 0:rows], keys[0][...])
+    for b in range(1, count):
+        acc = acc + plain(dscores[:, b * rows : (b + 1) * rows], keys[b][...])
+    dq_ref[...] = dq_in[...] + half(acc * 0.125, 0).astype(jnp.bfloat16)
+    scaled = query * jnp.asarray(0.125, jnp.bfloat16)
+    for b in range(count):
+        dk = coldot(dscores[:, b * rows : (b + 1) * rows], scaled)
+        dk_ref[b] = dk_in[b] + dk.astype(jnp.bfloat16)
+
+
+PAIR = 128
+
+
+def pick(scalars, query, keys):
+    rows, width = query.shape
+    cols = rows * len(keys)
+    one = pl.BlockSpec((rows, PAIR), lambda h, s: (0, 0))
+    return pl.pallas_call(
+        pick_kernel,
+        name="pick",
+        out_shape=(
+            jax.ShapeDtypeStruct((rows, cols), jnp.float32),
+            jax.ShapeDtypeStruct((1, cols), jnp.float32),
+        ),
+        grid_spec=pltpu.PrefetchScalarGridSpec(
+            num_scalar_prefetch=1,
+            grid=(1,),
+            in_specs=[one] * (1 + len(keys)),
+            out_specs=(
+                pl.BlockSpec((rows, cols), lambda h, s: (0, 0)),
+                pl.BlockSpec((1, cols), lambda h, s: (0, 0)),
+            ),
+        ),
+    )(scalars, query, *keys)
+
+
+def mix(scalars, query, carried, before, keys, values):
+    rows, width = query.shape
+    cols = rows * len(keys)
+    pair = pl.BlockSpec((rows, PAIR), lambda h, s: (0, h))
+    full = pl.BlockSpec((rows, cols), lambda h, s: (0, 0))
+    line = pl.BlockSpec((1, cols), lambda h, s: (0, 0))
+    return pl.pallas_call(
+        mix_kernel,
+        name="mix",
+        out_shape=(
+            jax.ShapeDtypeStruct((rows, width), jnp.bfloat16),
+            jax.ShapeDtypeStruct((rows, width), jnp.float32),
+        ),
+        grid_spec=pltpu.PrefetchScalarGridSpec(
+            num_scalar_prefetch=1,
+            grid=(width // PAIR,),
+            in_specs=[pair, full, line] + [pair] * (2 * len(keys)),
+            out_specs=(pair, pair),
+            scratch_shapes=[
+                pltpu.VMEM((rows, cols), jnp.float32),
+                pltpu.VMEM((2, rows, cols), jnp.float32),
+                pltpu.VMEM((2, rows, cols), jnp.bfloat16),
+            ],
+        ),
+    )(scalars, query, carried, before, *keys, *values)
+
+
+def back(scalars, query, grad_mixed, total, carried, before, keys, values):
+    rows, width = query.shape
+    count = len(keys)
+    cols = rows * count
+    pair = pl.BlockSpec((rows, PAIR), lambda h, s: (0, h))
+    full = pl.BlockSpec((rows, cols), lambda h, s: (0, 0))
+    line = pl.BlockSpec((1, cols), lambda h, s: (0, 0))
+    blocks = pl.BlockSpec((count, rows, PAIR), lambda h, s: (0, 0, h))
+    return pl.pallas_call(
+        back_kernel,
+        name="back",
+        out_shape=(
+            jax.ShapeDtypeStruct((rows, width), jnp.bfloat16),
+            jax.ShapeDtypeStruct((count, rows, width), jnp.bfloat16),
+            jax.ShapeDtypeStruct((count, rows, width), jnp.bfloat16),
+            jax.ShapeDtypeStruct((rows, cols), jnp.float32),
+            jax.ShapeDtypeStruct((rows, cols), jnp.float32),
+            jax.ShapeDtypeStruct((1, cols), jnp.float32),
+        ),
+        grid_spec=pltpu.PrefetchScalarGridSpec(
+            num_scalar_prefetch=1,
+            grid=(width // PAIR,),
+            in_specs=[pair, pair, pair, full, line] + [pair] * (2 * count),
+            out_specs=(pair, blocks, blocks, full, full, line),
+            scratch_shapes=[
+                pltpu.VMEM((rows, cols), jnp.float32),
+                pltpu.VMEM((2, rows, cols), jnp.float32),
+                pltpu.VMEM((2, rows, cols), jnp.float32),
+                pltpu.VMEM((2, rows, cols), jnp.bfloat16),
+                pltpu.VMEM((2, rows, cols), jnp.bfloat16),
+            ],
+        ),
+    )(scalars, query, grad_mixed, total, carried, before, *keys, *values)
+
+
+def first(scalars, query, sums, first_logits, later, dq, dk, keys):
+    rows, width = query.shape
+    count = len(keys)
+    cols = rows * count
+    one = pl.BlockSpec((rows, PAIR), lambda h, s: (0, 0))
+    full = pl.BlockSpec((rows, cols), lambda h, s: (0, 0))
+    line = pl.BlockSpec((1, cols), lambda h, s: (0, 0))
+    blocks = pl.BlockSpec((count, rows, PAIR), lambda h, s: (0, 0, 0))
+    return pl.pallas_call(
+        first_kernel,
+        name="first",
+        out_shape=(
+            jax.ShapeDtypeStruct((rows, width), jnp.bfloat16),
+            jax.ShapeDtypeStruct((count, rows, width), jnp.bfloat16),
+        ),
+        grid_spec=pltpu.PrefetchScalarGridSpec(
+            num_scalar_prefetch=1,
+            grid=(1,),
+            in_specs=[one, full, full, line, one, blocks] + [one] * count,
+            out_specs=(one, blocks),
+        ),
+        input_output_aliases={5: 0, 6: 1},
+    )(scalars, query, sums, first_logits, later, dq, dk, *keys)
+
+
+def spread(array, axis):
+    size = lax.axis_size(axis)
+    got = {0: array}
+    for bit in reversed(bits_of(axis)):
+        for b in list(got):
+            got[b ^ bit] = flip(got[b], axis, bit)
+    return [got[b] for b in range(size)]
+
+
+def collect(blocks, axis):
+    for bit in bits_of(axis):
+        size = blocks.shape[0] // 2
+        pairs = blocks.reshape((size, 2) + blocks.shape[1:])
+        blocks = pairs[:, 0] + flip(pairs[:, 1], axis, bit)
+    return blocks[0]
+
+
+def line_prefix(array, axis, reverse):
+    size = array.shape[0]
+    total = array
+    before = jnp.zeros_like(array)
+    for bit in bits_of(axis):
+        other = flip(total, axis, bit)
+        other = jnp.stack([other[b ^ bit] for b in range(size)])
+        is_upper = upper(axis, bit)
+        take = jnp.logical_not(is_upper) if reverse else is_upper
+        before = before + jnp.where(take, other, 0.0)
+        total = total + other
+    return before, total
 
 
 def local(
@@ -125,30 +453,15 @@
 ):
     layers = gain_attend.shape[0]
     seq_dev, local_len, width = inputs.shape
-    heads = HEADS
-    head = width // heads
     seq_count = lax.axis_size("seq")
     devices = lax.axis_size(("dp", "seq"))
-    full_len = local_len * seq_count
-    highest = lax.Precision.HIGHEST
     is_last = lax.axis_index("seq") == seq_count - 1
-    position = lax.axis_index("seq") * local_len + jnp.arange(local_len, dtype=jnp.int32)
-    key_place = jnp.arange(full_len, dtype=jnp.int32)
-    valid_keys = key_place[None, :] < lengths[:, None]
-    valid_query = position[None, :] < lengths[:, None]
-    select_mask = (
-        (position[None, :, None] > key_place[None, None, :])
-        & (key_place[None, None, :] >= 1)
-        & valid_query[:, :, None]
-        & valid_keys[:, None, :]
-    )
-    allowed = ((position[None, :, None] >= key_place[None, None, :]) & valid_keys[:, None, :])[
-        :, None
-    ]
-    row_index = jnp.arange(local_len, dtype=jnp.int32)
-    strict_lower = (row_index[:, None] > row_index[None, :]).astype(jnp.float32)
-    select_scale = select_strength / full_len
-
+    place = lax.axis_index("seq")
+    key_place = (place ^ jnp.arange(seq_count, dtype=jnp.int32))[:, None] * local_len + jnp.arange(
+        local_len, dtype=jnp.int32
+    )
+    valid_keys = key_place < lengths[0]
+    scalars = jnp.stack([place, lengths[0]]).astype(jnp.int32)
     both = ("dp", "seq")
     parts = weight_inner.shape[2] // width
     vectors = jnp.concatenate(
@@ -182,20 +495,6 @@
     ]
     w_outers = [unpack_outer(planes[4 + parts :], devices) for planes in whole]
 
-    def score_block(query, keys_whole):
-        scores = (
-            product(query, keys_whole.reshape(seq_dev, full_len, heads, head), "sqhe,skhe->shqk")
-            * 0.125
-        )
-        select = jnp.where(select_mask, jax.nn.relu(scores[:, 0]), 0.0) * select_scale
-        return (scores, select)
-
-    def logits_from(scores, select, before):
-        carried = before[:, None, :] + jnp.einsum(
-            "qr,srk->sqk", strict_lower, select, precision=highest
-        )
-        return jnp.where(allowed, scores - carried[:, None], masked_value)
-
     hidden = inputs.astype(jnp.float32)
     share_sum = jnp.zeros((), jnp.float32)
     saved = []
@@ -217,46 +516,22 @@
             .astype(jnp.bfloat16)
             .reshape(-1, width)
         )
-        forward_query = (
-            jnp.dot(forward_normed, forward_w_query, preferred_element_type=jnp.float32)
-            .astype(jnp.bfloat16)
-            .reshape(seq_dev, local_len, heads, head)
-        )
-        forward_keys = (
-            jnp.dot(forward_normed, forward_w_key, preferred_element_type=jnp.float32)
-            .astype(jnp.bfloat16)
-            .reshape(seq_dev, local_len, width)
-        )
-        forward_values = (
-            jnp.dot(forward_normed, forward_w_value, preferred_element_type=jnp.float32)
-            .astype(jnp.bfloat16)
-            .reshape(seq_dev, local_len, width)
-        )
-        forward_keys_whole = (
-            gather_line(forward_keys, "seq").transpose(1, 0, 2, 3).reshape(seq_dev, full_len, width)
-        )
-        forward_values_whole = (
-            gather_line(forward_values, "seq")
-            .transpose(1, 0, 2, 3)
-            .reshape(seq_dev, full_len, width)
-        )
-        forward_scores, forward_select = score_block(forward_query, forward_keys_whole)
-        column = jnp.sum(forward_select, axis=1)
-        forward_before, totals = line_prefix(column, "seq", False)
-        logits = logits_from(forward_scores, forward_select, forward_before)
-        peak = jnp.max(logits, axis=-1, keepdims=True)
-        expo = jnp.exp(logits - peak)
-        denominator = jnp.sum(expo, axis=-1, keepdims=True)
-        forward_probs = expo / denominator
-        forward_log_total = peak + jnp.log(denominator)
-        forward_mixed = (
-            product(
-                forward_probs.astype(jnp.bfloat16),
-                forward_values_whole.reshape(seq_dev, full_len, heads, head),
-                "shqk,skhe->sqhe",
-            )
-            .astype(jnp.bfloat16)
-            .reshape(-1, width)
+        forward_keys = jnp.dot(
+            forward_normed, forward_w_key, preferred_element_type=jnp.float32
+        ).astype(jnp.bfloat16)
+        forward_query = jnp.dot(
+            forward_normed, forward_w_query, preferred_element_type=jnp.float32
+        ).astype(jnp.bfloat16)
+        forward_values = jnp.dot(
+            forward_normed, forward_w_value, preferred_element_type=jnp.float32
+        ).astype(jnp.bfloat16)
+        all_keys = spread(forward_keys, "seq")
+        all_values = spread(forward_values, "seq")
+        carried, column = pick(scalars, forward_query, all_keys)
+        before, totals = line_prefix(column.reshape(seq_count, local_len), "seq", False)
+        before = before.reshape(1, -1)
+        forward_mixed, log_total = mix(
+            scalars, forward_query, carried, before, all_keys, all_values
         )
         forward_after = hidden + jnp.dot(
             forward_mixed, forward_w_output, preferred_element_type=jnp.float32
@@ -287,12 +562,11 @@
             hidden,
             forward_normed,
             forward_query,
-            forward_keys,
-            forward_values,
-            forward_keys_whole,
-            forward_values_whole,
-            forward_before,
-            forward_log_total,
+            all_keys,
+            all_values,
+            carried,
+            before,
+            log_total,
             forward_mixed,
             forward_after,
             forward_normed_two,
@@ -315,11 +589,10 @@
             backward_hidden,
             normed,
             backward_query,
-            keys,
-            values,
-            backward_keys_whole,
-            values_whole,
-            backward_before,
+            all_keys,
+            all_values,
+            carried,
+            before,
             log_total,
             mixed,
             after,
@@ -343,57 +616,23 @@
         grad_after = grad_hidden + after_part
         grad_attn = grad_after.astype(jnp.bfloat16).reshape(-1, width)
         grad_w_output = product(mixed, grad_attn, "tc,td->cd")
-        grad_mixed = (
-            product(grad_attn, w_output, "td,cd->tc")
-            .astype(jnp.bfloat16)
-            .reshape(seq_dev, local_len, heads, head)
-        )
-        backward_scores, backward_select = score_block(backward_query, backward_keys_whole)
-        probs = jnp.exp(logits_from(backward_scores, backward_select, backward_before) - log_total)
-        values_heads = values_whole.reshape(seq_dev, full_len, heads, head)
-        grad_probs = product(grad_mixed, values_heads, "sqhe,skhe->shqk")
-        delta = jnp.sum(probs * grad_probs, axis=-1, keepdims=True)
-        grad_logits = probs * (grad_probs - delta)
-        grad_carried = -jnp.sum(grad_logits, axis=1)
-        column_back = jnp.sum(grad_carried, axis=1)
-        later_rows, _ = line_prefix(column_back, "seq", True)
-        grad_select = later_rows[:, None, :] + jnp.einsum(
-            "qr,sqk->srk", strict_lower, grad_carried, precision=highest
-        )
-        grad_first = jnp.where(
-            select_mask & (backward_scores[:, 0] > 0.0), grad_select * select_scale, 0.0
-        )
-        grad_scores = grad_logits.at[:, 0].add(grad_first).astype(jnp.bfloat16)
-        grad_query = (
-            (
-                product(
-                    grad_scores,
-                    backward_keys_whole.reshape(seq_dev, full_len, heads, head),
-                    "shqk,skhe->sqhe",
-                )
-                * 0.125
-            )
-            .astype(jnp.bfloat16)
-            .reshape(-1, width)
-        )
-        grad_values = product(probs.astype(jnp.bfloat16), grad_mixed, "shqk,sqhe->skhe")
-        key_part = (product(grad_scores, backward_query, "shqk,sqhe->skhe") * 0.125).reshape(
-            seq_dev, full_len, width
-        )
-        grad_keys = scatter_line(
-            key_part.astype(jnp.bfloat16)
-            .reshape(seq_dev, seq_count, local_len, width)
-            .transpose(1, 0, 2, 3),
-            "seq",
-        )
-        grad_vals = scatter_line(
-            grad_values.astype(jnp.bfloat16)
-            .reshape(seq_dev, seq_count, local_len, width)
-            .transpose(1, 0, 2, 3),
-            "seq",
-        )
-        grad_keys = grad_keys.reshape(-1, width)
-        grad_vals = grad_vals.reshape(-1, width)
+        grad_mixed = product(grad_attn, w_output, "td,cd->tc").astype(jnp.bfloat16)
+        grad_query, key_part, value_part, sums, first_logits, column_back = back(
+            scalars, backward_query, grad_mixed, log_total, carried, before, all_keys, all_values
+        )
+        grad_vals = collect(value_part, "seq")
+        later, _ = line_prefix(column_back.reshape(seq_count, local_len), "seq", True)
+        grad_query, key_part = first(
+            scalars,
+            backward_query,
+            sums,
+            first_logits,
+            later.reshape(1, -1),
+            grad_query,
+            key_part,
+            all_keys,
+        )
+        grad_keys = collect(key_part, "seq")
         grad_w_query = product(normed, grad_query, "tc,td->cd")
         grad_w_key = product(normed, grad_keys, "tc,td->cd")
         grad_w_value = product(normed, grad_vals, "tc,td->cd")
@@ -436,12 +675,12 @@
     flat = sum_all(flat.reshape(-1, 128), ("seq", "dp")).reshape(-1)
     size = (5 + parts) * width
     selected = flat[layers * size] / (layers * flat[layers * size + 128])
-    place = lax.axis_index("dp") * seq_count + lax.axis_index("seq")
+    place_of = lax.axis_index("dp") * seq_count + place
     vec = flat[: layers * size].reshape(layers, size)
 
     def mine(first, length):
         return lax.dynamic_slice_in_dim(
-            vec[:, first * width : first * width + length], place * (length // devices),
+            vec[:, first * width : first * width + length], place_of * (length // devices),
             length // devices, axis=1,
         )
 

time: 858 us -> 744 us (0.87)
  local copies, waits for them, and re-layouts: 213 us -> 91.5 us
  waiting for transfers between devices: 274 us -> 389 us
  matrix products: 184 us -> 80 us
  other arithmetic: 128 us -> 27.1 us
  Pallas kernels: 0 us -> 93.1 us
    dot_general x36 -> x24, matrix products: 142 us -> 46.6 us  [product(): return jnp.einsum(form, left, right, preferred_element_type=jnp.float32)]
    pallas_call x0 -> x8, Pallas kernels: none -> 93.1 us  [the longest x2 55.3 us: back(): pl.pallas_call(back_kernel, name='back', out_shape=(jax.ShapeDtypeStruct(...]
    unnamed x6, waiting for transfers between devices: 123 us -> 185 us
    reduce_sum x6 -> x0, other arithmetic: 51.5 us -> none  [the longest x2 31.1 us: local(): grad_carried = -jnp.sum(grad_logits, axis=1)]
    unnamed x299 -> x260, local copies, waits for them, and re-layouts: 93.4 us -> 44.3 us
    all_gather x2, waiting for transfers between devices: 82.2 us -> 123 us  [local(): lax.all_gather(pack_weights(weight_query[k], weight_key[k], weight_value[...]
    mul x2 -> x1, other arithmetic: 25.8 us -> 0.01 us  [local(): (place ^ jnp.arange(seq_count, dtype=jnp.int32))[:, None] * local_len]
    another operation x6 -> x0, local copies, waits for them, and re-layouts: 20.4 us -> none
  transfers between devices with their start and end apart: 38 -> 42, of which waited for: 17 -> 26; matrix products, arithmetic and copies ran while one was open for 48% -> 20% of each run, Pallas kernels for 0% -> 7%
where the time goes in v2:
time: 744 us; the launch traced here: 736 us
  waiting for transfers between devices  389 us (52%)
  Pallas kernels  93.1 us (13%)
  local copies, waits for them, and re-layouts  91.5 us (12%)
  matrix products  80 us (11%)
  starting transfers between devices  34 us (5%)
  other arithmetic  27.1 us (4%)
  between operations  20.8 us (3%)
    unnamed x6, waiting for transfers between devices  185 us
    all_gather x2, waiting for transfers between devices, local(): lax.all_gather(pack_weights(weight_query[k], weight_key[k], weight_value[...  123 us
    ppermute x38, waiting for transfers between devices, flip(): return lax.ppermute(array, axis, [(i, i ^ bit) for i in range(size)])  81.6 us
    pallas_call x2, Pallas kernels, back(): pl.pallas_call(back_kernel, name='back', out_shape=(jax.ShapeDtypeStruct(...  55.3 us
    dot_general x24, matrix products, product(): return jnp.einsum(form, left, right, preferred_element_type=jnp.float32)  46.6 us
    unnamed x260, local copies, waits for them, and re-layouts  44.3 us
    ppermute x38, starting transfers between devices, flip(): return lax.ppermute(array, axis, [(i, i ^ bit) for i in range(size)])  33.8 us
    pallas_call x2, Pallas kernels, mix(): pl.pallas_call(mix_kernel, name='mix', out_shape=(jax.ShapeDtypeStruct((r...  21.4 us
  transfers between devices with their start and end apart: 42, of which 26 were waited for; matrix products, arithmetic and copies ran while one was open for 20% of the time, Pallas kernels for 7%

profile of v2, /device:TPU:0, one launch (start us, length us, event | category | flops | bytes accessed | tf_op | source)
XLA Modules:
  0.0 735.5 jit_solution(16933429068736410182)
XLA Ops:
  36.9 83.1 %all-gather.3.cloned.1.call-done = bf16[12,768,768]{2,1,0:T(8,128)(2,1)} async-done(((bf16[12,24,768]{2,1,0:T(8,128)(2,1)}), bf16[12,768,768]{2,1,0:T(8,128)(2,1)}) %all-gather.3.cloned.1.call-update) | async-done | bytes 14155792 | tf_op jit(solution)/shard_map/all_gather | solution.py:481
  124.8 9.1 %collective-permute-done.6.refs_2_ = bf16[256,768]{1,0:T(8,128)(2,1)S(1)} collective-permute-done((bf16[256,768]{1,0:T(8,128)(2,1)S(1)}, bf16[256,768]{1,0:T(8,128)(2,1)S(1)}, u32[]{:S(2)}, u32[]{:S(2)}) %collective-permute-start.6) | collective-permute-done | bytes 393248 | tf_op jit(solution)/shard_map/ppermute | solution.py:30
  140.0 3.7 pick.2
  150.8 6.5 fusion.161
  160.0 6.9 copy.203
  171.0 10.5 %mix.2 = (bf16[256,768]{1,0:T(8,128)(2,1)}, f32[256,768]{1,0:T(8,128)}) custom-call(s32[2]{0:T(128)} %pad_add_fusion.scalars, bf16[256,768]{1,0:T(8,128)(2,1)} %convolution_convert_fusion.19.q_ref, f32[256,1024]{1,0:T(8,128)} %get-tuple-element.39.carried_ref, f32[1,1024]{1,0:T(1,128)} %fusion.122.before_ref, bf16[256,768]{1,0:T(8,128)(2,1)} %copy-done.5, ...), custom_call_target="tpu_custom_call" | custom-call | tf_op jit(solution)/shard_map/mix/pallas_call | solution.py:325
  183.8 4.9 convolution_add_fusion.1
  191.8 39.4 %all-gather.5.cloned.1.call-done = bf16[12,768,768]{2,1,0:T(8,128)(2,1)} async-done(((bf16[12,24,768]{2,1,0:T(8,128)(2,1)}), bf16[12,768,768]{2,1,0:T(8,128)(2,1)}) %all-gather.5.cloned.1.call-update) | async-done | bytes 14155792 | tf_op jit(solution)/shard_map/all_gather | solution.py:481
  234.2 10.1 %collective-permute-done.14.refs_2_ = bf16[256,768]{1,0:T(8,128)(2,1)S(1)} collective-permute-done((bf16[256,768]{1,0:T(8,128)(2,1)S(1)}, bf16[256,768]{1,0:T(8,128)(2,1)S(1)}, u32[]{:S(2)}, u32[]{:S(2)}) %collective-permute-start.14) | collective-permute-done | bytes 393248 | tf_op jit(solution)/shard_map/ppermute | solution.py:30
  252.2 3.7 pick.3
  262.4 6.6 fusion.160
  271.9 6.6 copy.208
  283.3 10.9 %mix.3 = (bf16[256,768]{1,0:T(8,128)(2,1)}, f32[256,768]{1,0:T(8,128)}) custom-call(s32[2]{0:T(128)} %pad_add_fusion.scalars, bf16[256,768]{1,0:T(8,128)(2,1)} %convolution_convert_fusion.16.q_ref, f32[256,1024]{1,0:T(8,128)} %get-tuple-element.42.carried_ref, f32[1,1024]{1,0:T(1,128)} %get-tuple-element.131.before_ref, bf16[256,768]{1,0:T(8,128)(2,1)} %copy-done.9, ...), custom_call_target="tpu_custom_call" | custom-call | tf_op jit(solution)/shard_map/mix/pallas_call | solution.py:325
  296.5 3.9 convolution_add_fusion
  300.6 3.7 convert_reduce_fusion
  310.1 27.5 %back.2 = (bf16[256,768]{1,0:T(8,128)(2,1)}, bf16[4,256,768]{2,1,0:T(8,128)(2,1)}, bf16[4,256,768]{2,1,0:T(8,128)(2,1)}, f32[256,1024]{1,0:T(8,128)}, f32[256,1024]{1,0:T(8,128)}, /*index=5*/f32[1,1024]{1,0:T(1,128)}) custom-call(s32[2]{0:T(128)} %pad_add_fusion.scalars, bf16[256,768]{1,0:T(8,128)(2,1)} %convolution_convert_fusion.16.q_ref, ...), custom_call_target="tpu_custom_call" | custom-call | tf_op jit(solution)/shard_map/back/pallas_call | solution.py:354
  348.1 4.4 first.2
  353.8 4.3 convolution_convert_fusion
  365.4 9.3 %collective-permute-done.24 = bf16[1,256,768]{2,1,0:T(8,128)(2,1)S(1)} collective-permute-done((bf16[1,256,768]{2,1,0:T(8,128)(2,1)S(1)}, bf16[1,256,768]{2,1,0:T(8,128)(2,1)S(1)}, u32[]{:S(2)}, u32[]{:S(2)}) %collective-permute-start.24) | collective-permute-done | bytes 393248 | tf_op jit(solution)/shard_map/ppermute | solution.py:30
  375.3 7.3 collective-permute-done.26
  384.4 6.0 copy.224
  400.3 3.9 convert_reduce_fusion.1
  410.2 27.8 %back.3 = (bf16[256,768]{1,0:T(8,128)(2,1)}, bf16[4,256,768]{2,1,0:T(8,128)(2,1)}, bf16[4,256,768]{2,1,0:T(8,128)(2,1)}, f32[256,1024]{1,0:T(8,128)}, f32[256,1024]{1,0:T(8,128)}, /*index=5*/f32[1,1024]{1,0:T(1,128)}) custom-call(s32[2]{0:T(128)} %pad_add_fusion.scalars, bf16[256,768]{1,0:T(8,128)(2,1)} %convolution_convert_fusion.19.q_ref, ...), custom_call_target="tpu_custom_call" | custom-call | tf_op jit(solution)/shard_map/back/pallas_call | solution.py:354
  444.8 4.5 first.3
  450.6 4.2 convolution_convert_fusion.2
  462.3 9.1 %collective-permute-done.30 = bf16[1,256,768]{2,1,0:T(8,128)(2,1)S(1)} collective-permute-done((bf16[1,256,768]{2,1,0:T(8,128)(2,1)S(1)}, bf16[1,256,768]{2,1,0:T(8,128)(2,1)S(1)}, u32[]{:S(2)}, u32[]{:S(2)}) %collective-permute-start.30) | collective-permute-done | bytes 393248 | tf_op jit(solution)/shard_map/ppermute | solution.py:30
  472.1 7.4 %collective-permute-done.32 = bf16[1,256,768]{2,1,0:T(8,128)(2,1)S(1)} collective-permute-done((bf16[1,256,768]{2,1,0:T(8,128)(2,1)S(1)}, bf16[1,256,768]{2,1,0:T(8,128)(2,1)S(1)}, u32[]{:S(2)}, u32[]{:S(2)}) %collective-permute-start.32) | collective-permute-done | bytes 393248 | tf_op jit(solution)/shard_map/ppermute | solution.py:30
  481.3 6.4 copy.223
  510.4 6.1 fusion.37
  524.7 6.5 collective-permute-done.37
  536.9 18.6 %reduce-scatter.9.cloned.1.call-done = bf16[24,9216]{1,0:T(8,128)(2,1)} async-done(((bf16[768,9216]{1,0:T(8,128)(2,1)}), bf16[24,9216]{1,0:T(8,128)(2,1)}) %reduce-scatter.9.cloned.1.call-update) | async-done | bytes 442384
  557.0 166.3 %reduce-scatter.7.cloned.1.call-done = bf16[24,9216]{1,0:T(8,128)(2,1)} async-done(((bf16[768,9216]{1,0:T(8,128)(2,1)}), bf16[24,9216]{1,0:T(8,128)(2,1)}) %reduce-scatter.7.cloned.1.call-update) | async-done | bytes 442384
  (515 shorter events, 185.2 us)
Async XLA Ops:
  7.2 112.8 %all-gather.3.cloned.1.call-start = ((), (), s32[]{:S(2)}) async-start(), calls=%async_computation.2 | async-start | bytes 14598144 | tf_op jit(solution)/shard_map/all_gather | solution.py:481
  14.6 216.6 %all-gather.5.cloned.1.call-start = ((), (), s32[]{:S(2)}) async-start(), calls=%async_computation.3 | async-start | bytes 14598144 | tf_op jit(solution)/shard_map/all_gather | solution.py:481
  16.7 538.8 %reduce-scatter.9.cloned.1.call-start = ((), (), s32[]{:S(2)}) async-start(), calls=%async_computation.5 | async-start | bytes 14598144
  16.9 4.5 collective-permute-start
  22.8 4.8 collective-permute-start.2
  27.6 4.0 collective-permute-start.3
  31.7 3.9 collective-permute-start.4
  121.9 12.0 %collective-permute-start.6 = (bf16[256,768]{1,0:T(8,128)(2,1)S(1)}, bf16[256,768]{1,0:T(8,128)(2,1)S(1)}, u32[]{:S(2)}, u32[]{:S(2)}) collective-permute-start(bf16[256,768]{1,0:T(8,128)(2,1)S(1)} %convolution_convert_fusion.18.refs_0_), channel_id=1, source_target_pairs={{0,2},{1,3},{2,0},{3,1},{4,6},{5,7},{6,4},{7,5},{8,10},{9,11},{10,... | collective-permute-start | bytes 1179656 | tf_op jit(solution)/shard_map/ppermute | solution.py:30
  124.7 13.7 %collective-permute-start.5 = (bf16[256,768]{1,0:T(8,128)(2,1)S(1)}, bf16[256,768]{1,0:T(8,128)(2,1)S(1)}, u32[]{:S(2)}, u32[]{:S(2)}) collective-permute-start(bf16[256,768]{1,0:T(8,128)(2,1)S(1)} %convolution_convert_fusion.18.refs_0_), channel_id=1, source_target_pairs={{0,1},{1,0},{2,3},{3,2},{4,5},{5,4},{6,7},{7,6},{8,9},{9,8},{10,11... | collective-permute-start | bytes 1179656 | tf_op jit(solution)/shard_map/ppermute | solution.py:30
  133.9 4.6 collective-permute-start.7
  145.6 5.0 collective-permute-start.8
  148.0 21.3 %collective-permute-start.10 = (bf16[256,768]{1,0:T(8,128)(2,1)S(1)}, bf16[256,768]{1,0:T(8,128)(2,1)S(1)}, u32[]{:S(2)}, u32[]{:S(2)}) collective-permute-start(bf16[256,768]{1,0:T(8,128)(2,1)S(1)} %convolution_convert_fusion.17.refs_4_), channel_id=1, source_target_pairs={{0,1},{1,0},{2,3},{3,2},{4,5},{5,4},{6,7},{7,6},{8,9},{9,8},{10,11... | collective-permute-start | bytes 1179656 | tf_op jit(solution)/shard_map/ppermute | solution.py:30
  148.1 20.4 %collective-permute-start.11 = (bf16[256,768]{1,0:T(8,128)(2,1)S(1)}, bf16[256,768]{1,0:T(8,128)(2,1)S(1)}, u32[]{:S(2)}, u32[]{:S(2)}) collective-permute-start(bf16[256,768]{1,0:T(8,128)(2,1)S(1)} %convolution_convert_fusion.17.refs_4_), channel_id=1, source_target_pairs={{0,2},{1,3},{2,0},{3,1},{4,6},{5,7},{6,4},{7,5},{8,10},{9,11},{10,... | collective-permute-start | bytes 1179656 | tf_op jit(solution)/shard_map/ppermute | solution.py:30
  150.7 18.0 %collective-permute-start.9 = (f32[4,256]{1,0:T(4,128)S(1)}, f32[4,256]{1,0:T(4,128)S(1)}, u32[]{:S(2)}, u32[]{:S(2)}) collective-permute-start(f32[4,256]{1,0:T(4,128)S(1)} %get-tuple-element.156), channel_id=1, source_target_pairs={{0,2},{1,3},{2,0},{3,1},{4,6},{5,7},{6,4},{7,5},{8,10},{9,11},{10,... | collective-permute-start | bytes 12296 | tf_op jit(solution)/shard_map/ppermute | solution.py:30
  233.0 11.3 %collective-permute-start.14 = (bf16[256,768]{1,0:T(8,128)(2,1)S(1)}, bf16[256,768]{1,0:T(8,128)(2,1)S(1)}, u32[]{:S(2)}, u32[]{:S(2)}) collective-permute-start(bf16[256,768]{1,0:T(8,128)(2,1)S(1)} %convolution_convert_fusion.15.refs_0_), channel_id=1, source_target_pairs={{0,2},{1,3},{2,0},{3,1},{4,6},{5,7},{6,4},{7,5},{8,10},{9,11},{10,... | collective-permute-start | bytes 1179656 | tf_op jit(solution)/shard_map/ppermute | solution.py:30
  234.1 16.5 %collective-permute-start.13 = (bf16[256,768]{1,0:T(8,128)(2,1)S(1)}, bf16[256,768]{1,0:T(8,128)(2,1)S(1)}, u32[]{:S(2)}, u32[]{:S(2)}) collective-permute-start(bf16[256,768]{1,0:T(8,128)(2,1)S(1)} %convolution_convert_fusion.15.refs_0_), channel_id=1, source_target_pairs={{0,1},{1,0},{2,3},{3,2},{4,5},{5,4},{6,7},{7,6},{8,9},{9,8},{10,11... | collective-permute-start | bytes 1179656 | tf_op jit(solution)/shard_map/ppermute | solution.py:30
  244.3 6.4 collective-permute-start.15
  259.7 18.8 %collective-permute-start.19 = (bf16[256,768]{1,0:T(8,128)(2,1)S(1)}, bf16[256,768]{1,0:T(8,128)(2,1)S(1)}, u32[]{:S(2)}, u32[]{:S(2)}) collective-permute-start(bf16[256,768]{1,0:T(8,128)(2,1)S(1)} %convolution_convert_fusion.14.refs_4_), channel_id=1, source_target_pairs={{0,2},{1,3},{2,0},{3,1},{4,6},{5,7},{6,4},{7,5},{8,10},{9,11},{10,... | collective-permute-start | bytes 1179656 | tf_op jit(solution)/shard_map/ppermute | solution.py:30
  261.5 18.2 %collective-permute-start.17 = (f32[4,256]{1,0:T(4,128)}, f32[4,256]{1,0:T(4,128)}, u32[]{:S(2)}, u32[]{:S(2)}) collective-permute-start(f32[4,256]{1,0:T(4,128)} %get-tuple-element.148), channel_id=1, source_target_pairs={{0,2},{1,3},{2,0},{3,1},{4,6},{5,7},{6,4},{7,5},{8,10},{9,11},{10,... | collective-permute-start | bytes 12296 | tf_op jit(solution)/shard_map/ppermute | solution.py:30
  347.0 14.2 %collective-permute-start.25 = (bf16[2,256,768]{2,1,0:T(8,128)(2,1)}, bf16[2,256,768]{2,1,0:T(8,128)(2,1)}, u32[]{:S(2)}, u32[]{:S(2)}) collective-permute-start(bf16[2,256,768]{2,1,0:T(8,128)(2,1)} %slice_bitcast_fusion.28), channel_id=1, source_target_pairs={{0,1},{1,0},{2,3},{3,2},{4,5},{5,4},{6,7},{7,6},{8,9},{9,8},{10,11... | collective-permute-start | bytes 2359304 | tf_op jit(solution)/shard_map/ppermute | solution.py:30
  353.7 8.8 %collective-permute-start.23 = (bf16[2,256,768]{2,1,0:T(8,128)(2,1)S(1)}, bf16[2,256,768]{2,1,0:T(8,128)(2,1)S(1)}, u32[]{:S(2)}, u32[]{:S(2)}) collective-permute-start(bf16[2,256,768]{2,1,0:T(8,128)(2,1)S(1)} %slice_bitcast_fusion.30), channel_id=1, source_target_pairs={{0,1},{1,0},{2,3},{3,2},{4,5},{5,4},{6,7},{7,6},{8,9},{9,8},{10,11... | collective-permute-start | bytes 2359304 | tf_op jit(solution)/shard_map/ppermute | solution.py:30
  362.7 12.1 %collective-permute-start.24 = (bf16[1,256,768]{2,1,0:T(8,128)(2,1)S(1)}, bf16[1,256,768]{2,1,0:T(8,128)(2,1)S(1)}, u32[]{:S(2)}, u32[]{:S(2)}) collective-permute-start(bf16[1,256,768]{2,1,0:T(8,128)(2,1)S(1)} %slice_bitcast_fusion.38), channel_id=1, source_target_pairs={{0,2},{1,3},{2,0},{3,1},{4,6},{5,7},{6,4},{7,5},{8,10},{9,11},{10,... | collective-permute-start | bytes 1179656 | tf_op jit(solution)/shard_map/ppermute | solution.py:30
  363.8 18.8 %collective-permute-start.26 = (bf16[1,256,768]{2,1,0:T(8,128)(2,1)S(1)}, bf16[1,256,768]{2,1,0:T(8,128)(2,1)S(1)}, u32[]{:S(2)}, u32[]{:S(2)}) collective-permute-start(bf16[1,256,768]{2,1,0:T(8,128)(2,1)S(1)} %slice_bitcast_fusion.36), channel_id=1, source_target_pairs={{0,2},{1,3},{2,0},{3,1},{4,6},{5,7},{6,4},{7,5},{8,10},{9,11},{10,... | collective-permute-start | bytes 1179656 | tf_op jit(solution)/shard_map/ppermute | solution.py:30
  390.4 332.9 %reduce-scatter.7.cloned.1.call-start = ((), (), s32[]{:S(2)}) async-start(), calls=%async_computation.4 | async-start | bytes 14598144
  442.6 15.3 %collective-permute-start.31 = (bf16[2,256,768]{2,1,0:T(8,128)(2,1)S(1)}, bf16[2,256,768]{2,1,0:T(8,128)(2,1)}, u32[]{:S(2)}, u32[]{:S(2)}) collective-permute-start(bf16[2,256,768]{2,1,0:T(8,128)(2,1)S(1)} %slice_bitcast_fusion.24), channel_id=1, source_target_pairs={{0,1},{1,0},{2,3},{3,2},{4,5},{5,4},{6,7},{7,6},{8,9},{9,8},{10,11... | collective-permute-start | bytes 2359304 | tf_op jit(solution)/shard_map/ppermute | solution.py:30
  450.6 8.6 %collective-permute-start.29 = (bf16[2,256,768]{2,1,0:T(8,128)(2,1)S(1)}, bf16[2,256,768]{2,1,0:T(8,128)(2,1)S(1)}, u32[]{:S(2)}, u32[]{:S(2)}) collective-permute-start(bf16[2,256,768]{2,1,0:T(8,128)(2,1)S(1)} %slice_bitcast_fusion.26), channel_id=1, source_target_pairs={{0,1},{1,0},{2,3},{3,2},{4,5},{5,4},{6,7},{7,6},{8,9},{9,8},{10,11... | collective-permute-start | bytes 2359304 | tf_op jit(solution)/shard_map/ppermute | solution.py:30
  459.4 12.1 %collective-permute-start.30 = (bf16[1,256,768]{2,1,0:T(8,128)(2,1)S(1)}, bf16[1,256,768]{2,1,0:T(8,128)(2,1)S(1)}, u32[]{:S(2)}, u32[]{:S(2)}) collective-permute-start(bf16[1,256,768]{2,1,0:T(8,128)(2,1)S(1)} %slice_bitcast_fusion.34), channel_id=1, source_target_pairs={{0,2},{1,3},{2,0},{3,1},{4,6},{5,7},{6,4},{7,5},{8,10},{9,11},{10,... | collective-permute-start | bytes 1179656 | tf_op jit(solution)/shard_map/ppermute | solution.py:30
  460.9 18.6 %collective-permute-start.32 = (bf16[1,256,768]{2,1,0:T(8,128)(2,1)S(1)}, bf16[1,256,768]{2,1,0:T(8,128)(2,1)S(1)}, u32[]{:S(2)}, u32[]{:S(2)}) collective-permute-start(bf16[1,256,768]{2,1,0:T(8,128)(2,1)S(1)} %slice_bitcast_fusion.32), channel_id=1, source_target_pairs={{0,2},{1,3},{2,0},{3,1},{4,6},{5,7},{6,4},{7,5},{8,10},{9,11},{10,... | collective-permute-start | bytes 1179656 | tf_op jit(solution)/shard_map/ppermute | solution.py:30
  503.4 5.8 collective-permute-start.34
  509.2 7.3 collective-permute-start.35
  516.5 5.9 collective-permute-start.36
  522.4 8.8 %collective-permute-start.37 = (f32[110,128]{1,0:T(8,128)S(1)}, f32[110,128]{1,0:T(8,128)S(1)}, u32[]{:S(2)}, u32[]{:S(2)}) collective-permute-start(f32[110,128]{1,0:T(8,128)S(1)} %add.384), channel_id=1, source_target_pairs={{0,16},{4,20},{8,24},{12,28},{16,0},{20,4},{24,8},{28,12},{1,17},{... | collective-permute-start | bytes 168968 | tf_op jit(solution)/shard_map/ppermute | solution.py:30
  (121 other events, 1336.1 us)
Sparse Core Ops, SparseCore 0:
  14.7 105.2 all-gather.2
  123.5 107.6 all-gather.4
  390.5 164.9 reduce-scatter.8
  561.4 161.8 reduce-scatter.6

commit v3 on v2

--- a/solution.py
+++ b/solution.py
@@ -39,47 +39,153 @@
     return (lax.axis_index(axis) & bit) != 0
 
 
-def gather_line(array, axis):
-    blocks = array[None]
-    for bit in reversed(bits_of(axis)):
+def sum_all(array, axes):
+    for axis in axes:
+        for bit in bits_of(axis):
+            array = array + flip(array, axis, bit)
+    return array
+
+
+def reduce_blocks(planes, steps):
+    count, rows, width = planes.shape
+    dims = [("dp", bit) for bit in reversed(bits_of("dp"))]
+    dims += [("seq", bit) for bit in reversed(bits_of("seq"))]
+    blocks = planes.reshape((count,) + (2,) * len(dims) + (rows >> len(dims), width))
+    for step in steps:
+        axis, bit = step
+        dim = 1 + dims.index(step)
+        mine = upper(axis, bit).astype(jnp.int32)
+        keep = lax.dynamic_index_in_dim(blocks, mine, dim, False)
+        send = lax.dynamic_index_in_dim(blocks, 1 - mine, dim, False)
+        blocks = keep + flip(send, axis, bit)
+        dims.remove(step)
+    return blocks
+
+
+def step_orders():
+    near = [("seq", bit) for bit in bits_of("seq")][:1]
+    across = [("seq", bit) for bit in bits_of("seq")][1:]
+    beside = [("dp", bit) for bit in bits_of("dp")][:1]
+    along = [("dp", bit) for bit in bits_of("dp")][1:]
+    return (
+        near + along + beside + across,
+        near + beside + across + along,
+        near + across + beside + along,
+    )
+
+
+def gather_blocks(array, steps):
+    dims = []
+    blocks = array
+    for axis, bit in steps:
         other = flip(blocks, axis, bit)
         is_upper = upper(axis, bit)
         low = jnp.where(is_upper, other, blocks)
         high = jnp.where(is_upper, blocks, other)
         blocks = jnp.stack([low, high])
-        blocks = blocks.reshape((-1,) + array.shape)
-    steps = len(bits_of(axis))
-    blocks = blocks.reshape((2,) * steps + array.shape)
-    order = tuple(reversed(range(steps))) + tuple(range(steps, blocks.ndim))
-    return blocks.transpose(order).reshape((-1,) + array.shape)
-
-
-def sum_all(array, axes):
-    for axis in axes:
-        for bit in bits_of(axis):
-            array = array + flip(array, axis, bit)
-    return array
-
-
-def pack_weights(w_query, w_key, w_value, w_output, w_inner, w_outer):
-    rows, width = w_query.shape
-    parts = w_inner.shape[1] // width
-    inner = w_inner.reshape(rows, parts, width).transpose(1, 0, 2)
-    outer = w_outer.reshape(parts, rows, width)
-    square = jnp.stack([w_query, w_key, w_value, w_output])
-    return jnp.concatenate([square, inner, outer])
-
-
-def unpack_outer(planes, devices):
-    parts, rows, width = planes.shape
-    split = planes.reshape(parts, devices, rows // devices, width)
-    return split.transpose(1, 0, 2, 3).reshape(parts * rows, width)
-
-
-def pack_outer(grad, parts, devices):
-    rows, width = grad.shape
-    split = grad.reshape(devices, parts, rows // (parts * devices), width)
-    return split.transpose(1, 0, 2, 3).reshape(parts, rows // parts, width)
+        dims.insert(0, (axis, bit))
+    want = [("dp", bit) for bit in reversed(bits_of("dp"))]
+    want += [("seq", bit) for bit in reversed(bits_of("seq"))]
+    order = [dims.index(step) for step in want]
+    blocks = blocks.transpose(order + [len(order), len(order) + 1])
+    return blocks.reshape((-1,) + array.shape)
+
+
+def one_hot(shape, hit):
+    first = lax.broadcasted_iota(jnp.int32, shape, 0)
+    second = lax.broadcasted_iota(jnp.int32, shape, 1)
+    return jnp.where(hit(first, second), 1.0, 0.0).astype(jnp.bfloat16)
+
+
+def pack_kernel(*refs):
+    w_query, w_key, w_value, w_output, w_inner, w_outer = refs[:6]
+    outs = refs[6:]
+    layers, rows, width = w_query.shape
+    parts = w_inner.shape[2] // width
+    lane = width // 6
+    span = lane * parts
+    order = one_hot((span, span), lambda a, b: a == parts * (b % lane) + b // lane)
+    for k in range(layers):
+        out = outs[k]
+        at = 0
+        out[:, at : at + width] = w_output[k]
+        at = width
+        for w in range(6):
+            moved = plain(w_inner[k, :, w * span : (w + 1) * span], order).astype(jnp.bfloat16)
+            for c in range(parts):
+                start = at + c * width + w * lane
+                out[:, start : start + lane] = moved[:, c * lane : (c + 1) * lane]
+        at = at + parts * width
+        for c in range(parts):
+            take = one_hot((rows, parts * rows), lambda a, b, c=c: b == parts * a + c)
+            out[:, at : at + width] = plain(take, w_outer[k]).astype(jnp.bfloat16)
+            at = at + width
+        if k + 1 < layers:
+            for square in (w_query, w_key, w_value):
+                out[:, at : at + width] = square[k + 1]
+                at = at + width
+
+
+def pack(*weights):
+    layers, rows, width = weights[0].shape
+    parts = weights[4].shape[2] // width
+    count = 1 + 2 * parts
+    return pl.pallas_call(
+        pack_kernel,
+        name="pack",
+        out_shape=tuple(
+            jax.ShapeDtypeStruct(
+                (rows, (count + (3 if k + 1 < layers else 0)) * width), jnp.bfloat16
+            )
+            for k in range(layers)
+        ),
+    )(*weights)
+
+
+def spread_inner(grads, out, parts):
+    lane = grads.shape[1] // (6 * parts)
+    span = lane * parts
+    order = one_hot((span, span), lambda a, b: b == parts * (a % lane) + a // lane)
+    for w in range(6):
+        pieces = [grads[:, (c * 6 + w) * lane : (c * 6 + w + 1) * lane] for c in range(parts)]
+        out[:, w * span : (w + 1) * span] = plain(jnp.concatenate(pieces, axis=1), order)
+
+
+def finish_kernel(late_ref, early_ref, one_ref, two_ref, three_ref, *outs):
+    g_query, g_key, g_value, g_output, g_inner, g_outer = outs
+    rows = late_ref.shape[0]
+    width = g_query.shape[2]
+    parts = g_inner.shape[2] // width
+    g_query[0] = three_ref[0].astype(jnp.float32)
+    g_key[0] = three_ref[1].astype(jnp.float32)
+    g_value[0] = two_ref[0].astype(jnp.float32)
+    g_output[0] = one_ref[0].astype(jnp.float32)
+    g_query[1] = late_ref[:, :width].astype(jnp.float32)
+    g_key[1] = late_ref[:, width : 2 * width].astype(jnp.float32)
+    g_value[1] = two_ref[1].astype(jnp.float32)
+    g_output[1] = one_ref[1].astype(jnp.float32)
+    for k, ref, at in ((0, late_ref, 2 * width), (1, early_ref, 0)):
+        spread_inner(ref[:, at : at + parts * width], g_inner.at[k], parts)
+        at = at + parts * width
+        total = 0.0
+        for c in range(parts):
+            put = one_hot((parts * rows, rows), lambda a, b, c=c: a == parts * b + c)
+            total = total + plain(put, ref[:, at + c * width : at + (c + 1) * width])
+        g_outer[k] = total
+
+
+def finish(late, early, one, two, three, width, parts):
+    rows = late.shape[0]
+    square = jax.ShapeDtypeStruct((2, rows, width), jnp.float32)
+    return pl.pallas_call(
+        finish_kernel,
+        name="finish",
+        out_shape=(square,) * 4
+        + (
+            jax.ShapeDtypeStruct((2, rows, parts * width), jnp.float32),
+            jax.ShapeDtypeStruct((2, parts * rows, width), jnp.float32),
+        ),
+    )(late, early, one, two, three)
 
 
 def dims_of(scalars, rows, cols):
@@ -194,7 +300,7 @@
 
 
 def back_kernel(scalars, q_ref, dm_ref, total_ref, carried_ref, before_ref, *refs):
-    count = (len(refs) - 11) // 2
+    count = (len(refs) - 12) // 2
     keys = refs[:count]
     values = refs[count : 2 * count]
     (
@@ -209,6 +315,7 @@
         dprob_ref,
         prob_ref,
         ds_ref,
+        head_ref,
     ) = refs[2 * count :]
     rows = q_ref.shape[0]
     step = pl.program_id(0)
@@ -218,6 +325,7 @@
         fill_bias(scalars, bias_ref, carried_ref, before_ref)
         sum_ref[...] = jnp.zeros_like(sum_ref)
 
+    later_heads = jnp.where(step == 0, 0.0, 1.0)
     eighth = jnp.asarray(0.125, jnp.bfloat16)
     queries = [half(q_ref[...], which) * eighth for which in range(2)]
     grads = [half(dm_ref[...], which) for which in range(2)]
@@ -237,16 +345,10 @@
             dlogits = probs * (dprob - delta)
             prob_ref[which, at, :] = probs.astype(jnp.bfloat16)
             sum_ref[at, :] = sum_ref[at, :] + dlogits
+            if which == 0:
+                head_ref[at, :] = dlogits
+                dlogits = dlogits * later_heads
             ds_ref[which, at, :] = dlogits.astype(jnp.bfloat16)
-            if which == 0:
-
-                @pl.when(step == 0)
-                def _():
-                    first_ref[at, :] = dlogits
-
-    @pl.when(step == 0)
-    def _():
-        ds_ref[0] = jnp.zeros_like(ds_ref[0])
 
     dq = []
     for which in range(2):
@@ -261,6 +363,10 @@
         dv = coldot(prob_ref[0, :, at], grads[0]) + coldot(prob_ref[1, :, at], grads[1])
         dk_ref[b] = dk.astype(jnp.bfloat16)
         dv_ref[b] = dv.astype(jnp.bfloat16)
+
+    @pl.when(step == 0)
+    def _():
+        first_ref[...] = head_ref[...]
 
     @pl.when(step == pl.num_programs(0) - 1)
     def _():
@@ -320,6 +426,7 @@
     rows, width = query.shape
     cols = rows * len(keys)
     pair = pl.BlockSpec((rows, PAIR), lambda h, s: (0, h))
+    second = pl.BlockSpec((rows, PAIR), lambda h, s: (0, width // PAIR + h))
     full = pl.BlockSpec((rows, cols), lambda h, s: (0, 0))
     line = pl.BlockSpec((1, cols), lambda h, s: (0, 0))
     return pl.pallas_call(
@@ -332,7 +439,7 @@
         grid_spec=pltpu.PrefetchScalarGridSpec(
             num_scalar_prefetch=1,
             grid=(width // PAIR,),
-            in_specs=[pair, full, line] + [pair] * (2 * len(keys)),
+            in_specs=[pair, full, line] + [pair] * len(keys) + [second] * len(keys),
             out_specs=(pair, pair),
             scratch_shapes=[
                 pltpu.VMEM((rows, cols), jnp.float32),
@@ -348,6 +455,7 @@
     count = len(keys)
     cols = rows * count
     pair = pl.BlockSpec((rows, PAIR), lambda h, s: (0, h))
+    second = pl.BlockSpec((rows, PAIR), lambda h, s: (0, width // PAIR + h))
     full = pl.BlockSpec((rows, cols), lambda h, s: (0, 0))
     line = pl.BlockSpec((1, cols), lambda h, s: (0, 0))
     blocks = pl.BlockSpec((count, rows, PAIR), lambda h, s: (0, 0, h))
@@ -365,7 +473,7 @@
         grid_spec=pltpu.PrefetchScalarGridSpec(
             num_scalar_prefetch=1,
             grid=(width // PAIR,),
-            in_specs=[pair, pair, pair, full, line] + [pair] * (2 * count),
+            in_specs=[pair, pair, pair, full, line] + [pair] * count + [second] * count,
             out_specs=(pair, blocks, blocks, full, full, line),
             scratch_shapes=[
                 pltpu.VMEM((rows, cols), jnp.float32),
@@ -373,6 +481,7 @@
                 pltpu.VMEM((2, rows, cols), jnp.float32),
                 pltpu.VMEM((2, rows, cols), jnp.bfloat16),
                 pltpu.VMEM((2, rows, cols), jnp.bfloat16),
+                pltpu.VMEM((rows, cols), jnp.float32),
             ],
         ),
     )(scalars, query, grad_mixed, total, carried, before, *keys, *values)
@@ -412,12 +521,12 @@
     return [got[b] for b in range(size)]
 
 
-def collect(blocks, axis):
-    for bit in bits_of(axis):
+def collect(blocks, axis, steps):
+    for bit in steps:
         size = blocks.shape[0] // 2
         pairs = blocks.reshape((size, 2) + blocks.shape[1:])
         blocks = pairs[:, 0] + flip(pairs[:, 1], axis, bit)
-    return blocks[0]
+    return blocks
 
 
 def line_prefix(array, axis, reverse):
@@ -467,48 +576,59 @@
     vectors = jnp.concatenate(
         [gain_attend, shift_attend, gain_mixer, shift_mixer, bias_outer, bias_inner], axis=1
     )
-    vector_rows = gather_line(gather_line(vectors, "seq"), "dp")
     per = width // devices
+    lots = pack(weight_query, weight_key, weight_value, weight_output, weight_inner, weight_outer)
+    whole = [lax.all_gather(lot, both, axis=0, tiled=True) for lot in lots]
+    orders = step_orders()
+    line = jnp.pad(vectors.reshape(1, -1), ((0, 7), (0, width - vectors.size)))
+    first_lot = gather_blocks(
+        jnp.concatenate([weight_query[0], line]), tuple(reversed(orders[1]))
+    )
+    pair_lot = gather_blocks(
+        jnp.concatenate([weight_key[0], weight_value[0]], axis=1), tuple(reversed(orders[0]))
+    )
+    vector_rows = first_lot[:, per, : vectors.size]
+    first_query = first_lot[:, :per].reshape(width, width)
+    first_pair = pair_lot.reshape(width, 2 * width)
     vector_rows = vector_rows.reshape(devices, layers, -1)
     small = [
         vector_rows[:, :, k * per : (k + 1) * per].transpose(1, 0, 2).reshape(layers, width)
         for k in range(5)
     ]
-    small.append(
-        vector_rows[:, :, 5 * per :].transpose(1, 0, 2).reshape(layers, parts * width)
-    )
-    whole = [
-        lax.all_gather(
-            pack_weights(
-                weight_query[k],
-                weight_key[k],
-                weight_value[k],
-                weight_output[k],
-                weight_inner[k],
-                weight_outer[k],
-            ),
-            both,
-            axis=1,
-            tiled=True,
-        )
-        for k in range(layers)
-    ]
-    w_outers = [unpack_outer(planes[4 + parts :], devices) for planes in whole]
-
-    hidden = inputs.astype(jnp.float32)
+    bias_rows = vector_rows[:, :, 5 * per :].transpose(1, 0, 2).reshape(layers, width, parts)
+    small.append(bias_rows.transpose(0, 2, 1).reshape(layers, parts * width))
+    def square_of(matrix, k):
+        return matrix[:, k * width : (k + 1) * width]
+
+    last = 1 + 2 * parts
+
+    def square_at(layer, k):
+        if k >= 3:
+            return square_of(whole[layer], k - 3)
+        if layer == 0:
+            return first_query if k == 0 else square_of(first_pair, k - 1)
+        return square_of(whole[layer - 1], last + k)
+
+    def pair_at(layer):
+        if layer == 0:
+            return first_pair
+        return whole[layer - 1][:, (last + 1) * width : (last + 3) * width]
+
+    def inner_at(layer):
+        return whole[layer][:, width : (1 + parts) * width]
+
+    small, hidden = lax.optimization_barrier((small, inputs))
+    hidden = hidden.astype(jnp.float32)
     share_sum = jnp.zeros((), jnp.float32)
     saved = []
     for layer_index in range(layers):
-        planes = whole[layer_index]
         forward_gain_a, forward_shift_a, forward_gain_m, forward_shift_m = (
             small[k][layer_index] for k in range(4)
         )
         forward_b_outer, forward_b_inner = (small[k][layer_index] for k in (4, 5))
-        forward_w_query, forward_w_key, forward_w_value, forward_w_output = (
-            planes[k] for k in range(4)
-        )
-        forward_w_inner = planes[4 : 4 + parts].transpose(1, 0, 2).reshape(width, parts * width)
-        forward_w_outer = w_outers[layer_index]
+        forward_w_query = square_at(layer_index, 0)
+        forward_w_output = square_at(layer_index, 3)
+        forward_w_inner = inner_at(layer_index)
         forward_normed = (
             layer_norm(
                 hidden, forward_gain_a.astype(jnp.float32), forward_shift_a.astype(jnp.float32)
@@ -516,17 +636,13 @@
             .astype(jnp.bfloat16)
             .reshape(-1, width)
         )
-        forward_keys = jnp.dot(
-            forward_normed, forward_w_key, preferred_element_type=jnp.float32
+        forward_pair = jnp.dot(
+            forward_normed, pair_at(layer_index), preferred_element_type=jnp.float32
         ).astype(jnp.bfloat16)
         forward_query = jnp.dot(
             forward_normed, forward_w_query, preferred_element_type=jnp.float32
         ).astype(jnp.bfloat16)
-        forward_values = jnp.dot(
-            forward_normed, forward_w_value, preferred_element_type=jnp.float32
-        ).astype(jnp.bfloat16)
-        all_keys = spread(forward_keys, "seq")
-        all_values = spread(forward_values, "seq")
+        all_keys = all_values = spread(forward_pair, "seq")
         carried, column = pick(scalars, forward_query, all_keys)
         before, totals = line_prefix(column.reshape(seq_count, local_len), "seq", False)
         before = before.reshape(1, -1)
@@ -549,9 +665,13 @@
             forward_normed_two, forward_w_inner, preferred_element_type=jnp.float32
         ) + forward_b_inner.astype(jnp.float32)
         forward_active = jax.nn.gelu(forward_inner).astype(jnp.bfloat16)
-        outer = jnp.dot(
-            forward_active, forward_w_outer, preferred_element_type=jnp.float32
-        ) + forward_b_outer.astype(jnp.float32)
+        outer = forward_b_outer.astype(jnp.float32)
+        for k in range(parts):
+            outer = outer + jnp.dot(
+                square_of(forward_active, k),
+                square_at(layer_index, 4 + parts + k),
+                preferred_element_type=jnp.float32,
+            )
         result = forward_after + outer.reshape(hidden.shape)
         share = jnp.where(
             is_last,
@@ -576,15 +696,15 @@
         hidden = result
         share_sum = share_sum + share
         saved.append(forward_kept)
+    cotangent, _ = lax.optimization_barrier((cotangent, saved[-1][8]))
     grad_hidden = cotangent
-    reduced = [None] * layers
+    wide_sums = []
+    held = []
     vector_grads = [None] * layers
     for layer_index in reversed(range(layers)):
-        planes = whole[layer_index]
         gain_a, shift_a, gain_m, shift_m = (small[k][layer_index] for k in range(4))
-        w_query, w_key, w_value, w_output = (planes[k] for k in range(4))
-        w_inner = planes[4 : 4 + parts].transpose(1, 0, 2).reshape(width, parts * width)
-        w_outer = w_outers[layer_index]
+        w_query, w_key, w_value, w_output = (square_at(layer_index, k) for k in range(4))
+        w_inner = inner_at(layer_index)
         (
             backward_hidden,
             normed,
@@ -602,8 +722,14 @@
         ) = saved[layer_index]
         grad_y = grad_hidden.astype(jnp.bfloat16).reshape(-1, width)
         grad_b_outer = jnp.sum(grad_y, axis=0, dtype=jnp.float32)
-        grad_w_outer = product(active, grad_y, "tf,td->fd")
-        grad_active = product(grad_y, w_outer, "td,fd->tf")
+        grad_w_outer = [product(square_of(active, k), grad_y, "tf,td->fd") for k in range(parts)]
+        grad_active = jnp.concatenate(
+            [
+                product(grad_y, square_at(layer_index, 4 + parts + k), "td,fd->tf")
+                for k in range(parts)
+            ],
+            axis=1,
+        )
         gelu_back = jax.vjp(jax.nn.gelu, inner)[1]
         grad_inner = gelu_back(grad_active)[0].astype(jnp.bfloat16)
         grad_b_inner = jnp.sum(grad_inner, axis=0, dtype=jnp.float32)
@@ -615,13 +741,20 @@
         after_part, grad_gain_m, grad_shift_m = norm_back_two(grad_normed_two)
         grad_after = grad_hidden + after_part
         grad_attn = grad_after.astype(jnp.bfloat16).reshape(-1, width)
-        grad_w_output = product(mixed, grad_attn, "tc,td->cd")
+        wide = [piece.astype(jnp.bfloat16) for piece in [grad_w_inner] + grad_w_outer]
+        wide = jnp.concatenate(held[:2] + wide, axis=1)
+        wide, grad_attn = lax.optimization_barrier((wide, grad_attn))
+        wide_sums.append(lax.psum_scatter(wide, both, scatter_dimension=0, tiled=True))
         grad_mixed = product(grad_attn, w_output, "td,cd->tc").astype(jnp.bfloat16)
         grad_query, key_part, value_part, sums, first_logits, column_back = back(
             scalars, backward_query, grad_mixed, log_total, carried, before, all_keys, all_values
         )
-        grad_vals = collect(value_part, "seq")
+        steps = bits_of("seq")
+        grad_w_output = product(mixed, grad_attn, "tc,td->cd").astype(jnp.bfloat16)
+        value_part = collect(value_part, "seq", steps[:1])
         later, _ = line_prefix(column_back.reshape(seq_count, local_len), "seq", True)
+        grad_vals = collect(value_part, "seq", steps[1:])[0]
+        later, grad_vals = lax.optimization_barrier((later, grad_vals))
         grad_query, key_part = first(
             scalars,
             backward_query,
@@ -632,8 +765,11 @@
             key_part,
             all_keys,
         )
-        grad_keys = collect(key_part, "seq")
-        grad_w_query = product(normed, grad_query, "tc,td->cd")
+        grad_keys = collect(key_part, "seq", steps)[0]
+        grad_w_query = product(normed, grad_query, "tc,td->cd").astype(jnp.bfloat16)
+        grad_keys, grad_vals, grad_w_query, grad_w_output = lax.optimization_barrier(
+            (grad_keys, grad_vals, grad_w_query, grad_w_output)
+        )
         grad_w_key = product(normed, grad_keys, "tc,td->cd")
         grad_w_value = product(normed, grad_vals, "tc,td->cd")
         grad_normed = (
@@ -649,15 +785,12 @@
         )
         grad_hidden = grad_after + hidden_part
         low = jnp.bfloat16
-        pieces = [
-            piece.astype(low)[None]
+        squares = [
+            piece.astype(low)
             for piece in (grad_w_query, grad_w_key, grad_w_value, grad_w_output)
         ]
-        pieces.append(grad_w_inner.astype(low).reshape(width, parts, width).transpose(1, 0, 2))
-        pieces.append(pack_outer(grad_w_outer.astype(low), parts, devices))
-        reduced[layer_index] = lax.psum_scatter(
-            jnp.concatenate(pieces), both, scatter_dimension=1, tiled=True
-        ).astype(jnp.float32)
+        kept = held
+        held = squares
         vector_grads[layer_index] = jnp.concatenate(
             [
                 grad_gain_a,
@@ -677,6 +810,8 @@
     selected = flat[layers * size] / (layers * flat[layers * size + 128])
     place_of = lax.axis_index("dp") * seq_count + place
     vec = flat[: layers * size].reshape(layers, size)
+    bias_grads = vec[:, 5 * width :].reshape(layers, parts, width).transpose(0, 2, 1)
+    vec = jnp.concatenate([vec[:, : 5 * width], bias_grads.reshape(layers, -1)], axis=1)
 
     def mine(first, length):
         return lax.dynamic_slice_in_dim(
@@ -685,25 +820,25 @@
         )
 
     rows = width // devices
-    stack = jnp.stack(reduced)
-    grads_inner = (
-        stack[:, 4 : 4 + parts].transpose(0, 2, 1, 3).reshape(layers, rows, parts * width)
-    )
-    grads_outer = stack[:, 4 + parts :].reshape(layers, parts * rows, width)
+
+    one = reduce_blocks(jnp.stack([squares[3], kept[3]]), orders[0])
+    two = reduce_blocks(jnp.stack([squares[2], kept[2]]), orders[1])
+    three = reduce_blocks(jnp.stack(squares[:2]), orders[2])
+    square_sums = finish(wide_sums[1], wide_sums[0], one, two, three, width, parts)
     return (
         hidden,
         grad_hidden,
         mine(0, width),
         mine(1, width),
-        stack[:, 0],
-        stack[:, 1],
-        stack[:, 2],
-        stack[:, 3],
+        square_sums[0],
+        square_sums[1],
+        square_sums[2],
+        square_sums[3],
         mine(2, width),
         mine(3, width),
-        grads_inner,
+        square_sums[4],
         mine(5, parts * width),
-        grads_outer,
+        square_sums[5],
         mine(4, width),
         selected,
     )

time: 744 us -> 606 us (0.81)
  waiting for transfers between devices: 389 us -> 269 us
  local copies, waits for them, and re-layouts: 91.5 us -> 45.1 us
  other arithmetic: 27.1 us -> 50.7 us
  Pallas kernels: 93.1 us -> 78.3 us
  starting transfers between devices: 34 us -> 44.8 us
  matrix products: 80 us -> 89 us
    unnamed x6 -> x4, waiting for transfers between devices: 185 us -> 0.75 us
    ppermute x38 -> x52, waiting for transfers between devices: 81.6 us -> 227 us  [flip(): return lax.ppermute(array, axis, [(i, i ^ bit) for i in range(size)])]
    all_gather x2, waiting for transfers between devices: 123 us -> 20.7 us  [local(): whole = [lax.all_gather(lot, both, axis=0, tiled=True) for lot in lots]]
    unnamed x260 -> x252, local copies, waits for them, and re-layouts: 44.3 us -> 12.3 us
    pallas_call x2, Pallas kernels: 55.3 us -> 32.8 us  [back(): pl.pallas_call(back_kernel, name='back', out_shape=(jax.ShapeDtypeStruct(...]
    reduce_scatter x0 -> x2, waiting for transfers between devices: none -> 20.7 us  [local(): lax.psum_scatter(wide, both, scatter_dimension=0, tiled=True)]
    slice x8 -> x3, local copies, waits for them, and re-layouts: 18.3 us -> 1.6 us  [the longest x1 1.35 us: local(): vec[:, 5 * width:].reshape(layers, parts, width).transpose(0, 2, 1)]
    dot_general x24 -> x36, matrix products: 46.6 us -> 59.2 us  [product(): return jnp.einsum(form, left, right, preferred_element_type=jnp.float32)]
  transfers between devices with their start and end apart: 42 -> 56, of which waited for: 26 -> 32; matrix products, arithmetic and copies ran while one was open for 20% -> 25% of each run, Pallas kernels for 7% -> 12%
where the time goes in v3:
time: 606 us; the launch traced here: 598 us
  waiting for transfers between devices  269 us (44%)
  matrix products  89 us (15%)
  Pallas kernels  78.3 us (13%)
  other arithmetic  50.7 us (8%)
  local copies, waits for them, and re-layouts  45.1 us (7%)
  starting transfers between devices  44.8 us (7%)
  between operations  20.8 us (3%)
    ppermute x52, waiting for transfers between devices, flip(): return lax.ppermute(array, axis, [(i, i ^ bit) for i in range(size)])  227 us
    dot_general x36, matrix products, product(): return jnp.einsum(form, left, right, preferred_element_type=jnp.float32)  59.2 us
    ppermute x52, starting transfers between devices, flip(): return lax.ppermute(array, axis, [(i, i ^ bit) for i in range(size)])  44.6 us
    pallas_call x2, Pallas kernels, back(): pl.pallas_call(back_kernel, name='back', out_shape=(jax.ShapeDtypeStruct(...  32.8 us
    pallas_call x2, Pallas kernels, mix(): pl.pallas_call(mix_kernel, name='mix', out_shape=(jax.ShapeDtypeStruct((r...  22.1 us
    all_gather x2, waiting for transfers between devices, local(): whole = [lax.all_gather(lot, both, axis=0, tiled=True) for lot in lots]  20.7 us
    reduce_scatter x2, waiting for transfers between devices, local(): lax.psum_scatter(wide, both, scatter_dimension=0, tiled=True)  20.7 us
    unnamed x252, local copies, waits for them, and re-layouts  12.3 us
  transfers between devices with their start and end apart: 56, of which 32 were waited for; matrix products, arithmetic and copies ran while one was open for 25% of the time, Pallas kernels for 12%

profile of v3, /device:TPU:0, one launch (start us, length us, event | category | flops | bytes accessed | tf_op | source)
XLA Modules:
  0.0 597.8 jit_solution(6407509546637956442)
XLA Ops:
  7.2 3.4 pack.1
  13.1 4.1 collective-permute-start
  26.4 4.0 collective-permute-done.6
  34.3 14.7 %collective-permute-done.7 = bf16[2,2,24,1536]{3,2,1,0:T(8,128)(2,1)S(1)} collective-permute-done((bf16[2,2,24,1536]{3,2,1,0:T(8,128)(2,1)S(1)}, bf16[2,2,24,1536]{3,2,1,0:T(8,128)(2,1)S(1)}, u32[]{:S(2)}, u32[]{:S(2)}) %collective-permute-start.7) | collective-permute-done | bytes 294944 | tf_op jit(solution)/shard_map/ppermute | solution.py:30
  49.5 33.3 %collective-permute-done.8 = bf16[2,2,2,24,1536]{4,3,2,1,0:T(8,128)(2,1)} collective-permute-done((bf16[2,2,2,24,1536]{4,3,2,1,0:T(8,128)(2,1)S(1)}, bf16[2,2,2,24,1536]{4,3,2,1,0:T(8,128)(2,1)}, u32[]{:S(2)}, u32[]{:S(2)}) %collective-permute-start.8) | collective-permute-done | bytes 589856 | tf_op jit(solution)/shard_map/ppermute | solution.py:30
  97.7 33.3 %collective-permute-done.11.refs_2_.refs_6_ = bf16[256,1536]{1,0:T(8,128)(2,1)S(1)} collective-permute-done((bf16[256,1536]{1,0:T(8,128)(2,1)S(1)}, bf16[256,1536]{1,0:T(8,128)(2,1)S(1)}, u32[]{:S(2)}, u32[]{:S(2)}) %collective-permute-start.11) | collective-permute-done | bytes 786464 | tf_op jit(solution)/shard_map/ppermute | solution.py:30
  134.8 3.7 pick.2
  146.2 11.0 %mix.2 = (bf16[256,768]{1,0:T(8,128)(2,1)}, f32[256,768]{1,0:T(8,128)}) custom-call(s32[2]{0:T(128)} %pad_add_fusion.scalars, bf16[256,768]{1,0:T(8,128)(2,1)} %convolution_convert_fusion.23.q_ref, f32[256,1024]{1,0:T(8,128)} %get-tuple-element.74.carried_ref, f32[1,1024]{1,0:T(1,128)} %fusion.163.before_ref, bf16[256,1536]{1,0:T(8,128)(2,1)} %copy-done, ...), custom_call_target="tpu_custom_call" | custom-call | tf_op jit(solution)/shard_map/mix/pallas_call | solution.py:432
  159.5 6.4 %multiply_convert_fusion.1 = (bf16[256,3072]{1,0:T(8,128)(2,1)S(1)}, f32[256,3072]{1,0:T(8,128)}) fusion(f32[3072]{0:T(1024)S(1)} %bitcast.481, bf16[768,9216]{1,0:T(8,128)(2,1)} %all-gather.3.cloned.1.call-done, f32[1,256,768]{2,1,0:T(8,128)S(1)} %get-tuple-element.239, f32[768]{0:T(1024)S(1)} %get-tuple-element.140, f32[768]{0:T(1024)S(1)} %get-tuple-element.251, ...), kind=kOutput, calls=%fused_computation.37 | convolution fusion | flops 1216806912 | bytes 10244096 | tf_op jit(solution)/shard_map/dot_general | solution.py:664
  172.5 27.8 %collective-permute-done.16.refs_2_.refs_6_ = bf16[256,1536]{1,0:T(8,128)(2,1)S(1)} collective-permute-done((bf16[256,1536]{1,0:T(8,128)(2,1)S(1)}, bf16[256,1536]{1,0:T(8,128)(2,1)S(1)}, u32[]{:S(2)}, u32[]{:S(2)}) %collective-permute-start.16) | collective-permute-done | bytes 786464 | tf_op jit(solution)/shard_map/ppermute | solution.py:30
  203.4 3.7 pick.3
  215.5 11.1 %mix.3 = (bf16[256,768]{1,0:T(8,128)(2,1)}, f32[256,768]{1,0:T(8,128)}) custom-call(s32[2]{0:T(128)} %pad_add_fusion.scalars, bf16[256,768]{1,0:T(8,128)(2,1)} %convolution_convert_fusion.22.q_ref, f32[256,1024]{1,0:T(8,128)} %get-tuple-element.82.carried_ref, f32[1,1024]{1,0:T(1,128)} %get-tuple-element.209.before_ref, bf16[256,1536]{1,0:T(8,128)(2,1)} %copy-done.4, ...), custom_call_target="tpu_custom_call" | custom-call | tf_op jit(solution)/shard_map/mix/pallas_call | solution.py:432
  226.7 20.7 %all-gather.5.cloned.1.call-done = bf16[768,6912]{1,0:T(8,128)(2,1)} async-done(((bf16[24,6912]{1,0:T(8,128)(2,1)}), bf16[768,6912]{1,0:T(8,128)(2,1)}) %all-gather.5.cloned.1.call-update) | async-done | bytes 10616848 | tf_op jit(solution)/shard_map/all_gather | solution.py:581
  256.2 4.2 convert_reduce_fusion
  260.4 3.7 fusion
  278.4 16.4 %back.2 = (bf16[256,768]{1,0:T(8,128)(2,1)}, bf16[4,256,768]{2,1,0:T(8,128)(2,1)}, bf16[4,256,768]{2,1,0:T(8,128)(2,1)}, f32[256,1024]{1,0:T(8,128)}, f32[256,1024]{1,0:T(8,128)}, /*index=5*/f32[1,1024]{1,0:T(1,128)}) custom-call(s32[2]{0:T(128)} %pad_add_fusion.scalars, bf16[256,768]{1,0:T(8,128)(2,1)} %convolution_convert_fusion.22.q_ref, ...), custom_call_target="tpu_custom_call" | custom-call | tf_op jit(solution)/shard_map/back/pallas_call | solution.py:462
  302.9 9.3 %collective-permute-done.21 = f32[4,256]{1,0:T(4,128)S(1)} collective-permute-done((f32[4,256]{1,0:T(4,128)S(1)}, f32[4,256]{1,0:T(4,128)S(1)}, u32[]{:S(2)}, u32[]{:S(2)}) %collective-permute-start.21) | collective-permute-done | bytes 4128 | tf_op jit(solution)/shard_map/ppermute | solution.py:30
  314.6 4.5 first.2
  327.6 16.1 %collective-permute-done.25 = bf16[1,256,768]{2,1,0:T(8,128)(2,1)S(1)} collective-permute-done((bf16[1,256,768]{2,1,0:T(8,128)(2,1)S(1)}, bf16[1,256,768]{2,1,0:T(8,128)(2,1)S(1)}, u32[]{:S(2)}, u32[]{:S(2)}) %collective-permute-start.25) | collective-permute-done | bytes 393248 | tf_op jit(solution)/shard_map/ppermute | solution.py:30
  367.4 3.8 fusion.1
  381.2 16.4 %back.3 = (bf16[256,768]{1,0:T(8,128)(2,1)}, bf16[4,256,768]{2,1,0:T(8,128)(2,1)}, bf16[4,256,768]{2,1,0:T(8,128)(2,1)}, f32[256,1024]{1,0:T(8,128)}, f32[256,1024]{1,0:T(8,128)}, /*index=5*/f32[1,1024]{1,0:T(1,128)}) custom-call(s32[2]{0:T(128)} %pad_add_fusion.scalars, bf16[256,768]{1,0:T(8,128)(2,1)} %convolution_convert_fusion.23.q_ref, ...), custom_call_target="tpu_custom_call" | custom-call | tf_op jit(solution)/shard_map/back/pallas_call | solution.py:462
  412.5 6.1 %collective-permute-done.29 = bf16[1,256,768]{2,1,0:T(8,128)(2,1)} collective-permute-done((bf16[1,256,768]{2,1,0:T(8,128)(2,1)}, bf16[1,256,768]{2,1,0:T(8,128)(2,1)}, u32[]{:S(2)}, u32[]{:S(2)}) %collective-permute-start.29) | collective-permute-done | bytes 393248 | tf_op jit(solution)/shard_map/ppermute | solution.py:30
  421.1 4.4 first.3
  442.0 4.1 collective-permute-done.31
  496.0 22.3 %collective-permute-done.38 = bf16[2,2,2,2,24,768]{5,4,3,2,1,0:T(8,128)(2,1)S(1)} collective-permute-done((bf16[2,2,2,2,24,768]{5,4,3,2,1,0:T(8,128)(2,1)S(1)}, bf16[2,2,2,2,24,768]{5,4,3,2,1,0:T(8,128)(2,1)S(1)}, u32[]{:S(2)}, u32[]{:S(2)}) %collective-permute-start.38) | collective-permute-done | bytes 589856 | tf_op jit(solution)/shard_map/ppermute | solution.py:30
  522.3 12.2 %collective-permute-done.39 = bf16[2,2,2,24,768]{4,3,2,1,0:T(8,128)(2,1)S(1)} collective-permute-done((bf16[2,2,2,24,768]{4,3,2,1,0:T(8,128)(2,1)S(1)}, bf16[2,2,2,24,768]{4,3,2,1,0:T(8,128)(2,1)S(1)}, u32[]{:S(2)}, u32[]{:S(2)}) %collective-permute-start.39) | collective-permute-done | bytes 294944 | tf_op jit(solution)/shard_map/ppermute | solution.py:30
  542.0 6.6 %collective-permute-done.45 = bf16[2,2,24,768]{3,2,0,1:T(8,128)(2,1)S(1)} collective-permute-done((bf16[2,2,24,768]{3,2,0,1:T(8,128)(2,1)S(1)}, bf16[2,2,24,768]{3,2,0,1:T(8,128)(2,1)S(1)}, u32[]{:S(2)}, u32[]{:S(2)}) %collective-permute-start.45) | collective-permute-done | bytes 147488 | tf_op jit(solution)/shard_map/ppermute | solution.py:30
  548.7 6.5 %collective-permute-done.50 = bf16[2,2,24,768]{3,2,0,1:T(8,128)(2,1)S(1)} collective-permute-done((bf16[2,2,24,768]{3,2,0,1:T(8,128)(2,1)S(1)}, bf16[2,2,24,768]{3,2,0,1:T(8,128)(2,1)S(1)}, u32[]{:S(2)}, u32[]{:S(2)}) %collective-permute-start.50) | collective-permute-done | bytes 147488 | tf_op jit(solution)/shard_map/ppermute | solution.py:30
  556.0 4.9 collective-permute-done.46
  561.5 3.1 collective-permute-done.51
  565.2 20.7 %reduce-scatter.3.cloned.1.call-done.late_ref = bf16[24,7680]{1,0:T(8,128)(2,1)} async-done(((bf16[768,7680]{1,0:T(8,128)(2,1)}), bf16[24,7680]{1,0:T(8,128)(2,1)}) %reduce-scatter.3.cloned.1.call-update) | async-done | bytes 368656 | tf_op jit(solution)/shard_map/reduce_scatter | solution.py:747
  585.9 3.7 finish.1
  (585 shorter events, 230.7 us)
Async XLA Ops:
  7.2 150.0 %all-gather.3.cloned.1.call-start = ((), (), s32[]{:S(2)}) async-start(), calls=%async_computation.2 | async-start | bytes 14598144 | tf_op jit(solution)/shard_map/all_gather | solution.py:581
  10.6 236.8 %all-gather.5.cloned.1.call-start = ((), (), s32[]{:S(2)}) async-start(), calls=%async_computation.3 | async-start | bytes 10948608 | tf_op jit(solution)/shard_map/all_gather | solution.py:581
  11.4 553.8 %reduce-scatter.5.cloned.1.call-start = ((), (), s32[]{:S(2)}) async-start(), calls=%async_computation.5 | async-start | bytes 9732096 | tf_op jit(solution)/shard_map/reduce_scatter | solution.py:747
  24.6 8.2 %collective-permute-start.2 = (bf16[2,2,32,768]{3,2,0,1:T(8,128)(2,1)S(1)}, bf16[2,2,32,768]{3,2,0,1:T(8,128)(2,1)S(1)}, u32[]{:S(2)}, u32[]{:S(2)}) collective-permute-start(bf16[2,2,32,768]{3,2,0,1:T(8,128)(2,1)S(1)} %pad_maximum_fusion.9), channel_id=1, source_target_pairs={{0,2},{1,3},{2,0},{3,1},{4,6},{5,7},{6,4},{7,5},{8,10},{9,11},{10,... | collective-permute-start | bytes 589832 | tf_op jit(solution)/shard_map/ppermute | solution.py:30
  30.4 18.7 %collective-permute-start.7 = (bf16[2,2,24,1536]{3,2,1,0:T(8,128)(2,1)S(1)}, bf16[2,2,24,1536]{3,2,1,0:T(8,128)(2,1)S(1)}, u32[]{:S(2)}, u32[]{:S(2)}) collective-permute-start(bf16[2,2,24,1536]{3,2,1,0:T(8,128)(2,1)S(1)} %pad_maximum_fusion.8), channel_id=1, source_target_pairs={{0,16},{4,20},{8,24},{12,28},{16,0},{20,4},{24,8},{28,12},{1,17},{... | collective-permute-start | bytes 884744 | tf_op jit(solution)/shard_map/ppermute | solution.py:30
  32.9 16.4 %collective-permute-start.3 = (bf16[2,2,2,32,768]{4,3,0,1,2:T(8,128)(2,1)S(1)}, bf16[2,2,2,32,768]{4,3,0,1,2:T(8,128)(2,1)S(1)}, u32[]{:S(2)}, u32[]{:S(2)}) collective-permute-start(bf16[2,2,2,32,768]{4,3,0,1,2:T(8,128)(2,1)S(1)} %pad_maximum_fusion.7), channel_id=1, source_target_pairs={{0,4},{4,0},{8,12},{12,8},{16,20},{20,16},{24,28},{28,24},{1,5},{5... | collective-permute-start | bytes 1179656 | tf_op jit(solution)/shard_map/ppermute | solution.py:30
  49.2 33.6 %collective-permute-start.8 = (bf16[2,2,2,24,1536]{4,3,2,1,0:T(8,128)(2,1)S(1)}, bf16[2,2,2,24,1536]{4,3,2,1,0:T(8,128)(2,1)}, u32[]{:S(2)}, u32[]{:S(2)}) collective-permute-start(bf16[2,2,2,24,1536]{4,3,2,1,0:T(8,128)(2,1)S(1)} %pad_maximum_fusion.6), channel_id=1, source_target_pairs={{0,8},{4,12},{8,0},{12,4},{16,24},{20,28},{24,16},{28,20},{1,9},{5... | collective-permute-start | bytes 1769480 | tf_op jit(solution)/shard_map/ppermute | solution.py:30
  49.4 35.7 %collective-permute-start.4 = (bf16[2,2,2,2,32,768]{5,4,1,0,2,3:T(8,128)(2,1)S(1)}, bf16[2,2,2,2,32,768]{5,4,1,0,2,3:T(8,128)(2,1)}, u32[]{:S(2)}, u32[]{:S(2)}) collective-permute-start(bf16[2,2,2,2,32,768]{5,4,1,0,2,3:T(8,128)(2,1)S(1)} %pad_maximum_fusion.5), channel_id=1, source_target_pairs={{0,1},{1,0},{2,3},{3,2},{4,5},{5,4},{6,7},{7,6},{8,9},{9,8},{10,11... | collective-permute-start | bytes 2359304 | tf_op jit(solution)/shard_map/ppermute | solution.py:30
  94.9 36.1 %collective-permute-start.11 = (bf16[256,1536]{1,0:T(8,128)(2,1)S(1)}, bf16[256,1536]{1,0:T(8,128)(2,1)S(1)}, u32[]{:S(2)}, u32[]{:S(2)}) collective-permute-start(bf16[256,1536]{1,0:T(8,128)(2,1)S(1)} %convolution_convert_fusion.3.refs_0_.refs_4_), channel_id=1, source_target_pairs={{0,2},{1,3},{2,0},{3,1},{4,6},{5,7},{6,4},{7,5},{8,10},{9,11},{10,... | collective-permute-start | bytes 2359304 | tf_op jit(solution)/shard_map/ppermute | solution.py:30
  97.4 35.6 %collective-permute-start.10 = (bf16[256,1536]{1,0:T(8,128)(2,1)S(1)}, bf16[256,1536]{1,0:T(8,128)(2,1)S(1)}, u32[]{:S(2)}, u32[]{:S(2)}) collective-permute-start(bf16[256,1536]{1,0:T(8,128)(2,1)S(1)} %convolution_convert_fusion.3.refs_0_.refs_4_), channel_id=1, source_target_pairs={{0,1},{1,0},{2,3},{3,2},{4,5},{5,4},{6,7},{7,6},{8,9},{9,8},{10,11... | collective-permute-start | bytes 2359304 | tf_op jit(solution)/shard_map/ppermute | solution.py:30
  171.8 28.5 %collective-permute-start.16 = (bf16[256,1536]{1,0:T(8,128)(2,1)S(1)}, bf16[256,1536]{1,0:T(8,128)(2,1)S(1)}, u32[]{:S(2)}, u32[]{:S(2)}) collective-permute-start(bf16[256,1536]{1,0:T(8,128)(2,1)S(1)} %convolution_convert_fusion.2.refs_0_.refs_4_), channel_id=1, source_target_pairs={{0,2},{1,3},{2,0},{3,1},{4,6},{5,7},{6,4},{7,5},{8,10},{9,11},{10,... | collective-permute-start | bytes 2359304 | tf_op jit(solution)/shard_map/ppermute | solution.py:30
  172.5 29.0 %collective-permute-start.15 = (bf16[256,1536]{1,0:T(8,128)(2,1)S(1)}, bf16[256,1536]{1,0:T(8,128)(2,1)S(1)}, u32[]{:S(2)}, u32[]{:S(2)}) collective-permute-start(bf16[256,1536]{1,0:T(8,128)(2,1)S(1)} %convolution_convert_fusion.2.refs_0_.refs_4_), channel_id=1, source_target_pairs={{0,1},{1,0},{2,3},{3,2},{4,5},{5,4},{6,7},{7,6},{8,9},{9,8},{10,11... | collective-permute-start | bytes 2359304 | tf_op jit(solution)/shard_map/ppermute | solution.py:30
  275.2 310.7 %reduce-scatter.3.cloned.1.call-start = ((), (), s32[]{:S(2)}) async-start(), calls=%async_computation.4 | async-start | bytes 12165120 | tf_op jit(solution)/shard_map/reduce_scatter | solution.py:747
  300.6 12.3 %collective-permute-start.23 = (bf16[1,256,768]{2,1,0:T(8,128)(2,1)S(1)}, bf16[1,256,768]{2,1,0:T(8,128)(2,1)}, u32[]{:S(2)}, u32[]{:S(2)}) collective-permute-start(bf16[1,256,768]{2,1,0:T(8,128)(2,1)S(1)} %slice_bitcast_fusion.14), channel_id=1, source_target_pairs={{0,2},{1,3},{2,0},{3,1},{4,6},{5,7},{6,4},{7,5},{8,10},{9,11},{10,... | collective-permute-start | bytes 1179656 | tf_op jit(solution)/shard_map/ppermute | solution.py:30
  302.1 10.1 %collective-permute-start.21 = (f32[4,256]{1,0:T(4,128)S(1)}, f32[4,256]{1,0:T(4,128)S(1)}, u32[]{:S(2)}, u32[]{:S(2)}) collective-permute-start(f32[4,256]{1,0:T(4,128)S(1)} %fusion.169), channel_id=1, source_target_pairs={{0,2},{1,3},{2,0},{3,1},{4,6},{5,7},{6,4},{7,5},{8,10},{9,11},{10,... | collective-permute-start | bytes 12296 | tf_op jit(solution)/shard_map/ppermute | solution.py:30
  324.1 19.6 %collective-permute-start.25 = (bf16[1,256,768]{2,1,0:T(8,128)(2,1)S(1)}, bf16[1,256,768]{2,1,0:T(8,128)(2,1)S(1)}, u32[]{:S(2)}, u32[]{:S(2)}) collective-permute-start(bf16[1,256,768]{2,1,0:T(8,128)(2,1)S(1)} %slice_bitcast_fusion.12), channel_id=1, source_target_pairs={{0,2},{1,3},{2,0},{3,1},{4,6},{5,7},{6,4},{7,5},{8,10},{9,11},{10,... | collective-permute-start | bytes 1179656 | tf_op jit(solution)/shard_map/ppermute | solution.py:30
  407.2 11.4 %collective-permute-start.29 = (bf16[1,256,768]{2,1,0:T(8,128)(2,1)}, bf16[1,256,768]{2,1,0:T(8,128)(2,1)}, u32[]{:S(2)}, u32[]{:S(2)}) collective-permute-start(bf16[1,256,768]{2,1,0:T(8,128)(2,1)} %slice_bitcast_fusion.10), channel_id=1, source_target_pairs={{0,2},{1,3},{2,0},{3,1},{4,6},{5,7},{6,4},{7,5},{8,10},{9,11},{10,... | collective-permute-start | bytes 1179656 | tf_op jit(solution)/shard_map/ppermute | solution.py:30
  434.3 11.8 %collective-permute-start.31 = (bf16[1,256,768]{2,1,0:T(8,128)(2,1)}, bf16[1,256,768]{2,1,0:T(8,128)(2,1)}, u32[]{:S(2)}, u32[]{:S(2)}) collective-permute-start(bf16[1,256,768]{2,1,0:T(8,128)(2,1)} %slice_bitcast_fusion.8), channel_id=1, source_target_pairs={{0,2},{1,3},{2,0},{3,1},{4,6},{5,7},{6,4},{7,5},{8,10},{9,11},{10,... | collective-permute-start | bytes 1179656 | tf_op jit(solution)/shard_map/ppermute | solution.py:30
  459.7 28.5 %collective-permute-start.37 = (bf16[2,2,2,2,2,24,768]{6,5,4,3,1,0,2:T(8,128)(2,1)}, bf16[2,2,2,2,2,24,768]{6,5,4,3,1,0,2:T(8,128)(2,1)}, u32[]{:S(2)}, u32[]{:S(2)}) collective-permute-start(bf16[2,2,2,2,2,24,768]{6,5,4,3,1,0,2:T(8,128)(2,1)} %bitcast.429), channel_id=1, source_target_pairs={{0,1},{1,0},{2,3},{3,2},{4,5},{5,4},{6,7},{7,6},{8,9},{9,8},{10,11... | collective-permute-start | bytes 3538952 | tf_op jit(solution)/shard_map/ppermute | solution.py:30
  470.8 20.6 %collective-permute-start.42 = (bf16[2,2,2,2,2,24,768]{6,5,4,2,1,0,3:T(8,128)(2,1)}, bf16[2,2,2,2,2,24,768]{6,5,4,2,1,0,3:T(8,128)(2,1)}, u32[]{:S(2)}, u32[]{:S(2)}) collective-permute-start(bf16[2,2,2,2,2,24,768]{6,5,4,2,1,0,3:T(8,128)(2,1)} %bitcast.428), channel_id=1, source_target_pairs={{0,1},{1,0},{2,3},{3,2},{4,5},{5,4},{6,7},{7,6},{8,9},{9,8},{10,11... | collective-permute-start | bytes 3538952 | tf_op jit(solution)/shard_map/ppermute | solution.py:30
  470.8 22.5 %collective-permute-start.47 = (bf16[2,2,2,2,2,24,768]{6,5,3,2,1,0,4:T(8,128)(2,1)}, bf16[2,2,2,2,2,24,768]{6,5,3,2,1,0,4:T(8,128)(2,1)}, u32[]{:S(2)}, u32[]{:S(2)}) collective-permute-start(bf16[2,2,2,2,2,24,768]{6,5,3,2,1,0,4:T(8,128)(2,1)} %bitcast.427), channel_id=1, source_target_pairs={{0,1},{1,0},{2,3},{3,2},{4,5},{5,4},{6,7},{7,6},{8,9},{9,8},{10,11... | collective-permute-start | bytes 3538952 | tf_op jit(solution)/shard_map/ppermute | solution.py:30
  489.6 28.8 %collective-permute-start.38 = (bf16[2,2,2,2,24,768]{5,4,3,2,1,0:T(8,128)(2,1)S(1)}, bf16[2,2,2,2,24,768]{5,4,3,2,1,0:T(8,128)(2,1)S(1)}, u32[]{:S(2)}, u32[]{:S(2)}) collective-permute-start(bf16[2,2,2,2,24,768]{5,4,3,2,1,0:T(8,128)(2,1)S(1)} %dynamic-slice_bitcast_fusion.2), channel_id=1, source_target_pairs={{0,8},{4,12},{8,0},{12,4},{16,24},{20,28},{24,16},{28,20},{1,9},{5... | collective-permute-start | bytes 1769480 | tf_op jit(solution)/shard_map/ppermute | solution.py:30
  492.9 27.4 %collective-permute-start.43 = (bf16[2,2,2,2,24,768]{5,4,3,2,1,0:T(8,128)(2,1)S(1)}, bf16[2,2,2,2,24,768]{5,4,3,2,1,0:T(8,128)(2,1)S(1)}, u32[]{:S(2)}, u32[]{:S(2)}) collective-permute-start(bf16[2,2,2,2,24,768]{5,4,3,2,1,0:T(8,128)(2,1)S(1)} %dynamic-slice_bitcast_fusion.1), channel_id=1, source_target_pairs={{0,4},{4,0},{8,12},{12,8},{16,20},{20,16},{24,28},{28,24},{1,5},{5... | collective-permute-start | bytes 1769480 | tf_op jit(solution)/shard_map/ppermute | solution.py:30
  494.7 26.1 %collective-permute-start.48 = (bf16[2,2,2,2,24,768]{5,4,3,2,1,0:T(8,128)(2,1)S(1)}, bf16[2,2,2,2,24,768]{5,4,3,2,1,0:T(8,128)(2,1)S(1)}, u32[]{:S(2)}, u32[]{:S(2)}) collective-permute-start(bf16[2,2,2,2,24,768]{5,4,3,2,1,0:T(8,128)(2,1)S(1)} %dynamic-slice_bitcast_fusion), channel_id=1, source_target_pairs={{0,2},{1,3},{2,0},{3,1},{4,6},{5,7},{6,4},{7,5},{8,10},{9,11},{10,... | collective-permute-start | bytes 1769480 | tf_op jit(solution)/shard_map/ppermute | solution.py:30
  518.5 16.1 %collective-permute-start.39 = (bf16[2,2,2,24,768]{4,3,2,1,0:T(8,128)(2,1)S(1)}, bf16[2,2,2,24,768]{4,3,2,1,0:T(8,128)(2,1)S(1)}, u32[]{:S(2)}, u32[]{:S(2)}) collective-permute-start(bf16[2,2,2,24,768]{4,3,2,1,0:T(8,128)(2,1)S(1)} %dynamic-slice_bitcast_fusion.5), channel_id=1, source_target_pairs={{0,16},{4,20},{8,24},{12,28},{16,0},{20,4},{24,8},{28,12},{1,17},{... | collective-permute-start | bytes 884744 | tf_op jit(solution)/shard_map/ppermute | solution.py:30
  520.4 15.8 %collective-permute-start.44 = (bf16[2,2,2,24,768]{4,3,2,1,0:T(8,128)(2,1)S(1)}, bf16[2,2,2,24,768]{4,3,2,1,0:T(8,128)(2,1)S(1)}, u32[]{:S(2)}, u32[]{:S(2)}) collective-permute-start(bf16[2,2,2,24,768]{4,3,2,1,0:T(8,128)(2,1)S(1)} %dynamic-slice_bitcast_fusion.4), channel_id=1, source_target_pairs={{0,2},{1,3},{2,0},{3,1},{4,6},{5,7},{6,4},{7,5},{8,10},{9,11},{10,... | collective-permute-start | bytes 884744 | tf_op jit(solution)/shard_map/ppermute | solution.py:30
  521.0 15.3 %collective-permute-start.49 = (bf16[2,2,2,24,768]{4,3,2,1,0:T(8,128)(2,1)S(1)}, bf16[2,2,2,24,768]{4,3,2,1,0:T(8,128)(2,1)S(1)}, u32[]{:S(2)}, u32[]{:S(2)}) collective-permute-start(bf16[2,2,2,24,768]{4,3,2,1,0:T(8,128)(2,1)S(1)} %dynamic-slice_bitcast_fusion.3), channel_id=1, source_target_pairs={{0,4},{4,0},{8,12},{12,8},{16,20},{20,16},{24,28},{28,24},{1,5},{5... | collective-permute-start | bytes 884744 | tf_op jit(solution)/shard_map/ppermute | solution.py:30
  536.3 12.4 %collective-permute-start.45 = (bf16[2,2,24,768]{3,2,0,1:T(8,128)(2,1)S(1)}, bf16[2,2,24,768]{3,2,0,1:T(8,128)(2,1)S(1)}, u32[]{:S(2)}, u32[]{:S(2)}) collective-permute-start(bf16[2,2,24,768]{3,2,0,1:T(8,128)(2,1)S(1)} %bitcast.465), channel_id=1, source_target_pairs={{0,8},{4,12},{8,0},{12,4},{16,24},{20,28},{24,16},{28,20},{1,9},{5... | collective-permute-start | bytes 442376 | tf_op jit(solution)/shard_map/ppermute | solution.py:30
  536.4 18.7 %collective-permute-start.50 = (bf16[2,2,24,768]{3,2,0,1:T(8,128)(2,1)S(1)}, bf16[2,2,24,768]{3,2,0,1:T(8,128)(2,1)S(1)}, u32[]{:S(2)}, u32[]{:S(2)}) collective-permute-start(bf16[2,2,24,768]{3,2,0,1:T(8,128)(2,1)S(1)} %bitcast.466), channel_id=1, source_target_pairs={{0,8},{4,12},{8,0},{12,4},{16,24},{20,28},{24,16},{28,20},{1,9},{5... | collective-permute-start | bytes 442376 | tf_op jit(solution)/shard_map/ppermute | solution.py:30
  540.5 14.8 %collective-permute-start.41 = (bf16[2,24,768]{2,1,0:T(8,128)(2,1)S(1)}, bf16[2,24,768]{2,1,0:T(8,128)(2,1)S(1)}, u32[]{:S(2)}, u32[]{:S(2)}) collective-permute-start(bf16[2,24,768]{2,1,0:T(8,128)(2,1)S(1)} %dynamic-slice_bitcast_fusion.8), channel_id=1, source_target_pairs={{0,2},{1,3},{2,0},{3,1},{4,6},{5,7},{6,4},{7,5},{8,10},{9,11},{10,... | collective-permute-start | bytes 221192 | tf_op jit(solution)/shard_map/ppermute | solution.py:30
  548.6 12.2 %collective-permute-start.46 = (bf16[2,24,768]{2,1,0:T(8,128)(2,1)S(1)}, bf16[2,24,768]{2,1,0:T(8,128)(2,1)S(1)}, u32[]{:S(2)}, u32[]{:S(2)}) collective-permute-start(bf16[2,24,768]{2,1,0:T(8,128)(2,1)S(1)} %dynamic-slice_bitcast_fusion.7), channel_id=1, source_target_pairs={{0,16},{4,20},{8,24},{12,28},{16,0},{20,4},{24,8},{28,12},{1,17},{... | collective-permute-start | bytes 221192 | tf_op jit(solution)/shard_map/ppermute | solution.py:30
  555.2 9.3 %collective-permute-start.51 = (bf16[2,24,768]{2,1,0:T(8,128)(2,1)S(1)}, bf16[2,24,768]{2,1,0:T(8,128)(2,1)S(1)}, u32[]{:S(2)}, u32[]{:S(2)}) collective-permute-start(bf16[2,24,768]{2,1,0:T(8,128)(2,1)S(1)} %dynamic-slice_bitcast_fusion.6), channel_id=1, source_target_pairs={{0,16},{4,20},{8,24},{12,28},{16,0},{20,4},{24,8},{28,12},{1,17},{... | collective-permute-start | bytes 221192 | tf_op jit(solution)/shard_map/ppermute | solution.py:30
  (139 other events, 897.6 us)
Sparse Core Ops, SparseCore 0:
  11.5 137.9 all-gather.2
  152.4 94.9 all-gather.4
  275.3 138.6 reduce-scatter.4
  420.0 165.8 reduce-scatter.2

commit v4 on v3

--- a/solution.py
+++ b/solution.py
@@ -39,18 +39,28 @@
     return (lax.axis_index(axis) & bit) != 0
 
 
-def sum_all(array, axes):
-    for axis in axes:
-        for bit in bits_of(axis):
-            array = array + flip(array, axis, bit)
-    return array
-
-
-def reduce_blocks(planes, steps):
+share_unit = 8192.0
+
+
+def digits_of(number, length):
+    places = 2 * jnp.arange(length, dtype=jnp.int32)
+    return ((number >> places) & 3).astype(jnp.float32)
+
+
+def number_of(digits):
+    return jnp.sum(digits * 4.0 ** jnp.arange(digits.shape[0], dtype=jnp.float32))
+
+
+def split_rows(planes):
     count, rows, width = planes.shape
     dims = [("dp", bit) for bit in reversed(bits_of("dp"))]
     dims += [("seq", bit) for bit in reversed(bits_of("seq"))]
     blocks = planes.reshape((count,) + (2,) * len(dims) + (rows >> len(dims), width))
+    return blocks, dims
+
+
+def halve(blocks, dims, steps):
+    dims = list(dims)
     for step in steps:
         axis, bit = step
         dim = 1 + dims.index(step)
@@ -59,7 +69,7 @@
         send = lax.dynamic_index_in_dim(blocks, 1 - mine, dim, False)
         blocks = keep + flip(send, axis, bit)
         dims.remove(step)
-    return blocks
+    return blocks, dims
 
 
 def step_orders():
@@ -98,9 +108,9 @@
 
 
 def pack_kernel(*refs):
-    w_query, w_key, w_value, w_output, w_inner, w_outer = refs[:6]
-    outs = refs[6:]
-    layers, rows, width = w_query.shape
+    w_key, w_value, w_output, w_inner, w_outer = refs[:5]
+    outs = refs[5:]
+    layers, rows, width = w_key.shape
     parts = w_inner.shape[2] // width
     lane = width // 6
     span = lane * parts
@@ -108,8 +118,9 @@
     for k in range(layers):
         out = outs[k]
         at = 0
-        out[:, at : at + width] = w_output[k]
-        at = width
+        if k > 0:
+            out[:, :width] = w_output[k]
+            at = width
         for w in range(6):
             moved = plain(w_inner[k, :, w * span : (w + 1) * span], order).astype(jnp.bfloat16)
             for c in range(parts):
@@ -121,21 +132,21 @@
             out[:, at : at + width] = plain(take, w_outer[k]).astype(jnp.bfloat16)
             at = at + width
         if k + 1 < layers:
-            for square in (w_query, w_key, w_value):
+            for square in (w_key, w_value):
                 out[:, at : at + width] = square[k + 1]
                 at = at + width
 
 
 def pack(*weights):
     layers, rows, width = weights[0].shape
-    parts = weights[4].shape[2] // width
-    count = 1 + 2 * parts
+    parts = weights[3].shape[2] // width
     return pl.pallas_call(
         pack_kernel,
         name="pack",
         out_shape=tuple(
             jax.ShapeDtypeStruct(
-                (rows, (count + (3 if k + 1 < layers else 0)) * width), jnp.bfloat16
+                (rows, (2 * parts + min(k, 1) + (2 if k + 1 < layers else 0)) * width),
+                jnp.bfloat16,
             )
             for k in range(layers)
         ),
@@ -577,19 +588,22 @@
         [gain_attend, shift_attend, gain_mixer, shift_mixer, bias_outer, bias_inner], axis=1
     )
     per = width // devices
-    lots = pack(weight_query, weight_key, weight_value, weight_output, weight_inner, weight_outer)
+    lots = pack(weight_key, weight_value, weight_output, weight_inner, weight_outer)
     whole = [lax.all_gather(lot, both, axis=0, tiled=True) for lot in lots]
     orders = step_orders()
+    gather_orders = (tuple(reversed(orders[2])), tuple(reversed(orders[1])))
     line = jnp.pad(vectors.reshape(1, -1), ((0, 7), (0, width - vectors.size)))
     first_lot = gather_blocks(
-        jnp.concatenate([weight_query[0], line]), tuple(reversed(orders[1]))
+        jnp.concatenate([weight_query[0], weight_output[0], line]), gather_orders[1]
     )
     pair_lot = gather_blocks(
-        jnp.concatenate([weight_key[0], weight_value[0]], axis=1), tuple(reversed(orders[0]))
-    )
-    vector_rows = first_lot[:, per, : vectors.size]
+        jnp.concatenate([weight_key[0], weight_value[0]] + list(weight_query[1:]), axis=1),
+        gather_orders[0],
+    )
+    vector_rows = first_lot[:, 2 * per, : vectors.size]
     first_query = first_lot[:, :per].reshape(width, width)
-    first_pair = pair_lot.reshape(width, 2 * width)
+    first_output = first_lot[:, per : 2 * per].reshape(width, width)
+    first_pair = pair_lot.reshape(width, -1)
     vector_rows = vector_rows.reshape(devices, layers, -1)
     small = [
         vector_rows[:, :, k * per : (k + 1) * per].transpose(1, 0, 2).reshape(layers, width)
@@ -600,22 +614,28 @@
     def square_of(matrix, k):
         return matrix[:, k * width : (k + 1) * width]
 
-    last = 1 + 2 * parts
-
     def square_at(layer, k):
-        if k >= 3:
-            return square_of(whole[layer], k - 3)
         if layer == 0:
-            return first_query if k == 0 else square_of(first_pair, k - 1)
-        return square_of(whole[layer - 1], last + k)
+            if k == 0:
+                return first_query
+            if k < 3:
+                return square_of(first_pair, k - 1)
+            return first_output if k == 3 else square_of(whole[0], k - 4)
+        if k == 0:
+            return square_of(first_pair, 1 + layer)
+        if k < 3:
+            return square_of(whole[layer - 1], 2 * parts + min(layer - 1, 1) + k - 1)
+        return square_of(whole[layer], k - 3)
 
     def pair_at(layer):
         if layer == 0:
-            return first_pair
-        return whole[layer - 1][:, (last + 1) * width : (last + 3) * width]
+            return first_pair[:, : 2 * width]
+        at = (2 * parts + min(layer - 1, 1)) * width
+        return whole[layer - 1][:, at : at + 2 * width]
 
     def inner_at(layer):
-        return whole[layer][:, width : (1 + parts) * width]
+        at = min(layer, 1) * width
+        return whole[layer][:, at : at + parts * width]
 
     small, hidden = lax.optimization_barrier((small, inputs))
     hidden = hidden.astype(jnp.float32)
@@ -734,6 +754,8 @@
         grad_inner = gelu_back(grad_active)[0].astype(jnp.bfloat16)
         grad_b_inner = jnp.sum(grad_inner, axis=0, dtype=jnp.float32)
         grad_w_inner = product(normed_two, grad_inner, "td,tf->df")
+        wide = [piece.astype(jnp.bfloat16) for piece in [grad_w_inner] + grad_w_outer]
+        wide = jnp.concatenate(held[:2] + wide, axis=1)
         grad_normed_two = product(grad_inner, w_inner, "tf,df->td").reshape(after.shape)
         norm_back_two = jax.vjp(
             layer_norm, after, gain_m.astype(jnp.float32), shift_m.astype(jnp.float32)
@@ -741,8 +763,6 @@
         after_part, grad_gain_m, grad_shift_m = norm_back_two(grad_normed_two)
         grad_after = grad_hidden + after_part
         grad_attn = grad_after.astype(jnp.bfloat16).reshape(-1, width)
-        wide = [piece.astype(jnp.bfloat16) for piece in [grad_w_inner] + grad_w_outer]
-        wide = jnp.concatenate(held[:2] + wide, axis=1)
         wide, grad_attn = lax.optimization_barrier((wide, grad_attn))
         wide_sums.append(lax.psum_scatter(wide, both, scatter_dimension=0, tiled=True))
         grad_mixed = product(grad_attn, w_output, "td,cd->tc").astype(jnp.bfloat16)
@@ -801,29 +821,42 @@
                 grad_b_inner,
             ]
         )
-    count = jnp.where(is_last, jnp.sum(lengths).astype(jnp.float32), 0.0)
-    flat = jnp.concatenate(
-        vector_grads + [jnp.broadcast_to(share_sum, (128,)), jnp.broadcast_to(count, (128,))]
-    )
-    flat = sum_all(flat.reshape(-1, 128), ("seq", "dp")).reshape(-1)
-    size = (5 + parts) * width
-    selected = flat[layers * size] / (layers * flat[layers * size + 128])
-    place_of = lax.axis_index("dp") * seq_count + place
-    vec = flat[: layers * size].reshape(layers, size)
+    count = jnp.where(is_last, jnp.sum(lengths), 0)
+    fixed = jnp.round(share_sum * share_unit).astype(jnp.int32)
+    digits = jnp.concatenate([digits_of(fixed, 12), digits_of(count, 6)])
+    vec = jnp.stack(vector_grads)
     bias_grads = vec[:, 5 * width :].reshape(layers, parts, width).transpose(0, 2, 1)
-    vec = jnp.concatenate([vec[:, : 5 * width], bias_grads.reshape(layers, -1)], axis=1)
+    vec = jnp.concatenate(
+        [vec[:, : 5 * width].reshape(layers, 5, devices, per).transpose(2, 0, 1, 3).reshape(
+            devices, layers, 5 * per
+        ), bias_grads.reshape(layers, devices, parts * per).transpose(1, 0, 2)],
+        axis=2,
+    ).reshape(devices, 1, -1)
+    vec = jnp.concatenate([vec, jnp.broadcast_to(digits, (devices, 1, 18))], axis=2)
+    vec = jnp.pad(
+        vec.astype(jnp.bfloat16), ((0, 0), (0, per - 1), (0, width - vec.shape[2]))
+    ).reshape(width, width)
+    lots = (
+        [squares[3], kept[3]],
+        [squares[2], kept[2]],
+        [squares[0], squares[1], vec],
+    )
+    halves = []
+    for lot, order in zip(lots, orders):
+        blocks, dims = split_rows(jnp.stack(lot))
+        halves.append(halve(blocks, dims, order[:2]))
+    one, two, three = (
+        halve(blocks, dims, order[2:])[0] for (blocks, dims), order in zip(halves, orders)
+    )
+    row = three[2, 0].astype(jnp.float32)
+    size = layers * (5 + parts) * per
+    mine_all = row[:size].reshape(layers, -1)
+    share_all = number_of(row[size : size + 12]) / share_unit
+    selected = share_all / (layers * number_of(row[size + 12 : size + 18]))
 
     def mine(first, length):
-        return lax.dynamic_slice_in_dim(
-            vec[:, first * width : first * width + length], place_of * (length // devices),
-            length // devices, axis=1,
-        )
-
-    rows = width // devices
-
-    one = reduce_blocks(jnp.stack([squares[3], kept[3]]), orders[0])
-    two = reduce_blocks(jnp.stack([squares[2], kept[2]]), orders[1])
-    three = reduce_blocks(jnp.stack(squares[:2]), orders[2])
+        return mine_all[:, first * per : first * per + length // devices]
+
     square_sums = finish(wide_sums[1], wide_sums[0], one, two, three, width, parts)
     return (
         hidden,

time: 606 us -> 586 us (0.967)
  waiting for transfers between devices: 269 us -> 236 us
  starting transfers between devices: 44.8 us -> 57.8 us
    all_gather x2, waiting for transfers between devices: 20.7 us -> 0.02 us  [local(): whole = [lax.all_gather(lot, both, axis=0, tiled=True) for lot in lots]]
    ppermute x52 -> x47, starting transfers between devices: 44.6 us -> 57.6 us  [flip(): return lax.ppermute(array, axis, [(i, i ^ bit) for i in range(size)])]
    unnamed x252 -> x260, local copies, waits for them, and re-layouts: 12.3 us -> 21.5 us
    ppermute x52 -> x47, waiting for transfers between devices: 227 us -> 218 us  [flip(): return lax.ppermute(array, axis, [(i, i ^ bit) for i in range(size)])]
  transfers between devices with their start and end apart: 56 -> 51, of which waited for: 32 -> 28; matrix products, arithmetic and copies ran while one was open for 25% -> 25% of each run, Pallas kernels for 12% -> 12%
where the time goes in v4:
time: 586 us; the launch traced here: 577 us
  waiting for transfers between devices  236 us (40%)
  matrix products  86.7 us (15%)
  Pallas kernels  78.5 us (13%)
  starting transfers between devices  57.8 us (10%)
  other arithmetic  50.9 us (9%)
  local copies, waits for them, and re-layouts  46.8 us (8%)
  between operations  20.8 us (4%)
    ppermute x47, waiting for transfers between devices, flip(): return lax.ppermute(array, axis, [(i, i ^ bit) for i in range(size)])  218 us
    ppermute x47, starting transfers between devices, flip(): return lax.ppermute(array, axis, [(i, i ^ bit) for i in range(size)])  57.6 us
    dot_general x36, matrix products, product(): return jnp.einsum(form, left, right, preferred_element_type=jnp.float32)  55.4 us
    pallas_call x2, Pallas kernels, back(): pl.pallas_call(back_kernel, name='back', out_shape=(jax.ShapeDtypeStruct(...  32.9 us
    pallas_call x2, Pallas kernels, mix(): pl.pallas_call(mix_kernel, name='mix', out_shape=(jax.ShapeDtypeStruct((r...  22 us
    unnamed x260, local copies, waits for them, and re-layouts  21.5 us
    reduce_scatter x2, waiting for transfers between devices, local(): lax.psum_scatter(wide, both, scatter_dimension=0, tiled=True)  16.5 us
  transfers between devices with their start and end apart: 51, of which 28 were waited for; matrix products, arithmetic and copies ran while one was open for 25% of the time, Pallas kernels for 12%

profile of v4, /device:TPU:0, one launch (start us, length us, event | category | flops | bytes accessed | tf_op | source)
XLA Modules:
  0.0 577.0 jit_solution(6655468554660398927)
XLA Ops:
  13.8 4.1 collective-permute-start
  18.9 3.9 collective-permute-done
  22.9 4.7 collective-permute-start.1
  33.1 5.3 collective-permute-done.1
  44.9 6.3 %collective-permute-done.2 = bf16[2,2,56,768]{3,2,0,1:T(8,128)(2,1)S(1)} collective-permute-done((bf16[2,2,56,768]{3,2,0,1:T(8,128)(2,1)S(1)}, bf16[2,2,56,768]{3,2,0,1:T(8,128)(2,1)S(1)}, u32[]{:S(2)}, u32[]{:S(2)}) %collective-permute-start.2) | collective-permute-done | bytes 344096 | tf_op jit(solution)/shard_map/ppermute | solution.py:30
  52.9 8.7 %collective-permute-done.7 = bf16[2,2,24,2304]{3,2,0,1:T(8,128)(2,1)S(1)} collective-permute-done((bf16[2,2,24,2304]{3,2,0,1:T(8,128)(2,1)S(1)}, bf16[2,2,24,2304]{3,2,0,1:T(8,128)(2,1)S(1)}, u32[]{:S(2)}, u32[]{:S(2)}) %collective-permute-start.7) | collective-permute-done | bytes 442400 | tf_op jit(solution)/shard_map/ppermute | solution.py:30
  63.4 12.1 %collective-permute-done.3 = bf16[2,2,2,56,768]{4,3,0,1,2:T(8,128)(2,1)S(1)} collective-permute-done((bf16[2,2,2,56,768]{4,3,0,1,2:T(8,128)(2,1)S(1)}, bf16[2,2,2,56,768]{4,3,0,1,2:T(8,128)(2,1)S(1)}, u32[]{:S(2)}, u32[]{:S(2)}) %collective-permute-start.3) | collective-permute-done | bytes 688160 | tf_op jit(solution)/shard_map/ppermute | solution.py:30
  76.8 13.8 %collective-permute-done.8 = bf16[2,2,2,24,2304]{4,3,0,1,2:T(8,128)(2,1)} collective-permute-done((bf16[2,2,2,24,2304]{4,3,0,1,2:T(8,128)(2,1)S(1)}, bf16[2,2,2,24,2304]{4,3,0,1,2:T(8,128)(2,1)}, u32[]{:S(2)}, u32[]{:S(2)}) %collective-permute-start.8) | collective-permute-done | bytes 884768 | tf_op jit(solution)/shard_map/ppermute | solution.py:30
  108.2 15.5 %collective-permute-done.11.refs_2_.refs_6_ = bf16[256,1536]{1,0:T(8,128)(2,1)S(1)} collective-permute-done((bf16[256,1536]{1,0:T(8,128)(2,1)S(1)}, bf16[256,1536]{1,0:T(8,128)(2,1)S(1)}, u32[]{:S(2)}, u32[]{:S(2)}) %collective-permute-start.11) | collective-permute-done | bytes 786464 | tf_op jit(solution)/shard_map/ppermute | solution.py:30
  127.4 3.8 pick.2
  138.7 10.9 %mix.2 = (bf16[256,768]{1,0:T(8,128)(2,1)}, f32[256,768]{1,0:T(8,128)}) custom-call(s32[2]{0:T(128)} %pad_add_fusion.scalars, bf16[256,768]{1,0:T(8,128)(2,1)} %convolution_convert_fusion.23.q_ref, f32[256,1024]{1,0:T(8,128)} %get-tuple-element.74.carried_ref, f32[1,1024]{1,0:T(1,128)} %fusion.160.before_ref, bf16[256,1536]{1,0:T(8,128)(2,1)} %copy-done, ...), custom_call_target="tpu_custom_call" | custom-call | tf_op jit(solution)/shard_map/mix/pallas_call | solution.py:443
  151.5 6.3 %multiply_convert_fusion.1 = (bf16[256,3072]{1,0:T(8,128)(2,1)S(1)}, f32[256,3072]{1,0:T(8,128)}) fusion(f32[3072]{0:T(1024)S(1)} %bitcast.509, bf16[768,7680]{1,0:T(8,128)(2,1)} %all-gather.3.cloned.1.call-done, f32[1,256,768]{2,1,0:T(8,128)S(1)} %get-tuple-element.241, f32[768]{0:T(1024)S(1)} %get-tuple-element.140, f32[768]{0:T(1024)S(1)} %get-tuple-element.253, ...), kind=kOutput, calls=%fused_computation.39 | convolution fusion | flops 1216806912 | bytes 10244096 | tf_op jit(solution)/shard_map/dot_general | solution.py:684
  163.7 25.1 %collective-permute-done.16.refs_2_.refs_6_ = bf16[256,1536]{1,0:T(8,128)(2,1)S(1)} collective-permute-done((bf16[256,1536]{1,0:T(8,128)(2,1)S(1)}, bf16[256,1536]{1,0:T(8,128)(2,1)S(1)}, u32[]{:S(2)}, u32[]{:S(2)}) %collective-permute-start.16) | collective-permute-done | bytes 786464 | tf_op jit(solution)/shard_map/ppermute | solution.py:30
  205.8 11.1 %mix.3 = (bf16[256,768]{1,0:T(8,128)(2,1)}, f32[256,768]{1,0:T(8,128)}) custom-call(s32[2]{0:T(128)} %pad_add_fusion.scalars, bf16[256,768]{1,0:T(8,128)(2,1)} %convolution_convert_fusion.22.q_ref, f32[256,1024]{1,0:T(8,128)} %get-tuple-element.82.carried_ref, f32[1,1024]{1,0:T(1,128)} %get-tuple-element.206.before_ref, bf16[256,1536]{1,0:T(8,128)(2,1)} %copy-done.4, ...), custom_call_target="tpu_custom_call" | custom-call | tf_op jit(solution)/shard_map/mix/pallas_call | solution.py:443
  226.4 4.1 convert_reduce_fusion
  248.2 16.3 %back.2 = (bf16[256,768]{1,0:T(8,128)(2,1)}, bf16[4,256,768]{2,1,0:T(8,128)(2,1)}, bf16[4,256,768]{2,1,0:T(8,128)(2,1)}, f32[256,1024]{1,0:T(8,128)}, f32[256,1024]{1,0:T(8,128)}, /*index=5*/f32[1,1024]{1,0:T(1,128)}) custom-call(s32[2]{0:T(128)} %pad_add_fusion.scalars, bf16[256,768]{1,0:T(8,128)(2,1)} %convolution_convert_fusion.22.q_ref, ...), custom_call_target="tpu_custom_call" | custom-call | tf_op jit(solution)/shard_map/back/pallas_call | solution.py:473
  274.9 9.1 %collective-permute-done.23 = bf16[1,256,768]{2,1,0:T(8,128)(2,1)} collective-permute-done((bf16[1,256,768]{2,1,0:T(8,128)(2,1)S(1)}, bf16[1,256,768]{2,1,0:T(8,128)(2,1)}, u32[]{:S(2)}, u32[]{:S(2)}) %collective-permute-start.23) | collective-permute-done | bytes 393248 | tf_op jit(solution)/shard_map/ppermute | solution.py:30
  286.4 4.7 first.2
  301.9 16.3 %collective-permute-done.25 = bf16[1,256,768]{2,1,0:T(8,128)(2,1)S(1)} collective-permute-done((bf16[1,256,768]{2,1,0:T(8,128)(2,1)S(1)}, bf16[1,256,768]{2,1,0:T(8,128)(2,1)S(1)}, u32[]{:S(2)}, u32[]{:S(2)}) %collective-permute-start.25) | collective-permute-done | bytes 393248 | tf_op jit(solution)/shard_map/ppermute | solution.py:30
  350.8 16.5 %back.3 = (bf16[256,768]{1,0:T(8,128)(2,1)}, bf16[4,256,768]{2,1,0:T(8,128)(2,1)}, bf16[4,256,768]{2,1,0:T(8,128)(2,1)}, f32[256,1024]{1,0:T(8,128)}, f32[256,1024]{1,0:T(8,128)}, /*index=5*/f32[1,1024]{1,0:T(1,128)}) custom-call(s32[2]{0:T(128)} %pad_add_fusion.scalars, bf16[256,768]{1,0:T(8,128)(2,1)} %convolution_convert_fusion.23.q_ref, ...), custom_call_target="tpu_custom_call" | custom-call | tf_op jit(solution)/shard_map/back/pallas_call | solution.py:473
  380.4 8.1 %collective-permute-done.29 = bf16[1,256,768]{2,1,0:T(8,128)(2,1)S(1)} collective-permute-done((bf16[1,256,768]{2,1,0:T(8,128)(2,1)S(1)}, bf16[1,256,768]{2,1,0:T(8,128)(2,1)S(1)}, u32[]{:S(2)}, u32[]{:S(2)}) %collective-permute-start.29) | collective-permute-done | bytes 393248 | tf_op jit(solution)/shard_map/ppermute | solution.py:30
  389.9 4.5 first.3
  441.2 28.5 %collective-permute-done.38 = bf16[2,2,2,2,24,768]{5,4,3,2,1,0:T(8,128)(2,1)S(1)} collective-permute-done((bf16[2,2,2,2,24,768]{5,4,3,2,1,0:T(8,128)(2,1)S(1)}, bf16[2,2,2,2,24,768]{5,4,3,2,1,0:T(8,128)(2,1)S(1)}, u32[]{:S(2)}, u32[]{:S(2)}) %collective-permute-start.38) | collective-permute-done | bytes 589856 | tf_op jit(solution)/shard_map/ppermute | solution.py:30
  469.8 4.7 collective-permute-start.39
  478.2 18.9 %collective-permute-done.39 = bf16[2,2,2,24,768]{4,3,2,1,0:T(8,128)(2,1)S(1)} collective-permute-done((bf16[2,2,2,24,768]{4,3,2,1,0:T(8,128)(2,1)S(1)}, bf16[2,2,2,24,768]{4,3,2,1,0:T(8,128)(2,1)S(1)}, u32[]{:S(2)}, u32[]{:S(2)}) %collective-permute-start.39) | collective-permute-done | bytes 294944 | tf_op jit(solution)/shard_map/ppermute | solution.py:30
  499.6 6.1 %collective-permute-done.40 = bf16[2,2,24,768]{3,2,0,1:T(8,128)(2,1)S(1)} collective-permute-done((bf16[2,2,24,768]{3,2,0,1:T(8,128)(2,1)S(1)}, bf16[2,2,24,768]{3,2,0,1:T(8,128)(2,1)S(1)}, u32[]{:S(2)}, u32[]{:S(2)}) %collective-permute-start.40) | collective-permute-done | bytes 147488 | tf_op jit(solution)/shard_map/ppermute | solution.py:30
  505.6 4.9 collective-permute-done.33
  514.6 6.6 %collective-permute-done.34 = bf16[3,2,2,24,768]{4,3,2,1,0:T(8,128)(2,1)S(1)} collective-permute-done((bf16[3,2,2,24,768]{4,3,2,1,0:T(8,128)(2,1)S(1)}, bf16[3,2,2,24,768]{4,3,2,1,0:T(8,128)(2,1)S(1)}, u32[]{:S(2)}, u32[]{:S(2)}) %collective-permute-start.34) | collective-permute-done | bytes 442400 | tf_op jit(solution)/shard_map/ppermute | solution.py:30
  521.4 5.1 collective-permute-start.35
  527.1 7.6 %collective-permute-done.35 = bf16[3,2,24,768]{3,2,0,1:T(8,128)(2,1)S(1)} collective-permute-done((bf16[3,2,24,768]{3,2,0,1:T(8,128)(2,1)S(1)}, bf16[3,2,24,768]{3,2,0,1:T(8,128)(2,1)S(1)}, u32[]{:S(2)}, u32[]{:S(2)}) %collective-permute-start.35) | collective-permute-done | bytes 221216 | tf_op jit(solution)/shard_map/ppermute | solution.py:30
  535.5 9.0 %collective-permute-done.36 = bf16[3,24,768]{2,1,0:T(8,128)(2,1)S(1)} collective-permute-done((bf16[3,24,768]{2,1,0:T(8,128)(2,1)S(1)}, bf16[3,24,768]{2,1,0:T(8,128)(2,1)S(1)}, u32[]{:S(2)}, u32[]{:S(2)}) %collective-permute-start.36) | collective-permute-done | bytes 110624 | tf_op jit(solution)/shard_map/ppermute | solution.py:30
  548.6 16.5 %reduce-scatter.3.cloned.1.call-done.late_ref = bf16[24,7680]{1,0:T(8,128)(2,1)} async-done(((bf16[768,7680]{1,0:T(8,128)(2,1)}), bf16[24,7680]{1,0:T(8,128)(2,1)}) %reduce-scatter.3.cloned.1.call-update) | async-done | bytes 368656 | tf_op jit(solution)/shard_map/reduce_scatter | solution.py:767
  (595 shorter events, 236.9 us)
Async XLA Ops:
  7.2 144.3 %all-gather.3.cloned.1.call-start = ((), (), s32[]{:S(2)}) async-start(), calls=%async_computation.2 | async-start | bytes 12165120 | tf_op jit(solution)/shard_map/all_gather | solution.py:592
  10.5 207.0 %all-gather.5.cloned.1.call-start = ((), (), s32[]{:S(2)}) async-start(), calls=%async_computation.3 | async-start | bytes 10948608 | tf_op jit(solution)/shard_map/all_gather | solution.py:592
  11.3 537.3 %reduce-scatter.5.cloned.1.call-start = ((), (), s32[]{:S(2)}) async-start(), calls=%async_computation.5 | async-start | bytes 9732096 | tf_op jit(solution)/shard_map/reduce_scatter | solution.py:767
  18.8 11.1 %collective-permute-start.5 = (bf16[24,2304]{1,0:T(8,128)(2,1)S(1)}, bf16[24,2304]{1,0:T(8,128)(2,1)S(1)}, u32[]{:S(2)}, u32[]{:S(2)}) collective-permute-start(bf16[24,2304]{1,0:T(8,128)(2,1)S(1)} %pad_maximum_fusion.13), channel_id=1, source_target_pairs={{0,16},{4,20},{8,24},{12,28},{16,0},{20,4},{24,8},{28,12},{1,17},{... | collective-permute-start | bytes 331784 | tf_op jit(solution)/shard_map/ppermute | solution.py:30
  22.9 15.6 %collective-permute-start.1 = (bf16[2,56,768]{2,1,0:T(8,128)(2,1)S(1)}, bf16[2,56,768]{2,1,0:T(8,128)(2,1)S(1)}, u32[]{:S(2)}, u32[]{:S(2)}) collective-permute-start(bf16[2,56,768]{2,1,0:T(8,128)(2,1)S(1)} %pad_maximum_fusion.12), channel_id=1, source_target_pairs={{0,8},{4,12},{8,0},{12,4},{16,24},{20,28},{24,16},{28,20},{1,9},{5... | collective-permute-start | bytes 516104 | tf_op jit(solution)/shard_map/ppermute | solution.py:30
  30.0 13.1 %collective-permute-start.6 = (bf16[2,24,2304]{2,1,0:T(8,128)(2,1)S(1)}, bf16[2,24,2304]{2,1,0:T(8,128)(2,1)S(1)}, u32[]{:S(2)}, u32[]{:S(2)}) collective-permute-start(bf16[2,24,2304]{2,1,0:T(8,128)(2,1)S(1)} %pad_maximum_fusion.11), channel_id=1, source_target_pairs={{0,8},{4,12},{8,0},{12,4},{16,24},{20,28},{24,16},{28,20},{1,9},{5... | collective-permute-start | bytes 663560 | tf_op jit(solution)/shard_map/ppermute | solution.py:30
  38.5 12.6 %collective-permute-start.2 = (bf16[2,2,56,768]{3,2,0,1:T(8,128)(2,1)S(1)}, bf16[2,2,56,768]{3,2,0,1:T(8,128)(2,1)S(1)}, u32[]{:S(2)}, u32[]{:S(2)}) collective-permute-start(bf16[2,2,56,768]{3,2,0,1:T(8,128)(2,1)S(1)} %pad_maximum_fusion.10), channel_id=1, source_target_pairs={{0,2},{1,3},{2,0},{3,1},{4,6},{5,7},{6,4},{7,5},{8,10},{9,11},{10,... | collective-permute-start | bytes 1032200 | tf_op jit(solution)/shard_map/ppermute | solution.py:30
  43.2 18.4 %collective-permute-start.7 = (bf16[2,2,24,2304]{3,2,0,1:T(8,128)(2,1)S(1)}, bf16[2,2,24,2304]{3,2,0,1:T(8,128)(2,1)S(1)}, u32[]{:S(2)}, u32[]{:S(2)}) collective-permute-start(bf16[2,2,24,2304]{3,2,0,1:T(8,128)(2,1)S(1)} %pad_maximum_fusion.9), channel_id=1, source_target_pairs={{0,4},{4,0},{8,12},{12,8},{16,20},{20,16},{24,28},{28,24},{1,5},{5... | collective-permute-start | bytes 1327112 | tf_op jit(solution)/shard_map/ppermute | solution.py:30
  51.3 24.2 %collective-permute-start.3 = (bf16[2,2,2,56,768]{4,3,0,1,2:T(8,128)(2,1)S(1)}, bf16[2,2,2,56,768]{4,3,0,1,2:T(8,128)(2,1)S(1)}, u32[]{:S(2)}, u32[]{:S(2)}) collective-permute-start(bf16[2,2,2,56,768]{4,3,0,1,2:T(8,128)(2,1)S(1)} %pad_maximum_fusion.8), channel_id=1, source_target_pairs={{0,4},{4,0},{8,12},{12,8},{16,20},{20,16},{24,28},{28,24},{1,5},{5... | collective-permute-start | bytes 2064392 | tf_op jit(solution)/shard_map/ppermute | solution.py:30
  61.8 28.9 %collective-permute-start.8 = (bf16[2,2,2,24,2304]{4,3,0,1,2:T(8,128)(2,1)S(1)}, bf16[2,2,2,24,2304]{4,3,0,1,2:T(8,128)(2,1)}, u32[]{:S(2)}, u32[]{:S(2)}) collective-permute-start(bf16[2,2,2,24,2304]{4,3,0,1,2:T(8,128)(2,1)S(1)} %pad_maximum_fusion.7), channel_id=1, source_target_pairs={{0,2},{1,3},{2,0},{3,1},{4,6},{5,7},{6,4},{7,5},{8,10},{9,11},{10,... | collective-permute-start | bytes 2654216 | tf_op jit(solution)/shard_map/ppermute | solution.py:30
  76.8 16.7 %collective-permute-start.4 = (bf16[2,2,2,2,56,768]{5,4,1,0,2,3:T(8,128)(2,1)}, bf16[2,2,2,2,56,768]{5,4,1,0,2,3:T(8,128)(2,1)}, u32[]{:S(2)}, u32[]{:S(2)}) collective-permute-start(bf16[2,2,2,2,56,768]{5,4,1,0,2,3:T(8,128)(2,1)} %pad_maximum_fusion.6), channel_id=1, source_target_pairs={{0,1},{1,0},{2,3},{3,2},{4,5},{5,4},{6,7},{7,6},{8,9},{9,8},{10,11... | collective-permute-start | bytes 4128776 | tf_op jit(solution)/shard_map/ppermute | solution.py:30
  102.8 20.8 %collective-permute-start.11 = (bf16[256,1536]{1,0:T(8,128)(2,1)S(1)}, bf16[256,1536]{1,0:T(8,128)(2,1)S(1)}, u32[]{:S(2)}, u32[]{:S(2)}) collective-permute-start(bf16[256,1536]{1,0:T(8,128)(2,1)S(1)} %convolution_convert_fusion.3.refs_0_.refs_4_), channel_id=1, source_target_pairs={{0,2},{1,3},{2,0},{3,1},{4,6},{5,7},{6,4},{7,5},{8,10},{9,11},{10,... | collective-permute-start | bytes 2359304 | tf_op jit(solution)/shard_map/ppermute | solution.py:30
  107.9 17.7 %collective-permute-start.10 = (bf16[256,1536]{1,0:T(8,128)(2,1)S(1)}, bf16[256,1536]{1,0:T(8,128)(2,1)S(1)}, u32[]{:S(2)}, u32[]{:S(2)}) collective-permute-start(bf16[256,1536]{1,0:T(8,128)(2,1)S(1)} %convolution_convert_fusion.3.refs_0_.refs_4_), channel_id=1, source_target_pairs={{0,1},{1,0},{2,3},{3,2},{4,5},{5,4},{6,7},{7,6},{8,9},{9,8},{10,11... | collective-permute-start | bytes 2359304 | tf_op jit(solution)/shard_map/ppermute | solution.py:30
  161.9 26.9 %collective-permute-start.16 = (bf16[256,1536]{1,0:T(8,128)(2,1)S(1)}, bf16[256,1536]{1,0:T(8,128)(2,1)S(1)}, u32[]{:S(2)}, u32[]{:S(2)}) collective-permute-start(bf16[256,1536]{1,0:T(8,128)(2,1)S(1)} %convolution_convert_fusion.2.refs_0_.refs_4_), channel_id=1, source_target_pairs={{0,2},{1,3},{2,0},{3,1},{4,6},{5,7},{6,4},{7,5},{8,10},{9,11},{10,... | collective-permute-start | bytes 2359304 | tf_op jit(solution)/shard_map/ppermute | solution.py:30
  163.7 27.9 %collective-permute-start.15 = (bf16[256,1536]{1,0:T(8,128)(2,1)S(1)}, bf16[256,1536]{1,0:T(8,128)(2,1)S(1)}, u32[]{:S(2)}, u32[]{:S(2)}) collective-permute-start(bf16[256,1536]{1,0:T(8,128)(2,1)S(1)} %convolution_convert_fusion.2.refs_0_.refs_4_), channel_id=1, source_target_pairs={{0,1},{1,0},{2,3},{3,2},{4,5},{5,4},{6,7},{7,6},{8,9},{9,8},{10,11... | collective-permute-start | bytes 2359304 | tf_op jit(solution)/shard_map/ppermute | solution.py:30
  244.9 320.2 %reduce-scatter.3.cloned.1.call-start = ((), (), s32[]{:S(2)}) async-start(), calls=%async_computation.4 | async-start | bytes 12165120 | tf_op jit(solution)/shard_map/reduce_scatter | solution.py:767
  272.8 11.3 %collective-permute-start.23 = (bf16[1,256,768]{2,1,0:T(8,128)(2,1)S(1)}, bf16[1,256,768]{2,1,0:T(8,128)(2,1)}, u32[]{:S(2)}, u32[]{:S(2)}) collective-permute-start(bf16[1,256,768]{2,1,0:T(8,128)(2,1)S(1)} %slice_bitcast_fusion.14), channel_id=1, source_target_pairs={{0,2},{1,3},{2,0},{3,1},{4,6},{5,7},{6,4},{7,5},{8,10},{9,11},{10,... | collective-permute-start | bytes 1179656 | tf_op jit(solution)/shard_map/ppermute | solution.py:30
  299.4 18.8 %collective-permute-start.25 = (bf16[1,256,768]{2,1,0:T(8,128)(2,1)S(1)}, bf16[1,256,768]{2,1,0:T(8,128)(2,1)S(1)}, u32[]{:S(2)}, u32[]{:S(2)}) collective-permute-start(bf16[1,256,768]{2,1,0:T(8,128)(2,1)S(1)} %slice_bitcast_fusion.12), channel_id=1, source_target_pairs={{0,2},{1,3},{2,0},{3,1},{4,6},{5,7},{6,4},{7,5},{8,10},{9,11},{10,... | collective-permute-start | bytes 1179656 | tf_op jit(solution)/shard_map/ppermute | solution.py:30
  377.3 11.1 %collective-permute-start.29 = (bf16[1,256,768]{2,1,0:T(8,128)(2,1)S(1)}, bf16[1,256,768]{2,1,0:T(8,128)(2,1)S(1)}, u32[]{:S(2)}, u32[]{:S(2)}) collective-permute-start(bf16[1,256,768]{2,1,0:T(8,128)(2,1)S(1)} %slice_bitcast_fusion.10), channel_id=1, source_target_pairs={{0,2},{1,3},{2,0},{3,1},{4,6},{5,7},{6,4},{7,5},{8,10},{9,11},{10,... | collective-permute-start | bytes 1179656 | tf_op jit(solution)/shard_map/ppermute | solution.py:30
  404.6 11.7 %collective-permute-start.31 = (bf16[1,256,768]{2,1,0:T(8,128)(2,1)}, bf16[1,256,768]{2,1,0:T(8,128)(2,1)}, u32[]{:S(2)}, u32[]{:S(2)}) collective-permute-start(bf16[1,256,768]{2,1,0:T(8,128)(2,1)} %slice_bitcast_fusion.8), channel_id=1, source_target_pairs={{0,2},{1,3},{2,0},{3,1},{4,6},{5,7},{6,4},{7,5},{8,10},{9,11},{10,... | collective-permute-start | bytes 1179656 | tf_op jit(solution)/shard_map/ppermute | solution.py:30
  436.2 41.6 %collective-permute-start.32 = (bf16[3,2,2,2,2,24,768]{6,5,3,2,1,0,4:T(8,128)(2,1)S(1)}, bf16[3,2,2,2,2,24,768]{6,5,3,2,1,0,4:T(8,128)(2,1)S(1)}, u32[]{:S(2)}, u32[]{:S(2)}) collective-permute-start(bf16[3,2,2,2,2,24,768]{6,5,3,2,1,0,4:T(8,128)(2,1)S(1)} %bitcast.477), channel_id=1, source_target_pairs={{0,1},{1,0},{2,3},{3,2},{4,5},{5,4},{6,7},{7,6},{8,9},{9,8},{10,11... | collective-permute-start | bytes 5308424 | tf_op jit(solution)/shard_map/ppermute | solution.py:30
  438.2 31.5 %collective-permute-start.38 = (bf16[2,2,2,2,24,768]{5,4,3,2,1,0:T(8,128)(2,1)S(1)}, bf16[2,2,2,2,24,768]{5,4,3,2,1,0:T(8,128)(2,1)S(1)}, u32[]{:S(2)}, u32[]{:S(2)}) collective-permute-start(bf16[2,2,2,2,24,768]{5,4,3,2,1,0:T(8,128)(2,1)S(1)} %dynamic-slice_bitcast_fusion.2), channel_id=1, source_target_pairs={{0,8},{4,12},{8,0},{12,4},{16,24},{20,28},{24,16},{28,20},{1,9},{5... | collective-permute-start | bytes 1769480 | tf_op jit(solution)/shard_map/ppermute | solution.py:30
  438.5 36.1 %collective-permute-start.43 = (bf16[2,2,2,2,24,768]{5,4,3,2,1,0:T(8,128)(2,1)S(1)}, bf16[2,2,2,2,24,768]{5,4,3,2,1,0:T(8,128)(2,1)S(1)}, u32[]{:S(2)}, u32[]{:S(2)}) collective-permute-start(bf16[2,2,2,2,24,768]{5,4,3,2,1,0:T(8,128)(2,1)S(1)} %dynamic-slice_bitcast_fusion.1), channel_id=1, source_target_pairs={{0,4},{4,0},{8,12},{12,8},{16,20},{20,16},{24,28},{28,24},{1,5},{5... | collective-permute-start | bytes 1769480 | tf_op jit(solution)/shard_map/ppermute | solution.py:30
  469.8 27.4 %collective-permute-start.39 = (bf16[2,2,2,24,768]{4,3,2,1,0:T(8,128)(2,1)S(1)}, bf16[2,2,2,24,768]{4,3,2,1,0:T(8,128)(2,1)S(1)}, u32[]{:S(2)}, u32[]{:S(2)}) collective-permute-start(bf16[2,2,2,24,768]{4,3,2,1,0:T(8,128)(2,1)S(1)} %dynamic-slice_bitcast_fusion.5), channel_id=1, source_target_pairs={{0,16},{4,20},{8,24},{12,28},{16,0},{20,4},{24,8},{28,12},{1,17},{... | collective-permute-start | bytes 884744 | tf_op jit(solution)/shard_map/ppermute | solution.py:30
  474.6 24.8 %collective-permute-start.44 = (bf16[2,2,2,24,768]{4,3,2,1,0:T(8,128)(2,1)S(1)}, bf16[2,2,2,24,768]{4,3,2,1,0:T(8,128)(2,1)S(1)}, u32[]{:S(2)}, u32[]{:S(2)}) collective-permute-start(bf16[2,2,2,24,768]{4,3,2,1,0:T(8,128)(2,1)S(1)} %dynamic-slice_bitcast_fusion.4), channel_id=1, source_target_pairs={{0,2},{1,3},{2,0},{3,1},{4,6},{5,7},{6,4},{7,5},{8,10},{9,11},{10,... | collective-permute-start | bytes 884744 | tf_op jit(solution)/shard_map/ppermute | solution.py:30
  478.1 32.4 %collective-permute-start.33 = (bf16[3,2,2,2,24,768]{5,4,3,2,1,0:T(8,128)(2,1)S(1)}, bf16[3,2,2,2,24,768]{5,4,3,2,1,0:T(8,128)(2,1)S(1)}, u32[]{:S(2)}, u32[]{:S(2)}) collective-permute-start(bf16[3,2,2,2,24,768]{5,4,3,2,1,0:T(8,128)(2,1)S(1)} %dynamic-slice_bitcast_fusion), channel_id=1, source_target_pairs={{0,2},{1,3},{2,0},{3,1},{4,6},{5,7},{6,4},{7,5},{8,10},{9,11},{10,... | collective-permute-start | bytes 2654216 | tf_op jit(solution)/shard_map/ppermute | solution.py:30
  499.5 14.7 %collective-permute-start.45 = (bf16[2,2,24,768]{3,2,0,1:T(8,128)(2,1)S(1)}, bf16[2,2,24,768]{3,2,0,1:T(8,128)(2,1)S(1)}, u32[]{:S(2)}, u32[]{:S(2)}) collective-permute-start(bf16[2,2,24,768]{3,2,0,1:T(8,128)(2,1)S(1)} %bitcast.492), channel_id=1, source_target_pairs={{0,8},{4,12},{8,0},{12,4},{16,24},{20,28},{24,16},{28,20},{1,9},{5... | collective-permute-start | bytes 442376 | tf_op jit(solution)/shard_map/ppermute | solution.py:30
  510.7 10.5 %collective-permute-start.34 = (bf16[3,2,2,24,768]{4,3,2,1,0:T(8,128)(2,1)S(1)}, bf16[3,2,2,24,768]{4,3,2,1,0:T(8,128)(2,1)S(1)}, u32[]{:S(2)}, u32[]{:S(2)}) collective-permute-start(bf16[3,2,2,24,768]{4,3,2,1,0:T(8,128)(2,1)S(1)} %dynamic-slice_bitcast_fusion.3), channel_id=1, source_target_pairs={{0,4},{4,0},{8,12},{12,8},{16,20},{20,16},{24,28},{28,24},{1,5},{5... | collective-permute-start | bytes 1327112 | tf_op jit(solution)/shard_map/ppermute | solution.py:30
  513.8 12.7 %collective-permute-start.41 = (bf16[2,24,768]{2,1,0:T(8,128)(2,1)S(1)}, bf16[2,24,768]{2,1,0:T(8,128)(2,1)S(1)}, u32[]{:S(2)}, u32[]{:S(2)}) collective-permute-start(bf16[2,24,768]{2,1,0:T(8,128)(2,1)S(1)} %dynamic-slice_bitcast_fusion.8), channel_id=1, source_target_pairs={{0,2},{1,3},{2,0},{3,1},{4,6},{5,7},{6,4},{7,5},{8,10},{9,11},{10,... | collective-permute-start | bytes 221192 | tf_op jit(solution)/shard_map/ppermute | solution.py:30
  514.2 20.6 %collective-permute-start.46 = (bf16[2,24,768]{2,1,0:T(8,128)(2,1)S(1)}, bf16[2,24,768]{2,1,0:T(8,128)(2,1)S(1)}, u32[]{:S(2)}, u32[]{:S(2)}) collective-permute-start(bf16[2,24,768]{2,1,0:T(8,128)(2,1)S(1)} %dynamic-slice_bitcast_fusion.7), channel_id=1, source_target_pairs={{0,16},{4,20},{8,24},{12,28},{16,0},{20,4},{24,8},{28,12},{1,17},{... | collective-permute-start | bytes 221192 | tf_op jit(solution)/shard_map/ppermute | solution.py:30
  521.4 13.3 %collective-permute-start.35 = (bf16[3,2,24,768]{3,2,0,1:T(8,128)(2,1)S(1)}, bf16[3,2,24,768]{3,2,0,1:T(8,128)(2,1)S(1)}, u32[]{:S(2)}, u32[]{:S(2)}) collective-permute-start(bf16[3,2,24,768]{3,2,0,1:T(8,128)(2,1)S(1)} %bitcast.490), channel_id=1, source_target_pairs={{0,8},{4,12},{8,0},{12,4},{16,24},{20,28},{24,16},{28,20},{1,9},{5... | collective-permute-start | bytes 663560 | tf_op jit(solution)/shard_map/ppermute | solution.py:30
  534.8 9.7 %collective-permute-start.36 = (bf16[3,24,768]{2,1,0:T(8,128)(2,1)S(1)}, bf16[3,24,768]{2,1,0:T(8,128)(2,1)S(1)}, u32[]{:S(2)}, u32[]{:S(2)}) collective-permute-start(bf16[3,24,768]{2,1,0:T(8,128)(2,1)S(1)} %dynamic-slice_bitcast_fusion.6), channel_id=1, source_target_pairs={{0,16},{4,20},{8,24},{12,28},{16,0},{20,4},{24,8},{28,12},{1,17},{... | collective-permute-start | bytes 331784 | tf_op jit(solution)/shard_map/ppermute | solution.py:30
  (139 other events, 761.7 us)
Sparse Core Ops, SparseCore 0:
  10.9 106.3 all-gather.2
  120.2 91.5 all-gather.4
  245.1 142.4 reduce-scatter.4
  393.5 171.6 reduce-scatter.2

commit v5 on v4

--- a/solution.py
+++ b/solution.py
@@ -833,22 +833,24 @@
         axis=2,
     ).reshape(devices, 1, -1)
     vec = jnp.concatenate([vec, jnp.broadcast_to(digits, (devices, 1, 18))], axis=2)
-    vec = jnp.pad(
-        vec.astype(jnp.bfloat16), ((0, 0), (0, per - 1), (0, width - vec.shape[2]))
-    ).reshape(width, width)
+    vec = jnp.pad(vec.astype(jnp.bfloat16), ((0, 0), (0, 7), (0, width - vec.shape[2])))
+    ends = [square.reshape(devices, per, width) for square in squares[:2]] + [vec]
+    ends = jnp.concatenate(ends, axis=1).reshape(1, -1, width)
     lots = (
-        [squares[3], kept[3]],
-        [squares[2], kept[2]],
-        [squares[0], squares[1], vec],
+        jnp.stack([squares[3], kept[3]]),
+        jnp.stack([squares[2], kept[2]]),
+        ends,
     )
     halves = []
-    for lot, order in zip(lots, orders):
-        blocks, dims = split_rows(jnp.stack(lot))
+    halving = (orders[2], orders[0], orders[1])
+    for lot, order in zip(lots, halving):
+        blocks, dims = split_rows(lot)
         halves.append(halve(blocks, dims, order[:2]))
     one, two, three = (
-        halve(blocks, dims, order[2:])[0] for (blocks, dims), order in zip(halves, orders)
-    )
-    row = three[2, 0].astype(jnp.float32)
+        halve(blocks, dims, order[2:])[0] for (blocks, dims), order in zip(halves, halving)
+    )
+    row = three[0, 2 * per].astype(jnp.float32)
+    three = three[0, : 2 * per].reshape(2, per, width)
     size = layers * (5 + parts) * per
     mine_all = row[:size].reshape(layers, -1)
     share_all = number_of(row[size : size + 12]) / share_unit

time: 586 us -> 578 us (0.986)
  local copies, waits for them, and re-layouts: 46.8 us -> 62.3 us
  waiting for transfers between devices: 236 us -> 221 us
  starting transfers between devices: 57.8 us -> 48.8 us
    unnamed x260 -> x250, local copies, waits for them, and re-layouts: 21.5 us -> 30.7 us
    ppermute x47, starting transfers between devices: 57.6 us -> 48.6 us  [flip(): return lax.ppermute(array, axis, [(i, i ^ bit) for i in range(size)])]
    ppermute x47, waiting for transfers between devices: 218 us -> 210 us  [flip(): return lax.ppermute(array, axis, [(i, i ^ bit) for i in range(size)])]
    reduce_scatter x2, waiting for transfers between devices: 16.5 us -> 9.91 us  [local(): lax.psum_scatter(wide, both, scatter_dimension=0, tiled=True)]
  transfers between devices with their start and end apart: 51 -> 51, of which waited for: 28 -> 29; matrix products, arithmetic and copies ran while one was open for 25% -> 28% of each run, Pallas kernels for 12% -> 13%
where the time goes in v5:
time: 578 us; the launch traced here: 569 us
  waiting for transfers between devices  221 us (38%)
  matrix products  86.8 us (15%)
  Pallas kernels  78.3 us (14%)
  local copies, waits for them, and re-layouts  62.3 us (11%)
  other arithmetic  51.5 us (9%)
  starting transfers between devices  48.8 us (8%)
  between operations  20.6 us (4%)
    ppermute x47, waiting for transfers between devices, flip(): return lax.ppermute(array, axis, [(i, i ^ bit) for i in range(size)])  210 us
    dot_general x36, matrix products, product(): return jnp.einsum(form, left, right, preferred_element_type=jnp.float32)  55.3 us
    ppermute x47, starting transfers between devices, flip(): return lax.ppermute(array, axis, [(i, i ^ bit) for i in range(size)])  48.6 us
    pallas_call x2, Pallas kernels, back(): pl.pallas_call(back_kernel, name='back', out_shape=(jax.ShapeDtypeStruct(...  32.7 us
    unnamed x250, local copies, waits for them, and re-layouts  30.7 us
    pallas_call x2, Pallas kernels, mix(): pl.pallas_call(mix_kernel, name='mix', out_shape=(jax.ShapeDtypeStruct((r...  21.9 us
    dot_general x8, matrix products, local(): jnp.dot(square_of(forward_active, k), square_at(layer_index, 4 + parts +...  11.6 us
  transfers between devices with their start and end apart: 51, of which 29 were waited for; matrix products, arithmetic and copies ran while one was open for 28% of the time, Pallas kernels for 13%

profile of v5, /device:TPU:0, one launch (start us, length us, event | category | flops | bytes accessed | tf_op | source)
XLA Modules:
  0.0 569.0 jit_solution(15977220776061097381)
XLA Ops:
  13.8 4.1 collective-permute-start
  18.9 3.9 collective-permute-done
  22.9 4.7 collective-permute-start.1
  33.1 5.4 collective-permute-done.1
  44.9 6.3 %collective-permute-done.2 = bf16[2,2,56,768]{3,2,0,1:T(8,128)(2,1)S(1)} collective-permute-done((bf16[2,2,56,768]{3,2,0,1:T(8,128)(2,1)S(1)}, bf16[2,2,56,768]{3,2,0,1:T(8,128)(2,1)S(1)}, u32[]{:S(2)}, u32[]{:S(2)}) %collective-permute-start.2) | collective-permute-done | bytes 344096 | tf_op jit(solution)/shard_map/ppermute | solution.py:30
  52.9 8.7 %collective-permute-done.7 = bf16[2,2,24,2304]{3,2,0,1:T(8,128)(2,1)S(1)} collective-permute-done((bf16[2,2,24,2304]{3,2,0,1:T(8,128)(2,1)S(1)}, bf16[2,2,24,2304]{3,2,0,1:T(8,128)(2,1)S(1)}, u32[]{:S(2)}, u32[]{:S(2)}) %collective-permute-start.7) | collective-permute-done | bytes 442400 | tf_op jit(solution)/shard_map/ppermute | solution.py:30
  63.4 12.1 %collective-permute-done.3 = bf16[2,2,2,56,768]{4,3,0,1,2:T(8,128)(2,1)S(1)} collective-permute-done((bf16[2,2,2,56,768]{4,3,0,1,2:T(8,128)(2,1)S(1)}, bf16[2,2,2,56,768]{4,3,0,1,2:T(8,128)(2,1)S(1)}, u32[]{:S(2)}, u32[]{:S(2)}) %collective-permute-start.3) | collective-permute-done | bytes 688160 | tf_op jit(solution)/shard_map/ppermute | solution.py:30
  76.8 13.8 %collective-permute-done.8 = bf16[2,2,2,24,2304]{4,3,0,1,2:T(8,128)(2,1)} collective-permute-done((bf16[2,2,2,24,2304]{4,3,0,1,2:T(8,128)(2,1)S(1)}, bf16[2,2,2,24,2304]{4,3,0,1,2:T(8,128)(2,1)}, u32[]{:S(2)}, u32[]{:S(2)}) %collective-permute-start.8) | collective-permute-done | bytes 884768 | tf_op jit(solution)/shard_map/ppermute | solution.py:30
  108.1 15.6 %collective-permute-done.11.refs_2_.refs_6_ = bf16[256,1536]{1,0:T(8,128)(2,1)S(1)} collective-permute-done((bf16[256,1536]{1,0:T(8,128)(2,1)S(1)}, bf16[256,1536]{1,0:T(8,128)(2,1)S(1)}, u32[]{:S(2)}, u32[]{:S(2)}) %collective-permute-start.11) | collective-permute-done | bytes 786464 | tf_op jit(solution)/shard_map/ppermute | solution.py:30
  127.4 3.8 pick.2
  138.8 10.9 %mix.2 = (bf16[256,768]{1,0:T(8,128)(2,1)}, f32[256,768]{1,0:T(8,128)}) custom-call(s32[2]{0:T(128)} %pad_add_fusion.scalars, bf16[256,768]{1,0:T(8,128)(2,1)} %convolution_convert_fusion.23.q_ref, f32[256,1024]{1,0:T(8,128)} %get-tuple-element.74.carried_ref, f32[1,1024]{1,0:T(1,128)} %fusion.160.before_ref, bf16[256,1536]{1,0:T(8,128)(2,1)} %copy-done, ...), custom_call_target="tpu_custom_call" | custom-call | tf_op jit(solution)/shard_map/mix/pallas_call | solution.py:443
  151.6 6.3 %multiply_convert_fusion.1 = (bf16[256,3072]{1,0:T(8,128)(2,1)S(1)}, f32[256,3072]{1,0:T(8,128)}) fusion(f32[3072]{0:T(1024)S(1)} %bitcast.510, bf16[768,7680]{1,0:T(8,128)(2,1)} %all-gather.3.cloned.1.call-done, f32[1,256,768]{2,1,0:T(8,128)S(1)} %get-tuple-element.239, f32[768]{0:T(1024)S(1)} %get-tuple-element.140, f32[768]{0:T(1024)S(1)} %get-tuple-element.251, ...), kind=kOutput, calls=%fused_computation.38 | convolution fusion | flops 1216806912 | bytes 10244096 | tf_op jit(solution)/shard_map/dot_general | solution.py:684
  163.8 25.2 %collective-permute-done.16.refs_2_.refs_6_ = bf16[256,1536]{1,0:T(8,128)(2,1)S(1)} collective-permute-done((bf16[256,1536]{1,0:T(8,128)(2,1)S(1)}, bf16[256,1536]{1,0:T(8,128)(2,1)S(1)}, u32[]{:S(2)}, u32[]{:S(2)}) %collective-permute-start.16) | collective-permute-done | bytes 786464 | tf_op jit(solution)/shard_map/ppermute | solution.py:30
  206.0 11.0 %mix.3 = (bf16[256,768]{1,0:T(8,128)(2,1)}, f32[256,768]{1,0:T(8,128)}) custom-call(s32[2]{0:T(128)} %pad_add_fusion.scalars, bf16[256,768]{1,0:T(8,128)(2,1)} %convolution_convert_fusion.22.q_ref, f32[256,1024]{1,0:T(8,128)} %get-tuple-element.82.carried_ref, f32[1,1024]{1,0:T(1,128)} %get-tuple-element.204.before_ref, bf16[256,1536]{1,0:T(8,128)(2,1)} %copy-done.4, ...), custom_call_target="tpu_custom_call" | custom-call | tf_op jit(solution)/shard_map/mix/pallas_call | solution.py:443
  226.6 4.1 convert_reduce_fusion
  230.8 3.8 fusion
  248.5 16.3 %back.2 = (bf16[256,768]{1,0:T(8,128)(2,1)}, bf16[4,256,768]{2,1,0:T(8,128)(2,1)}, bf16[4,256,768]{2,1,0:T(8,128)(2,1)}, f32[256,1024]{1,0:T(8,128)}, f32[256,1024]{1,0:T(8,128)}, /*index=5*/f32[1,1024]{1,0:T(1,128)}) custom-call(s32[2]{0:T(128)} %pad_add_fusion.scalars, bf16[256,768]{1,0:T(8,128)(2,1)} %convolution_convert_fusion.22.q_ref, ...), custom_call_target="tpu_custom_call" | custom-call | tf_op jit(solution)/shard_map/back/pallas_call | solution.py:473
  275.2 9.1 %collective-permute-done.23 = bf16[1,256,768]{2,1,0:T(8,128)(2,1)} collective-permute-done((bf16[1,256,768]{2,1,0:T(8,128)(2,1)S(1)}, bf16[1,256,768]{2,1,0:T(8,128)(2,1)}, u32[]{:S(2)}, u32[]{:S(2)}) %collective-permute-start.23) | collective-permute-done | bytes 393248 | tf_op jit(solution)/shard_map/ppermute | solution.py:30
  286.8 4.7 first.2
  302.2 16.4 %collective-permute-done.25 = bf16[1,256,768]{2,1,0:T(8,128)(2,1)S(1)} collective-permute-done((bf16[1,256,768]{2,1,0:T(8,128)(2,1)S(1)}, bf16[1,256,768]{2,1,0:T(8,128)(2,1)S(1)}, u32[]{:S(2)}, u32[]{:S(2)}) %collective-permute-start.25) | collective-permute-done | bytes 393248 | tf_op jit(solution)/shard_map/ppermute | solution.py:30
  338.4 3.8 fusion.1
  351.3 16.4 %back.3 = (bf16[256,768]{1,0:T(8,128)(2,1)}, bf16[4,256,768]{2,1,0:T(8,128)(2,1)}, bf16[4,256,768]{2,1,0:T(8,128)(2,1)}, f32[256,1024]{1,0:T(8,128)}, f32[256,1024]{1,0:T(8,128)}, /*index=5*/f32[1,1024]{1,0:T(1,128)}) custom-call(s32[2]{0:T(128)} %pad_add_fusion.scalars, bf16[256,768]{1,0:T(8,128)(2,1)} %convolution_convert_fusion.23.q_ref, ...), custom_call_target="tpu_custom_call" | custom-call | tf_op jit(solution)/shard_map/back/pallas_call | solution.py:473
  382.0 7.9 %collective-permute-done.29 = bf16[1,256,768]{2,1,0:T(8,128)(2,1)S(1)} collective-permute-done((bf16[1,256,768]{2,1,0:T(8,128)(2,1)S(1)}, bf16[1,256,768]{2,1,0:T(8,128)(2,1)S(1)}, u32[]{:S(2)}, u32[]{:S(2)}) %collective-permute-start.29) | collective-permute-done | bytes 393248 | tf_op jit(solution)/shard_map/ppermute | solution.py:30
  391.3 4.5 first.3
  457.5 13.5 %collective-permute-done.38 = bf16[2,2,2,2,24,768]{5,4,3,2,1,0:T(8,128)(2,1)S(1)} collective-permute-done((bf16[2,2,2,2,24,768]{5,4,3,2,1,0:T(8,128)(2,1)S(1)}, bf16[2,2,2,2,24,768]{5,4,3,2,1,0:T(8,128)(2,1)S(1)}, u32[]{:S(2)}, u32[]{:S(2)}) %collective-permute-start.38) | collective-permute-done | bytes 589856 | tf_op jit(solution)/shard_map/ppermute | solution.py:30
  472.6 19.5 %collective-permute-done.43 = bf16[2,2,2,2,24,768]{5,4,3,2,1,0:T(8,128)(2,1)S(1)} collective-permute-done((bf16[2,2,2,2,24,768]{5,4,3,2,1,0:T(8,128)(2,1)S(1)}, bf16[2,2,2,2,24,768]{5,4,3,2,1,0:T(8,128)(2,1)S(1)}, u32[]{:S(2)}, u32[]{:S(2)}) %collective-permute-start.43) | collective-permute-done | bytes 589856 | tf_op jit(solution)/shard_map/ppermute | solution.py:30
  495.4 12.8 %collective-permute-done.44 = bf16[2,2,2,24,768]{4,3,2,1,0:T(8,128)(2,1)S(1)} collective-permute-done((bf16[2,2,2,24,768]{4,3,2,1,0:T(8,128)(2,1)S(1)}, bf16[2,2,2,24,768]{4,3,2,1,0:T(8,128)(2,1)S(1)}, u32[]{:S(2)}, u32[]{:S(2)}) %collective-permute-start.44) | collective-permute-done | bytes 294944 | tf_op jit(solution)/shard_map/ppermute | solution.py:30
  511.6 5.5 collective-permute-done.45
  518.9 6.2 %collective-permute-done.34 = bf16[1,2,2,56,768]{4,3,2,1,0:T(8,128)(2,1)S(1)} collective-permute-done((bf16[1,2,2,56,768]{4,3,2,1,0:T(8,128)(2,1)S(1)}, bf16[1,2,2,56,768]{4,3,2,1,0:T(8,128)(2,1)S(1)}, u32[]{:S(2)}, u32[]{:S(2)}) %collective-permute-start.34) | collective-permute-done | bytes 344096 | tf_op jit(solution)/shard_map/ppermute | solution.py:30
  525.9 10.2 %collective-permute-done.35 = bf16[1,2,56,768]{3,2,1,0:T(8,128)(2,1)S(1)} collective-permute-done((bf16[1,2,56,768]{3,2,1,0:T(8,128)(2,1)S(1)}, bf16[1,2,56,768]{3,2,1,0:T(8,128)(2,1)S(1)}, u32[]{:S(2)}, u32[]{:S(2)}) %collective-permute-start.35) | collective-permute-done | bytes 172064 | tf_op jit(solution)/shard_map/ppermute | solution.py:30
  537.0 5.6 collective-permute-done.36
  547.3 9.9 %reduce-scatter.3.cloned.1.call-done.late_ref = bf16[24,7680]{1,0:T(8,128)(2,1)} async-done(((bf16[768,7680]{1,0:T(8,128)(2,1)}), bf16[24,7680]{1,0:T(8,128)(2,1)}) %reduce-scatter.3.cloned.1.call-update) | async-done | bytes 368656 | tf_op jit(solution)/shard_map/reduce_scatter | solution.py:767
  (585 shorter events, 246.5 us)
Async XLA Ops:
  7.2 144.4 %all-gather.3.cloned.1.call-start = ((), (), s32[]{:S(2)}) async-start(), calls=%async_computation.2 | async-start | bytes 12165120 | tf_op jit(solution)/shard_map/all_gather | solution.py:592
  10.5 207.2 %all-gather.5.cloned.1.call-start = ((), (), s32[]{:S(2)}) async-start(), calls=%async_computation.3 | async-start | bytes 10948608 | tf_op jit(solution)/shard_map/all_gather | solution.py:592
  11.3 536.0 %reduce-scatter.5.cloned.1.call-start = ((), (), s32[]{:S(2)}) async-start(), calls=%async_computation.5 | async-start | bytes 9732096 | tf_op jit(solution)/shard_map/reduce_scatter | solution.py:767
  13.8 9.0 %collective-permute-start = (bf16[56,768]{1,0:T(8,128)(2,1)S(1)}, bf16[56,768]{1,0:T(8,128)(2,1)S(1)}, u32[]{:S(2)}, u32[]{:S(2)}) collective-permute-start(bf16[56,768]{1,0:T(8,128)(2,1)S(1)} %fusion.159), channel_id=1, source_target_pairs={{0,16},{4,20},{8,24},{12,28},{16,0},{20,4},{24,8},{28,12},{1,17},{... | collective-permute-start | bytes 258056 | tf_op jit(solution)/shard_map/ppermute | solution.py:30
  18.8 11.1 %collective-permute-start.5 = (bf16[24,2304]{1,0:T(8,128)(2,1)S(1)}, bf16[24,2304]{1,0:T(8,128)(2,1)S(1)}, u32[]{:S(2)}, u32[]{:S(2)}) collective-permute-start(bf16[24,2304]{1,0:T(8,128)(2,1)S(1)} %pad_maximum_fusion.13), channel_id=1, source_target_pairs={{0,16},{4,20},{8,24},{12,28},{16,0},{20,4},{24,8},{28,12},{1,17},{... | collective-permute-start | bytes 331784 | tf_op jit(solution)/shard_map/ppermute | solution.py:30
  22.9 15.6 %collective-permute-start.1 = (bf16[2,56,768]{2,1,0:T(8,128)(2,1)S(1)}, bf16[2,56,768]{2,1,0:T(8,128)(2,1)S(1)}, u32[]{:S(2)}, u32[]{:S(2)}) collective-permute-start(bf16[2,56,768]{2,1,0:T(8,128)(2,1)S(1)} %pad_maximum_fusion.12), channel_id=1, source_target_pairs={{0,8},{4,12},{8,0},{12,4},{16,24},{20,28},{24,16},{28,20},{1,9},{5... | collective-permute-start | bytes 516104 | tf_op jit(solution)/shard_map/ppermute | solution.py:30
  30.0 13.1 %collective-permute-start.6 = (bf16[2,24,2304]{2,1,0:T(8,128)(2,1)S(1)}, bf16[2,24,2304]{2,1,0:T(8,128)(2,1)S(1)}, u32[]{:S(2)}, u32[]{:S(2)}) collective-permute-start(bf16[2,24,2304]{2,1,0:T(8,128)(2,1)S(1)} %pad_maximum_fusion.11), channel_id=1, source_target_pairs={{0,8},{4,12},{8,0},{12,4},{16,24},{20,28},{24,16},{28,20},{1,9},{5... | collective-permute-start | bytes 663560 | tf_op jit(solution)/shard_map/ppermute | solution.py:30
  38.6 12.5 %collective-permute-start.2 = (bf16[2,2,56,768]{3,2,0,1:T(8,128)(2,1)S(1)}, bf16[2,2,56,768]{3,2,0,1:T(8,128)(2,1)S(1)}, u32[]{:S(2)}, u32[]{:S(2)}) collective-permute-start(bf16[2,2,56,768]{3,2,0,1:T(8,128)(2,1)S(1)} %pad_maximum_fusion.10), channel_id=1, source_target_pairs={{0,2},{1,3},{2,0},{3,1},{4,6},{5,7},{6,4},{7,5},{8,10},{9,11},{10,... | collective-permute-start | bytes 1032200 | tf_op jit(solution)/shard_map/ppermute | solution.py:30
  43.2 18.4 %collective-permute-start.7 = (bf16[2,2,24,2304]{3,2,0,1:T(8,128)(2,1)S(1)}, bf16[2,2,24,2304]{3,2,0,1:T(8,128)(2,1)S(1)}, u32[]{:S(2)}, u32[]{:S(2)}) collective-permute-start(bf16[2,2,24,2304]{3,2,0,1:T(8,128)(2,1)S(1)} %pad_maximum_fusion.9), channel_id=1, source_target_pairs={{0,4},{4,0},{8,12},{12,8},{16,20},{20,16},{24,28},{28,24},{1,5},{5... | collective-permute-start | bytes 1327112 | tf_op jit(solution)/shard_map/ppermute | solution.py:30
  51.3 24.2 %collective-permute-start.3 = (bf16[2,2,2,56,768]{4,3,0,1,2:T(8,128)(2,1)S(1)}, bf16[2,2,2,56,768]{4,3,0,1,2:T(8,128)(2,1)S(1)}, u32[]{:S(2)}, u32[]{:S(2)}) collective-permute-start(bf16[2,2,2,56,768]{4,3,0,1,2:T(8,128)(2,1)S(1)} %pad_maximum_fusion.8), channel_id=1, source_target_pairs={{0,4},{4,0},{8,12},{12,8},{16,20},{20,16},{24,28},{28,24},{1,5},{5... | collective-permute-start | bytes 2064392 | tf_op jit(solution)/shard_map/ppermute | solution.py:30
  61.8 28.8 %collective-permute-start.8 = (bf16[2,2,2,24,2304]{4,3,0,1,2:T(8,128)(2,1)S(1)}, bf16[2,2,2,24,2304]{4,3,0,1,2:T(8,128)(2,1)}, u32[]{:S(2)}, u32[]{:S(2)}) collective-permute-start(bf16[2,2,2,24,2304]{4,3,0,1,2:T(8,128)(2,1)S(1)} %pad_maximum_fusion.7), channel_id=1, source_target_pairs={{0,2},{1,3},{2,0},{3,1},{4,6},{5,7},{6,4},{7,5},{8,10},{9,11},{10,... | collective-permute-start | bytes 2654216 | tf_op jit(solution)/shard_map/ppermute | solution.py:30
  76.8 16.7 %collective-permute-start.4 = (bf16[2,2,2,2,56,768]{5,4,1,0,2,3:T(8,128)(2,1)}, bf16[2,2,2,2,56,768]{5,4,1,0,2,3:T(8,128)(2,1)}, u32[]{:S(2)}, u32[]{:S(2)}) collective-permute-start(bf16[2,2,2,2,56,768]{5,4,1,0,2,3:T(8,128)(2,1)} %pad_maximum_fusion.6), channel_id=1, source_target_pairs={{0,1},{1,0},{2,3},{3,2},{4,5},{5,4},{6,7},{7,6},{8,9},{9,8},{10,11... | collective-permute-start | bytes 4128776 | tf_op jit(solution)/shard_map/ppermute | solution.py:30
  102.8 20.8 %collective-permute-start.11 = (bf16[256,1536]{1,0:T(8,128)(2,1)S(1)}, bf16[256,1536]{1,0:T(8,128)(2,1)S(1)}, u32[]{:S(2)}, u32[]{:S(2)}) collective-permute-start(bf16[256,1536]{1,0:T(8,128)(2,1)S(1)} %convolution_convert_fusion.3.refs_0_.refs_4_), channel_id=1, source_target_pairs={{0,2},{1,3},{2,0},{3,1},{4,6},{5,7},{6,4},{7,5},{8,10},{9,11},{10,... | collective-permute-start | bytes 2359304 | tf_op jit(solution)/shard_map/ppermute | solution.py:30
  107.9 17.8 %collective-permute-start.10 = (bf16[256,1536]{1,0:T(8,128)(2,1)S(1)}, bf16[256,1536]{1,0:T(8,128)(2,1)S(1)}, u32[]{:S(2)}, u32[]{:S(2)}) collective-permute-start(bf16[256,1536]{1,0:T(8,128)(2,1)S(1)} %convolution_convert_fusion.3.refs_0_.refs_4_), channel_id=1, source_target_pairs={{0,1},{1,0},{2,3},{3,2},{4,5},{5,4},{6,7},{7,6},{8,9},{9,8},{10,11... | collective-permute-start | bytes 2359304 | tf_op jit(solution)/shard_map/ppermute | solution.py:30
  162.0 27.0 %collective-permute-start.16 = (bf16[256,1536]{1,0:T(8,128)(2,1)S(1)}, bf16[256,1536]{1,0:T(8,128)(2,1)S(1)}, u32[]{:S(2)}, u32[]{:S(2)}) collective-permute-start(bf16[256,1536]{1,0:T(8,128)(2,1)S(1)} %convolution_convert_fusion.2.refs_0_.refs_4_), channel_id=1, source_target_pairs={{0,2},{1,3},{2,0},{3,1},{4,6},{5,7},{6,4},{7,5},{8,10},{9,11},{10,... | collective-permute-start | bytes 2359304 | tf_op jit(solution)/shard_map/ppermute | solution.py:30
  163.8 28.0 %collective-permute-start.15 = (bf16[256,1536]{1,0:T(8,128)(2,1)S(1)}, bf16[256,1536]{1,0:T(8,128)(2,1)S(1)}, u32[]{:S(2)}, u32[]{:S(2)}) collective-permute-start(bf16[256,1536]{1,0:T(8,128)(2,1)S(1)} %convolution_convert_fusion.2.refs_0_.refs_4_), channel_id=1, source_target_pairs={{0,1},{1,0},{2,3},{3,2},{4,5},{5,4},{6,7},{7,6},{8,9},{9,8},{10,11... | collective-permute-start | bytes 2359304 | tf_op jit(solution)/shard_map/ppermute | solution.py:30
  245.2 312.0 %reduce-scatter.3.cloned.1.call-start = ((), (), s32[]{:S(2)}) async-start(), calls=%async_computation.4 | async-start | bytes 12165120 | tf_op jit(solution)/shard_map/reduce_scatter | solution.py:767
  273.1 11.3 %collective-permute-start.23 = (bf16[1,256,768]{2,1,0:T(8,128)(2,1)S(1)}, bf16[1,256,768]{2,1,0:T(8,128)(2,1)}, u32[]{:S(2)}, u32[]{:S(2)}) collective-permute-start(bf16[1,256,768]{2,1,0:T(8,128)(2,1)S(1)} %slice_bitcast_fusion.14), channel_id=1, source_target_pairs={{0,2},{1,3},{2,0},{3,1},{4,6},{5,7},{6,4},{7,5},{8,10},{9,11},{10,... | collective-permute-start | bytes 1179656 | tf_op jit(solution)/shard_map/ppermute | solution.py:30
  299.8 18.8 %collective-permute-start.25 = (bf16[1,256,768]{2,1,0:T(8,128)(2,1)S(1)}, bf16[1,256,768]{2,1,0:T(8,128)(2,1)S(1)}, u32[]{:S(2)}, u32[]{:S(2)}) collective-permute-start(bf16[1,256,768]{2,1,0:T(8,128)(2,1)S(1)} %slice_bitcast_fusion.12), channel_id=1, source_target_pairs={{0,2},{1,3},{2,0},{3,1},{4,6},{5,7},{6,4},{7,5},{8,10},{9,11},{10,... | collective-permute-start | bytes 1179656 | tf_op jit(solution)/shard_map/ppermute | solution.py:30
  378.9 11.0 %collective-permute-start.29 = (bf16[1,256,768]{2,1,0:T(8,128)(2,1)S(1)}, bf16[1,256,768]{2,1,0:T(8,128)(2,1)S(1)}, u32[]{:S(2)}, u32[]{:S(2)}) collective-permute-start(bf16[1,256,768]{2,1,0:T(8,128)(2,1)S(1)} %slice_bitcast_fusion.10), channel_id=1, source_target_pairs={{0,2},{1,3},{2,0},{3,1},{4,6},{5,7},{6,4},{7,5},{8,10},{9,11},{10,... | collective-permute-start | bytes 1179656 | tf_op jit(solution)/shard_map/ppermute | solution.py:30
  406.0 11.7 %collective-permute-start.31 = (bf16[1,256,768]{2,1,0:T(8,128)(2,1)}, bf16[1,256,768]{2,1,0:T(8,128)(2,1)}, u32[]{:S(2)}, u32[]{:S(2)}) collective-permute-start(bf16[1,256,768]{2,1,0:T(8,128)(2,1)} %slice_bitcast_fusion.8), channel_id=1, source_target_pairs={{0,2},{1,3},{2,0},{3,1},{4,6},{5,7},{6,4},{7,5},{8,10},{9,11},{10,... | collective-permute-start | bytes 1179656 | tf_op jit(solution)/shard_map/ppermute | solution.py:30
  453.9 17.0 %collective-permute-start.38 = (bf16[2,2,2,2,24,768]{5,4,3,2,1,0:T(8,128)(2,1)S(1)}, bf16[2,2,2,2,24,768]{5,4,3,2,1,0:T(8,128)(2,1)S(1)}, u32[]{:S(2)}, u32[]{:S(2)}) collective-permute-start(bf16[2,2,2,2,24,768]{5,4,3,2,1,0:T(8,128)(2,1)S(1)} %dynamic-slice_bitcast_fusion.2), channel_id=1, source_target_pairs={{0,2},{1,3},{2,0},{3,1},{4,6},{5,7},{6,4},{7,5},{8,10},{9,11},{10,... | collective-permute-start | bytes 1769480 | tf_op jit(solution)/shard_map/ppermute | solution.py:30
  455.8 36.3 %collective-permute-start.43 = (bf16[2,2,2,2,24,768]{5,4,3,2,1,0:T(8,128)(2,1)S(1)}, bf16[2,2,2,2,24,768]{5,4,3,2,1,0:T(8,128)(2,1)S(1)}, u32[]{:S(2)}, u32[]{:S(2)}) collective-permute-start(bf16[2,2,2,2,24,768]{5,4,3,2,1,0:T(8,128)(2,1)S(1)} %dynamic-slice_bitcast_fusion.1), channel_id=1, source_target_pairs={{0,8},{4,12},{8,0},{12,4},{16,24},{20,28},{24,16},{28,20},{1,9},{5... | collective-permute-start | bytes 1769480 | tf_op jit(solution)/shard_map/ppermute | solution.py:30
  456.1 53.8 %collective-permute-start.33 = (bf16[1,2,2,2,56,768]{5,4,3,2,1,0:T(8,128)(2,1)S(1)}, bf16[1,2,2,2,56,768]{5,4,3,2,1,0:T(8,128)(2,1)S(1)}, u32[]{:S(2)}, u32[]{:S(2)}) collective-permute-start(bf16[1,2,2,2,56,768]{5,4,3,2,1,0:T(8,128)(2,1)S(1)} %dynamic-slice_bitcast_fusion), channel_id=1, source_target_pairs={{0,4},{4,0},{8,12},{12,8},{16,20},{20,16},{24,28},{28,24},{1,5},{5... | collective-permute-start | bytes 2064392 | tf_op jit(solution)/shard_map/ppermute | solution.py:30
  471.1 21.6 %collective-permute-start.39 = (bf16[2,2,2,24,768]{4,3,2,1,0:T(8,128)(2,1)S(1)}, bf16[2,2,2,24,768]{4,3,2,1,0:T(8,128)(2,1)S(1)}, u32[]{:S(2)}, u32[]{:S(2)}) collective-permute-start(bf16[2,2,2,24,768]{4,3,2,1,0:T(8,128)(2,1)S(1)} %dynamic-slice_bitcast_fusion.5), channel_id=1, source_target_pairs={{0,4},{4,0},{8,12},{12,8},{16,20},{20,16},{24,28},{28,24},{1,5},{5... | collective-permute-start | bytes 884744 | tf_op jit(solution)/shard_map/ppermute | solution.py:30
  492.2 16.0 %collective-permute-start.44 = (bf16[2,2,2,24,768]{4,3,2,1,0:T(8,128)(2,1)S(1)}, bf16[2,2,2,24,768]{4,3,2,1,0:T(8,128)(2,1)S(1)}, u32[]{:S(2)}, u32[]{:S(2)}) collective-permute-start(bf16[2,2,2,24,768]{4,3,2,1,0:T(8,128)(2,1)S(1)} %dynamic-slice_bitcast_fusion.4), channel_id=1, source_target_pairs={{0,16},{4,20},{8,24},{12,28},{16,0},{20,4},{24,8},{28,12},{1,17},{... | collective-permute-start | bytes 884744 | tf_op jit(solution)/shard_map/ppermute | solution.py:30
  492.8 18.7 %collective-permute-start.40 = (bf16[2,2,24,768]{3,2,0,1:T(8,128)(2,1)S(1)}, bf16[2,2,24,768]{3,2,0,1:T(8,128)(2,1)S(1)}, u32[]{:S(2)}, u32[]{:S(2)}) collective-permute-start(bf16[2,2,24,768]{3,2,0,1:T(8,128)(2,1)S(1)} %bitcast.493), channel_id=1, source_target_pairs={{0,8},{4,12},{8,0},{12,4},{16,24},{20,28},{24,16},{28,20},{1,9},{5... | collective-permute-start | bytes 442376 | tf_op jit(solution)/shard_map/ppermute | solution.py:30
  508.2 8.8 %collective-permute-start.45 = (bf16[2,2,24,768]{3,2,0,1:T(8,128)(2,1)S(1)}, bf16[2,2,24,768]{3,2,0,1:T(8,128)(2,1)S(1)}, u32[]{:S(2)}, u32[]{:S(2)}) collective-permute-start(bf16[2,2,24,768]{3,2,0,1:T(8,128)(2,1)S(1)} %bitcast.494), channel_id=1, source_target_pairs={{0,4},{4,0},{8,12},{12,8},{16,20},{20,16},{24,28},{28,24},{1,5},{5... | collective-permute-start | bytes 442376 | tf_op jit(solution)/shard_map/ppermute | solution.py:30
  510.0 15.1 %collective-permute-start.34 = (bf16[1,2,2,56,768]{4,3,2,1,0:T(8,128)(2,1)S(1)}, bf16[1,2,2,56,768]{4,3,2,1,0:T(8,128)(2,1)S(1)}, u32[]{:S(2)}, u32[]{:S(2)}) collective-permute-start(bf16[1,2,2,56,768]{4,3,2,1,0:T(8,128)(2,1)S(1)} %dynamic-slice_bitcast_fusion.3), channel_id=1, source_target_pairs={{0,2},{1,3},{2,0},{3,1},{4,6},{5,7},{6,4},{7,5},{8,10},{9,11},{10,... | collective-permute-start | bytes 1032200 | tf_op jit(solution)/shard_map/ppermute | solution.py:30
  511.6 13.7 %collective-permute-start.41 = (bf16[2,24,768]{2,1,0:T(8,128)(2,1)S(1)}, bf16[2,24,768]{2,1,0:T(8,128)(2,1)S(1)}, u32[]{:S(2)}, u32[]{:S(2)}) collective-permute-start(bf16[2,24,768]{2,1,0:T(8,128)(2,1)S(1)} %dynamic-slice_bitcast_fusion.9), channel_id=1, source_target_pairs={{0,16},{4,20},{8,24},{12,28},{16,0},{20,4},{24,8},{28,12},{1,17},{... | collective-permute-start | bytes 221192 | tf_op jit(solution)/shard_map/ppermute | solution.py:30
  517.1 19.2 %collective-permute-start.46 = (bf16[2,24,768]{2,1,0:T(8,128)(2,1)S(1)}, bf16[2,24,768]{2,1,0:T(8,128)(2,1)S(1)}, u32[]{:S(2)}, u32[]{:S(2)}) collective-permute-start(bf16[2,24,768]{2,1,0:T(8,128)(2,1)S(1)} %dynamic-slice_bitcast_fusion.8), channel_id=1, source_target_pairs={{0,2},{1,3},{2,0},{3,1},{4,6},{5,7},{6,4},{7,5},{8,10},{9,11},{10,... | collective-permute-start | bytes 221192 | tf_op jit(solution)/shard_map/ppermute | solution.py:30
  525.2 11.0 %collective-permute-start.35 = (bf16[1,2,56,768]{3,2,1,0:T(8,128)(2,1)S(1)}, bf16[1,2,56,768]{3,2,1,0:T(8,128)(2,1)S(1)}, u32[]{:S(2)}, u32[]{:S(2)}) collective-permute-start(bf16[1,2,56,768]{3,2,1,0:T(8,128)(2,1)S(1)} %dynamic-slice_bitcast_fusion.6), channel_id=1, source_target_pairs={{0,8},{4,12},{8,0},{12,4},{16,24},{20,28},{24,16},{28,20},{1,9},{5... | collective-permute-start | bytes 516104 | tf_op jit(solution)/shard_map/ppermute | solution.py:30
  (134 other events, 1410.6 us)
Sparse Core Ops, SparseCore 0:
  10.9 106.4 all-gather.2
  120.2 91.6 all-gather.4
  245.3 142.4 reduce-scatter.4
  393.7 163.4 reduce-scatter.2
